TPU v7x, 32 devices: a whole 2x2x4 slice. The times are simulated.
32 devices in a mesh: seq: 8 (over z, x), head: 4 (over y, core).
Axes of the slice: x: 2, y: 2, z: 4, core: 2. Of those that a mesh axis runs over, the one named last changes fastest.
Arguments:
- queries: bfloat16 [1024, 2048], P('seq', 'head'), may hold values from -6 to 6
- keys: bfloat16 [1024, 2048], P('seq', 'head'), may hold values from -6 to 6
- values: bfloat16 [1024, 2048], P('seq', 'head'), may hold values from -7 to 7
- d_out: bfloat16 [1024, 2048], P('seq', 'head'), may hold values from -6 to 6
- gain: float32 [2048], P('head'), may hold values from 0.25 to 1.75
Outputs:
- normed: bfloat16 [1024, 2048], P('seq', 'head')
- query_grad: bfloat16 [1024, 2048], P('seq', 'head')
- key_grad: bfloat16 [1024, 2048], P('seq', 'head')
- value_grad: bfloat16 [1024, 2048], P('seq', 'head')
All inputs are finite; a program needn't handle non-finite values.
Results may differ from a plain program's by a relative error of at most 0.0049.
Values sent between devices are 32-bit elements; how exact they have to be, the bound alone decides.
No kernel may reach another device: no remote copies, remote signals or barrier semaphores. Data moves between devices by JAX's collectives and lax.ppermute only.
A program may use at most 64 MiB of HBM per device.

v0:
```python
import math

import jax
import jax.numpy as jnp
from jax import lax
from jax.sharding import PartitionSpec as P

HEAD_DIM = 64
BLOCK = 128


epsilon = 1e-06


def entering(shard, axis, combine, identity, reverse):
    count, position = (lax.axis_size(axis), lax.axis_index(axis))
    everything = lax.all_gather(shard, axis)
    start = jnp.broadcast_to(jnp.asarray(identity, shard.dtype), shard.shape)

    def step(k, before):
        at = count - 1 - k if reverse else k
        reached = at > position if reverse else at < position
        new = combine(before, everything[at])
        return jnp.where(reached, new, before)

    return lax.fori_loop(0, count, step, start)


def add_states(earlier, later):
    return jax.tree.map(jnp.add, earlier, later)


def body(queries, keys, values, d_out, gain):
    length = queries.shape[0]
    head_width = HEAD_DIM
    head_count = queries.shape[1] // head_width
    block_count = length // BLOCK
    seq_total = length * lax.axis_size("seq")
    factor = 1.0 / math.sqrt(head_width * seq_total)
    shape_blocks = (block_count, BLOCK, head_count, head_width)
    query_blocks = queries.reshape(shape_blocks)
    key_blocks = keys.reshape(shape_blocks)
    value_blocks = values.reshape(shape_blocks)
    grad_blocks = d_out.reshape(shape_blocks)
    row_index = lax.broadcasted_iota(jnp.int32, (BLOCK, BLOCK), 0)
    column_index = lax.broadcasted_iota(jnp.int32, (BLOCK, BLOCK), 1)
    causal = (row_index >= column_index)[None, None]
    kv_blocks = jnp.einsum(
        "bjhd,bjhe->bhde", key_blocks, value_blocks, preferred_element_type=jnp.float32
    )
    qg_blocks = jnp.einsum(
        "bihe,bihd->bhed", grad_blocks, query_blocks, preferred_element_type=jnp.float32
    )
    state_shape = (head_count, head_width, head_width)
    flat_shape = (head_count * head_width * head_width // 128, 128)
    kv_local = jnp.sum(kv_blocks, axis=0).reshape(flat_shape)
    qg_local = jnp.sum(qg_blocks, axis=0).reshape(flat_shape)
    zeros = jnp.zeros_like(kv_local)
    kv_before_dev = entering(kv_local, "seq", add_states, zeros, False)
    qg_after_dev = entering(qg_local, "seq", add_states, zeros, True)
    kv_before_dev = kv_before_dev.reshape(state_shape)
    qg_after_dev = qg_after_dev.reshape(state_shape)
    scores = jnp.einsum(
        "bihd,bjhd->bhij", query_blocks, key_blocks, preferred_element_type=jnp.float32
    )
    weights = (factor * jnp.where(causal, scores, 0.0)).astype(jnp.bfloat16)
    grad_scores = jnp.einsum(
        "bihe,bjhe->bhij", grad_blocks, value_blocks, preferred_element_type=jnp.float32
    )
    dweights = (factor * jnp.where(causal, grad_scores, 0.0)).astype(jnp.bfloat16)
    kv_before = jnp.cumsum(kv_blocks, axis=0) - kv_blocks
    qg_after = jnp.flip(jnp.cumsum(jnp.flip(qg_blocks, 0), axis=0), 0) - qg_blocks
    prefix_state = (factor * (kv_before_dev[None] + kv_before)).astype(jnp.bfloat16)
    grad_state = (factor * (qg_after_dev[None] + qg_after)).astype(jnp.bfloat16)
    output = jnp.einsum(
        "bhij,bjhe->bihe", weights, value_blocks, preferred_element_type=jnp.float32
    )
    output = output + jnp.einsum(
        "bihd,bhde->bihe", query_blocks, prefix_state, preferred_element_type=jnp.float32
    )
    query_grad = jnp.einsum(
        "bhij,bjhd->bihd", dweights, key_blocks, preferred_element_type=jnp.float32
    )
    query_grad = query_grad + jnp.einsum(
        "bihe,bhde->bihd", grad_blocks, prefix_state, preferred_element_type=jnp.float32
    )
    key_grad = jnp.einsum(
        "bhij,bihd->bjhd", dweights, query_blocks, preferred_element_type=jnp.float32
    )
    key_grad = key_grad + jnp.einsum(
        "bjhe,bhed->bjhd", value_blocks, grad_state, preferred_element_type=jnp.float32
    )
    value_grad = jnp.einsum(
        "bhij,bihe->bjhe", weights, grad_blocks, preferred_element_type=jnp.float32
    )
    value_grad = value_grad + jnp.einsum(
        "bjhd,bhed->bjhe", key_blocks, grad_state, preferred_element_type=jnp.float32
    )
    shape_flat = (length, head_count * head_width)
    output = output.reshape(shape_flat)
    squares = jnp.sum(output * output, axis=1)
    row_total = lax.psum(squares, "head")
    mean_square = row_total / (head_count * lax.axis_size("head") * head_width)
    normed = (output * lax.rsqrt(mean_square + epsilon)[:, None] * gain[None]).astype(jnp.bfloat16)
    return (
        normed,
        query_grad.reshape(shape_flat).astype(jnp.bfloat16),
        key_grad.reshape(shape_flat).astype(jnp.bfloat16),
        value_grad.reshape(shape_flat).astype(jnp.bfloat16),
    )


def solution(mesh):
    placed = (P("seq", "head"), P("seq", "head"), P("seq", "head"), P("seq", "head"), P("head"))
    return jax.shard_map(
        body,
        mesh=mesh,
        in_specs=placed,
        out_specs=(P("seq", "head"), P("seq", "head"), P("seq", "head"), P("seq", "head")),
        check_vma=False,
    )
```

profile of v0, /device:TPU:0, one launch (start us, length us, event | category | flops | bytes accessed | tf_op | source)
XLA Modules:
  0.0 119.9 jit_solution(10128996307814906752)
XLA Ops:
  7.2 0.0 copy-start
  7.2 0.0 all-gather.5.cloned.1.call-start
  7.2 1.1 copy.41
  8.3 0.0 copy-done
  8.3 0.1 copy.46
  8.4 0.2 fusion.11
  8.6 0.8 all_gather_reshape.7
  9.4 0.0 copy-start.1
  9.4 0.0 all-gather.5.cloned.1.call-update
  9.4 0.0 copy-start.2
  9.4 0.0 all-gather.3.cloned.1.call-start
  9.5 0.8 copy-done.1
  10.3 0.1 copy.42
  10.4 0.0 copy-done.2
  10.4 0.1 copy.43
  10.5 0.2 fusion.10
  10.7 0.8 all_gather_reshape.6
  11.5 0.0 all-gather.3.cloned.1.call-update
  11.6 0.3 fusion.2
  11.9 0.3 fusion.3
  12.2 0.3 convolution_bitcast_fusion.3
  12.4 0.3 convolution_bitcast_fusion.2
  12.7 41.0 %all-gather.5.cloned.1.call-done = f32[8,256,128]{2,1,0:T(8,128)} async-done(((f32[1,256,128]{2,1,0:T(8,128)}), f32[8,256,128]{2,1,0:T(8,128)}) %all-gather.5.cloned.1.call-update) | async-done | bytes 1048592 | tf_op jit(solution)/shard_map/all_gather | solution.py:17
  53.7 7.8 %while.31 = (s32[]{:T(128)}, f32[256,128]{1,0:T(8,128)S(1)}, s32[]{:T(128)}, f32[8,256,128]{2,1,0:T(8,128)}, s32[]{:T(128)}, /*index=5*/s32[]{:T(128)}, s32[]{:T(128)}, s32[]{:T(128)}) while((s32[]{:T(128)}, f32[256,128]{1,0:T(8,128)S(1)}, s32[]{:T(128)}, f32[8,256,128]{2,1,0:T(8,128)}, s32[]{:T(128)}, /*index=5*/s32[]{:T(128)}, ...), condition=%wide.region_5.6_spmd.clone, body=%wide.region_4.5_spmd.clone.sunk | while | flops 98312 | bytes 393379 | solution.py:26
  53.7 0.9 add_select_fusion.5
  54.7 0.9 add_select_fusion.5
  55.7 0.9 add_select_fusion.5
  56.6 0.9 add_select_fusion.5
  57.6 0.9 add_select_fusion.5
  58.6 0.9 add_select_fusion.5
  59.6 0.9 add_select_fusion.5
  60.5 0.9 add_select_fusion.5
  61.5 0.1 broadcast_in_dim_reshape.7
  61.7 0.2 fusion.12
  61.9 0.2 fusion.13
  62.1 33.4 %all-gather.3.cloned.1.call-done = f32[8,256,128]{2,1,0:T(8,128)} async-done(((f32[1,256,128]{2,1,0:T(8,128)}), f32[8,256,128]{2,1,0:T(8,128)}) %all-gather.3.cloned.1.call-update) | async-done | bytes 1048592 | tf_op jit(solution)/shard_map/all_gather | solution.py:17
  95.4 7.7 %while.30 = (s32[]{:T(128)}, f32[256,128]{1,0:T(8,128)S(1)}, s32[]{:T(128)}, f32[8,256,128]{2,1,0:T(8,128)}, s32[]{:T(128)}, /*index=5*/s32[]{:T(128)}) while((s32[]{:T(128)}, f32[256,128]{1,0:T(8,128)S(1)}, s32[]{:T(128)}, f32[8,256,128]{2,1,0:T(8,128)}, s32[]{:T(128)}, /*index=5*/s32[]{:T(128)}) %tuple.75), condition=%wide.region_1.0_spmd.clone, body=%wide.region_0.0_spmd.clone.sunk | while | flops 98308 | bytes 393317 | solution.py:26
  95.4 0.9 add_select_fusion.4
  96.4 0.9 add_select_fusion.4
  97.4 0.9 add_select_fusion.4
  98.3 0.9 add_select_fusion.4
  99.3 0.9 add_select_fusion.4
  100.3 0.9 add_select_fusion.4
  101.2 0.9 add_select_fusion.4
  102.2 0.9 add_select_fusion.4
  103.2 0.1 broadcast_in_dim_reshape.6
  103.3 0.3 fusion.9
  103.6 5.7 %psum.7 = f32[128]{0:T(128)S(1)} all-reduce(f32[128]{0:T(128)S(1)} %get-tuple-element.253), channel_id=1, replica_groups=mesh['seq'=8,'head'=4] {'head'}, use_global_device_ids=true, to_apply=%region_3.4 | all-reduce | flops 128 | bytes 1024 | tf_op jit(solution)/shard_map/psum | solution.py:102
  109.3 0.1 copy.45
  109.4 0.2 fusion.7
  109.6 0.2 fusion.6
  109.8 0.8 copy.48
  110.6 0.2 fusion.8
  110.8 0.8 copy.50
  111.5 0.0 copy-start.3
  111.5 0.8 copy.49
  112.3 0.0 copy-done.3
  112.3 0.7 multiply_convert_fusion.1
  (6 shorter events, 0.1 us)
Async XLA Ops:
  7.2 1.1 copy-start
  7.2 46.5 %all-gather.5.cloned.1.call-start = ((), (), s32[]{:S(2)}) async-start(), calls=%async_computation.1 | async-start | bytes 1179648 | tf_op jit(solution)/shard_map/all_gather | solution.py:17
  9.4 0.9 copy-start.1
  9.4 1.0 copy-start.2
  9.4 86.0 %all-gather.3.cloned.1.call-start = ((), (), s32[]{:S(2)}) async-start(), calls=%async_computation | async-start | bytes 1179648 | tf_op jit(solution)/shard_map/all_gather | solution.py:17
  111.5 0.8 copy-start.3
Sparse Core Ops, SparseCore 0:
  10.7 42.9 all-gather.4
  56.4 38.9 all-gather.2
where the time goes:
time: 120 us
  waiting for transfers between devices  74.4 us (62%)
  other arithmetic  16 us (13%)
  between operations  14.2 us (12%)
  local copies, waits for them, and re-layouts  6.41 us (5%)
  blocking collectives  5.66 us (5%)
  matrix products  2.72 us (2%)
    all_gather x2, waiting for transfers between devices, entering(): everything = lax.all_gather(shard, axis)  74.4 us
    select_n x16, other arithmetic, step(): return jnp.where(reached, new, before)  15.2 us
    psum x1, blocking collectives, body(): row_total = lax.psum(squares, 'head')  5.66 us
    unnamed x15, local copies, waits for them, and re-layouts  4.55 us
  transfers between devices with their start and end apart: 2, of which 2 were waited for; matrix products, arithmetic and copies ran while one was open for 9% of the time, Pallas kernels for 0%

commit v1 on v0

v1 whole, which is shorter than its diff:
```python
import functools
import math

import jax
import jax.numpy as jnp
from jax import lax
from jax.experimental import pallas as pl
from jax.experimental.pallas import tpu as pltpu
from jax.sharding import PartitionSpec as P

HEAD_DIM = 64
BLOCK = 128
LANES = 128

epsilon = 1e-06


f32 = jnp.float32
bf16 = jnp.bfloat16


def dot(x, y, dims=((1,), (0,))):
    return lax.dot_general(x, y, (dims, ((), ())), preferred_element_type=f32)


NT = ((1,), (1,))
TN = ((0,), (0,))


def tiles(ref):
    return ref.shape[1] // LANES


def tile(ref, t):
    return ref[:, t * LANES : (t + 1) * LANES]


def lane_is_low(shape):
    return lax.broadcasted_iota(jnp.int32, shape, 1) < HEAD_DIM


def by_head(x):
    low = lane_is_low(x.shape)
    zero = jnp.zeros_like(x)
    return jnp.where(low, x, zero), jnp.where(low, zero, x)


def pack_state(product):
    low = lane_is_low((HEAD_DIM, LANES))
    return jnp.where(low, product[:HEAD_DIM], product[HEAD_DIM:])


def unpack_state(state):
    low = lane_is_low(state.shape)
    zero = jnp.zeros_like(state)
    return jnp.concatenate([jnp.where(low, state, zero), jnp.where(low, zero, state)], axis=0)


def states_kernel(q_ref, k_ref, v_ref, g_ref, kv_ref, qg_ref):
    for t in range(tiles(q_ref)):
        rows = slice(t * HEAD_DIM, (t + 1) * HEAD_DIM)
        kv_ref[rows] = pack_state(dot(tile(k_ref, t), tile(v_ref, t), TN))
        qg_ref[rows] = pack_state(dot(tile(g_ref, t), tile(q_ref, t), TN))


def block_kernel(factor, q_ref, k_ref, v_ref, g_ref, out_ref, dq_ref, dk_ref, dv_ref):
    row = lax.broadcasted_iota(jnp.int32, (BLOCK, BLOCK), 0)
    column = lax.broadcasted_iota(jnp.int32, (BLOCK, BLOCK), 1)
    causal = row >= column
    for t in range(tiles(q_ref)):
        q, k, v, g = (tile(ref, t) for ref in (q_ref, k_ref, v_ref, g_ref))
        cols = slice(t * LANES, (t + 1) * LANES)
        out = dq = dk = dv = None
        for qh, gh, kh, vh in zip(by_head(q), by_head(g), by_head(k), by_head(v)):
            weights = (factor * jnp.where(causal, dot(qh, k, NT), 0.0)).astype(bf16)
            dweights = (factor * jnp.where(causal, dot(gh, v, NT), 0.0)).astype(bf16)
            parts = (dot(weights, vh), dot(dweights, kh), dot(dweights, qh, TN), dot(weights, gh, TN))
            if out is None:
                out, dq, dk, dv = parts
            else:
                out, dq, dk, dv = (x + y for x, y in zip((out, dq, dk, dv), parts))
        out_ref[:, cols] = out
        dq_ref[:, cols] = dq
        dk_ref[:, cols] = dk
        dv_ref[:, cols] = dv


def output_kernel(factor, q_ref, part_ref, kv_ref, out_ref, squares_ref):
    total = None
    for t in range(tiles(q_ref)):
        cols = slice(t * LANES, (t + 1) * LANES)
        state = unpack_state((factor * kv_ref[t * HEAD_DIM : (t + 1) * HEAD_DIM]).astype(bf16))
        out = part_ref[:, cols] + dot(tile(q_ref, t), state)
        out_ref[:, cols] = out
        square = out * out
        total = square if total is None else total + square
    squares_ref[...] = jnp.sum(total.T, axis=0, keepdims=True)


def grads_kernel(
    factor, k_ref, v_ref, g_ref, dq_part, dk_part, dv_part, kv_ref, qg_ref, dq_ref, dk_ref, dv_ref
):
    for t in range(tiles(k_ref)):
        cols = slice(t * LANES, (t + 1) * LANES)
        rows = slice(t * HEAD_DIM, (t + 1) * HEAD_DIM)
        state = unpack_state((factor * kv_ref[rows]).astype(bf16))
        grad_state = unpack_state((factor * qg_ref[rows]).astype(bf16))
        dq_ref[:, cols] = (dq_part[:, cols] + dot(tile(g_ref, t), state, NT)).astype(bf16)
        dk_ref[:, cols] = (dk_part[:, cols] + dot(tile(v_ref, t), grad_state)).astype(bf16)
        dv_ref[:, cols] = (dv_part[:, cols] + dot(tile(k_ref, t), grad_state, NT)).astype(bf16)


def norm_kernel(width, out_ref, squares_ref, gain_ref, normed_ref):
    total = jnp.sum(squares_ref[...], axis=0, keepdims=True)
    scale = lax.rsqrt(total / width + epsilon)
    scale = jnp.broadcast_to(scale, (LANES, scale.shape[1])).T
    for t in range(tiles(out_ref)):
        cols = slice(t * LANES, (t + 1) * LANES)
        normed_ref[:, cols] = (out_ref[:, cols] * scale * gain_ref[:, cols]).astype(bf16)


def call(kernel, outs, args, flops):
    moved = sum(math.prod(a.shape) * jnp.dtype(a.dtype).itemsize for a in (*args, *outs))
    whole = pl.BlockSpec(memory_space=pltpu.VMEM)
    single = len(outs) == 1
    return pl.pallas_call(
        kernel,
        out_shape=outs[0] if single else tuple(outs),
        in_specs=[whole] * len(args),
        out_specs=whole if single else tuple([whole] * len(outs)),
        compiler_params=pltpu.CompilerParams(vmem_limit_bytes=16 * 2**20),
        cost_estimate=pl.CostEstimate(flops=flops, bytes_accessed=moved, transcendentals=0),
    )(*args)


def swap(x, axis, distance):
    size = lax.axis_size(axis)
    return lax.ppermute(x, axis, [(i, i ^ distance) for i in range(size)])


def halves(x, odd):
    mid = x.shape[0] // 2
    low, high = x[:mid], x[mid:]
    return jnp.where(odd, high, low), jnp.where(odd, low, high)


def join(mine, other, odd):
    return jnp.concatenate([jnp.where(odd, other, mine), jnp.where(odd, mine, other)], axis=0)


def scan_states(kv, qg, axis):
    count = lax.axis_size(axis)
    index = lax.axis_index(axis)
    bit = lambda d: (index & d) != 0
    zero = jnp.zeros_like(kv)
    top = count // 2
    if count & (count - 1):
        position = jnp.arange(count)[:, None, None]
        every_kv = lax.all_gather(kv, axis)
        every_qg = lax.all_gather(qg, axis)
        return (
            jnp.sum(jnp.where(position < index, every_kv, 0.0), axis=0),
            jnp.sum(jnp.where(position > index, every_qg, 0.0), axis=0),
        )
    if count < 8:
        before, after, total_kv, total_qg = zero, zero, kv, qg
        distance = 1
        while distance < count:
            got_kv, got_qg = swap(total_kv, axis, distance), swap(total_qg, axis, distance)
            before = before + jnp.where(bit(distance), got_kv, 0.0)
            after = after + jnp.where(bit(distance), 0.0, got_qg)
            total_kv, total_qg = total_kv + got_kv, total_qg + got_qg
            distance *= 2
        return before, after
    odd, upper = bit(1), bit(top)
    a, b = jnp.where(upper, qg, kv), jnp.where(upper, kv, qg)
    (a_mine, a_other), (b_mine, b_other) = halves(a, odd), halves(b, odd)
    a1 = swap(a_other, axis, 1)
    a2 = swap(a_mine, axis, 2)
    a3 = swap(a_other, axis, 3)
    b1 = swap(b_other, axis, 1)
    b2 = swap(b_mine, axis, 2)
    b3 = swap(b_other, axis, 3)
    a_enters = lambda d: bit(d) != upper
    b_enters = lambda d: bit(d) == upper
    a_pair, b_pair = a2 + a3, b2 + b3
    a_sum = jnp.where(a_enters(2), a_pair, 0.0)
    b_sum = jnp.where(b_enters(2), b_pair, 0.0)
    a_total, b_total = a_mine + a1 + a_pair, b_mine + b1 + b_pair
    distance = 4
    while distance < top:
        a_got, b_got = swap(a_total, axis, distance), swap(b_total, axis, distance)
        a_sum = a_sum + jnp.where(a_enters(distance), a_got, 0.0)
        b_sum = b_sum + jnp.where(b_enters(distance), b_got, 0.0)
        a_total, b_total = a_total + a_got, b_total + b_got
        distance *= 2
    t_mine = swap(a_total, axis, top)
    t_other = swap(a_total, axis, top | 1)
    a_out = a_sum + jnp.where(a_enters(1), 0.0, a_mine)
    b_out = b_sum + jnp.where(b_enters(1), 0.0, b_mine)
    got = swap(jnp.concatenate([a_out, b_out], axis=0), axis, 1)
    mid = a_mine.shape[0]
    a_own = a_sum + jnp.where(a_enters(1), a1, 0.0)
    b_own = b_sum + jnp.where(b_enters(1), b1, 0.0) + t_mine
    a_all = join(a_own, got[:mid], odd)
    b_all = join(b_own, got[mid:] + t_other, odd)
    return jnp.where(upper, b_all, a_all), jnp.where(upper, a_all, b_all)


def all_shares(row, axis):
    count = lax.axis_size(axis)
    if count & (count - 1):
        return lax.psum(row, axis)
    if count > 4:
        distance = 1
        while distance < count:
            row = row + swap(row, axis, distance)
            distance *= 2
        return row
    return jnp.concatenate([row] + [swap(row, axis, d) for d in range(1, count)], axis=0)


def body(queries, keys, values, d_out, gain):
    length, width = queries.shape
    factor = 1.0 / math.sqrt(HEAD_DIM * length * lax.axis_size("seq"))
    row_bytes = jax.ShapeDtypeStruct((width // LANES * HEAD_DIM, LANES), f32)
    wide = jax.ShapeDtypeStruct((length, width), f32)
    narrow = jax.ShapeDtypeStruct((length, width), bf16)
    inputs = (queries, keys, values, d_out)
    kv, qg = call(states_kernel, [row_bytes] * 2, inputs, 4 * length * LANES * width)
    out_part, dq_part, dk_part, dv_part = call(
        functools.partial(block_kernel, factor), [wide] * 4, inputs, 24 * length * LANES * width
    )
    before, after = scan_states(kv, qg, "seq")
    out, squares = call(
        functools.partial(output_kernel, factor),
        [wide, jax.ShapeDtypeStruct((1, length), f32)],
        (queries, out_part, before),
        2 * length * LANES * width,
    )
    shares = all_shares(squares, "head")
    dq, dk, dv = call(
        functools.partial(grads_kernel, factor),
        [narrow] * 3,
        (keys, values, d_out, dq_part, dk_part, dv_part, before, after),
        6 * length * LANES * width,
    )
    normed = call(
        functools.partial(norm_kernel, width * lax.axis_size("head")),
        [narrow],
        (out, shares, gain[None]),
        2 * length * width,
    )
    return normed, dq, dk, dv


def solution(mesh):
    placed = (P("seq", "head"), P("seq", "head"), P("seq", "head"), P("seq", "head"), P("head"))

    return jax.shard_map(
        body,
        mesh=mesh,
        in_specs=placed,
        out_specs=(P("seq", "head"), P("seq", "head"), P("seq", "head"), P("seq", "head")),
        check_vma=False,
    )
```

time: 120 us -> 34.5 us (0.29)
  waiting for transfers between devices: 74.4 us -> 9.51 us
  other arithmetic: 16 us -> 0.19 us
  starting transfers between devices: 0.08 us -> 15.8 us
  between operations: 14.2 us -> 0.79 us
  blocking collectives: 5.66 us -> 0 us
  Pallas kernels: 0 us -> 3.75 us
  matrix products: 2.72 us -> 0 us
  local copies, waits for them, and re-layouts: 6.41 us -> 4.31 us
    all_gather x2 -> x0, waiting for transfers between devices: 74.4 us -> none  [entering(): everything = lax.all_gather(shard, axis)]
    ppermute x0 -> x12, starting transfers between devices: none -> 15.8 us  [swap(): return lax.ppermute(x, axis, [(i, i ^ distance) for i in range(size)])]
    select_n x16 -> x6, other arithmetic: 15.2 us -> 0.13 us  [the longest x2 0.06 us: join(): jnp.where(odd, other, mine)]
    ppermute x0 -> x12, waiting for transfers between devices: none -> 9.51 us  [swap(): return lax.ppermute(x, axis, [(i, i ^ distance) for i in range(size)])]
    psum x1 -> x0, blocking collectives: 5.66 us -> none  [body(): row_total = lax.psum(squares, 'head')]
    pallas_call x0 -> x5, Pallas kernels: none -> 3.75 us  [call(): pl.pallas_call(kernel, out_shape=outs[0] if single else tuple(outs), in_s...]
    dot_general x12 -> x0, matrix products: 2.72 us -> none  [the longest x1 0.29 us: body(): jnp.einsum('bihd,bjhd->bhij', query_blocks, key_blocks, preferred_element...]
    another operation x4 -> x0, local copies, waits for them, and re-layouts: 1.73 us -> none  [the longest x2 1.53 us: entering(): everything = lax.all_gather(shard, axis)]
  transfers between devices with their start and end apart: 2 -> 12, of which waited for: 2 -> 7; matrix products, arithmetic and copies ran while one was open for 9% -> 0% of each run, Pallas kernels for 0% -> 7%
where the time goes in v1:
time: 34.5 us; the launch traced here: 34.3 us
  starting transfers between devices  15.8 us (46%)
  waiting for transfers between devices  9.51 us (28%)
  local copies, waits for them, and re-layouts  4.31 us (12%)
  Pallas kernels  3.75 us (11%)
  between operations  0.79 us (2%)
    ppermute x12, starting transfers between devices, swap(): return lax.ppermute(x, axis, [(i, i ^ distance) for i in range(size)])  15.8 us
    ppermute x12, waiting for transfers between devices, swap(): return lax.ppermute(x, axis, [(i, i ^ distance) for i in range(size)])  9.51 us
    unnamed x18, local copies, waits for them, and re-layouts  4.31 us
    pallas_call x5, Pallas kernels, call(): pl.pallas_call(kernel, out_shape=outs[0] if single else tuple(outs), in_s...  3.75 us
  transfers between devices with their start and end apart: 12, of which 7 were waited for; matrix products, arithmetic and copies ran while one was open for 0% of the time, Pallas kernels for 7%

profile of v1, /device:TPU:0, one launch (start us, length us, event | category | flops | bytes accessed | tf_op | source)
XLA Modules:
  0.0 34.3 jit_solution(14993947094017873602)
XLA Ops:
  0.6 0.0 copy-start
  0.7 0.9 %copy-done = bf16[128,512]{1,0:T(8,128)(2,1)S(1)} copy-done((bf16[128,512]{1,0:T(8,128)(2,1)S(1)}, bf16[128,512]{1,0:T(8,128)(2,1)}, u32[]{:S(2)}) %copy-start) | copy-done | bytes 131096
  1.5 0.0 copy-start.2
  1.5 0.9 %copy-done.2 = bf16[128,512]{1,0:T(8,128)(2,1)S(1)} copy-done((bf16[128,512]{1,0:T(8,128)(2,1)S(1)}, bf16[128,512]{1,0:T(8,128)(2,1)}, u32[]{:S(2)}) %copy-start.2) | copy-done | bytes 131096
  2.5 0.0 copy-start.4
  2.5 0.9 %copy-done.4 = bf16[128,512]{1,0:T(8,128)(2,1)S(1)} copy-done((bf16[128,512]{1,0:T(8,128)(2,1)S(1)}, bf16[128,512]{1,0:T(8,128)(2,1)}, u32[]{:S(2)}) %copy-start.4) | copy-done | bytes 131096
  3.4 0.0 copy-start.6
  3.4 0.9 %copy-done.6 = bf16[128,512]{1,0:T(8,128)(2,1)S(1)} copy-done((bf16[128,512]{1,0:T(8,128)(2,1)S(1)}, bf16[128,512]{1,0:T(8,128)(2,1)}, u32[]{:S(2)}) %copy-start.6) | copy-done | bytes 131096
  4.3 0.3 shard_map.85
  4.6 3.0 %collective-permute-start.5 = (f32[128,128]{1,0:T(8,128)S(1)}, f32[128,128]{1,0:T(8,128)S(1)}, u32[]{:S(2)}, u32[]{:S(2)}) collective-permute-start(f32[128,128]{1,0:T(8,128)S(1)} %get-tuple-element.37), channel_id=1, source_target_pairs={{0,4},{4,0},{8,12},{12,8},{16,20},{20,16},{24,28},{28,24},{1,5},{5... | collective-permute-start | bytes 196616 | tf_op jit(solution)/shard_map/ppermute | solution.py:138
  7.6 1.5 %collective-permute-start.1 = (f32[128,128]{1,0:T(8,128)S(1)}, f32[128,128]{1,0:T(8,128)S(1)}, u32[]{:S(2)}, u32[]{:S(2)}) collective-permute-start(f32[128,128]{1,0:T(8,128)S(1)} %get-tuple-element.37), channel_id=1, source_target_pairs={{0,12},{4,8},{8,4},{12,0},{16,28},{20,24},{24,20},{28,16},{1,13},{... | collective-permute-start | bytes 196616 | tf_op jit(solution)/shard_map/ppermute | solution.py:138
  9.2 0.0 collective-permute-start
  9.2 2.1 %collective-permute-start.2 = (f32[128,128]{1,0:T(8,128)S(1)}, f32[128,128]{1,0:T(8,128)S(1)}, u32[]{:S(2)}, u32[]{:S(2)}) collective-permute-start(f32[128,128]{1,0:T(8,128)S(1)} %get-tuple-element.40), channel_id=1, source_target_pairs={{0,8},{4,12},{8,0},{12,4},{16,24},{20,28},{24,16},{28,20},{1,9},{5... | collective-permute-start | bytes 196616 | tf_op jit(solution)/shard_map/ppermute | solution.py:138
  11.3 1.4 %collective-permute-start.3 = (f32[128,128]{1,0:T(8,128)S(1)}, f32[128,128]{1,0:T(8,128)S(1)}, u32[]{:S(2)}, u32[]{:S(2)}) collective-permute-start(f32[128,128]{1,0:T(8,128)S(1)} %get-tuple-element.39), channel_id=1, source_target_pairs={{0,12},{4,8},{8,4},{12,0},{16,28},{20,24},{24,20},{28,16},{1,13},{... | collective-permute-start | bytes 196616 | tf_op jit(solution)/shard_map/ppermute | solution.py:138
  12.6 0.9 %collective-permute-done = f32[128,128]{1,0:T(8,128)S(1)} collective-permute-done((f32[128,128]{1,0:T(8,128)S(1)}, f32[128,128]{1,0:T(8,128)S(1)}, u32[]{:S(2)}, u32[]{:S(2)}) %collective-permute-start) | collective-permute-done | bytes 65568 | tf_op jit(solution)/shard_map/ppermute | solution.py:138
  13.6 0.0 collective-permute-done.5
  13.6 0.0 collective-permute-done.1
  13.6 1.3 %collective-permute-done.2 = f32[128,128]{1,0:T(8,128)S(1)} collective-permute-done((f32[128,128]{1,0:T(8,128)S(1)}, f32[128,128]{1,0:T(8,128)S(1)}, u32[]{:S(2)}, u32[]{:S(2)}) %collective-permute-start.2) | collective-permute-done | bytes 65568 | tf_op jit(solution)/shard_map/ppermute | solution.py:138
  14.9 1.9 %collective-permute-done.3 = f32[128,128]{1,0:T(8,128)S(1)} collective-permute-done((f32[128,128]{1,0:T(8,128)S(1)}, f32[128,128]{1,0:T(8,128)S(1)}, u32[]{:S(2)}, u32[]{:S(2)}) %collective-permute-start.3) | collective-permute-done | bytes 65568 | tf_op jit(solution)/shard_map/ppermute | solution.py:138
  16.9 0.0 copy-start.5
  16.9 0.0 copy-start.7
  16.9 0.0 copy-start.1
  16.9 0.0 copy-start.3
  16.9 1.1 %collective-permute-start.4 = (f32[256,128]{1,0:T(8,128)S(1)}, f32[256,128]{1,0:T(8,128)S(1)}, u32[]{:S(2)}, u32[]{:S(2)}) collective-permute-start(f32[256,128]{1,0:T(8,128)S(1)} %pad_maximum_fusion), channel_id=1, source_target_pairs={{0,4},{4,0},{8,12},{12,8},{16,20},{20,16},{24,28},{28,24},{1,5},{5... | collective-permute-start | bytes 393224 | tf_op jit(solution)/shard_map/ppermute | solution.py:138
  18.0 1.0 %collective-permute-start.7 = (f32[128,128]{1,0:T(8,128)S(1)}, f32[128,128]{1,0:T(8,128)S(1)}, u32[]{:S(2)}, u32[]{:S(2)}) collective-permute-start(f32[128,128]{1,0:T(8,128)S(1)} %get-tuple-element.39), channel_id=1, source_target_pairs={{0,4},{4,0},{8,12},{12,8},{16,20},{20,16},{24,28},{28,24},{1,5},{5... | collective-permute-start | bytes 196616 | tf_op jit(solution)/shard_map/ppermute | solution.py:138
  19.0 3.1 %collective-permute-start.6 = (f32[128,128]{1,0:T(8,128)S(1)}, f32[128,128]{1,0:T(8,128)S(1)}, u32[]{:S(2)}, u32[]{:S(2)}) collective-permute-start(f32[128,128]{1,0:T(8,128)S(1)} %get-tuple-element.28), channel_id=1, source_target_pairs={{0,20},{4,16},{8,28},{12,24},{16,4},{20,0},{24,12},{28,8},{1,21},{... | collective-permute-start | bytes 196616 | tf_op jit(solution)/shard_map/ppermute | solution.py:138
  22.1 0.3 collective-permute-start.8
  22.4 0.0 copy-done.5
  22.4 0.0 copy-done.7
  22.4 0.0 copy-done.1
  22.4 0.0 copy-done.3
  22.4 1.4 %shard_map.84 = (f32[128,512]{1,0:T(8,128)S(1)}, f32[128,512]{1,0:T(8,128)S(1)}, f32[128,512]{1,0:T(8,128)S(1)}, f32[128,512]{1,0:T(8,128)S(1)}) custom-call(bf16[128,512]{1,0:T(8,128)(2,1)S(1)} %copy-done.1, bf16[128,512]{1,0:T(8,128)(2,1)S(1)} %copy-done.3, bf16[128,512]{1,0:T(8,128)(2,1)S(1)} %copy-done.5, bf16[128,512]{1,0:T(8,128)(2,1)S(1)} %copy-done.7), custom_call_target="tpu_custom_call" | custom-call | flops 201326592 | bytes 1572864 | tf_op jit(solution)/shard_map/pallas_call | solution.py:126
  23.9 0.0 collective-permute-done.7
  23.9 2.9 %collective-permute-done.6 = f32[128,128]{1,0:T(8,128)S(1)} collective-permute-done((f32[128,128]{1,0:T(8,128)S(1)}, f32[128,128]{1,0:T(8,128)S(1)}, u32[]{:S(2)}, u32[]{:S(2)}) %collective-permute-start.6) | collective-permute-done | bytes 65568 | tf_op jit(solution)/shard_map/ppermute | solution.py:138
  26.8 1.1 %collective-permute-done.8 = f32[128,128]{1,0:T(8,128)S(1)} collective-permute-done((f32[128,128]{1,0:T(8,128)S(1)}, f32[128,128]{1,0:T(8,128)S(1)}, u32[]{:S(2)}, u32[]{:S(2)}) %collective-permute-start.8) | collective-permute-done | bytes 65568 | tf_op jit(solution)/shard_map/ppermute | solution.py:138
  27.9 0.0 collective-permute-done.4
  28.0 0.3 shard_map.86
  28.2 1.6 %collective-permute-start.10 = (f32[1,128]{1,0:T(1,128)S(1)}, f32[1,128]{1,0:T(1,128)S(1)}, u32[]{:S(2)}, u32[]{:S(2)}) collective-permute-start(f32[1,128]{1,0:T(1,128)S(1)} %get-tuple-element.19), channel_id=1, source_target_pairs={{0,2},{1,3},{2,0},{3,1},{4,6},{5,7},{6,4},{7,5},{8,10},{9,11},{10,... | collective-permute-start | bytes 1544 | tf_op jit(solution)/shard_map/ppermute | solution.py:138
  29.8 0.0 collective-permute-start.11
  29.8 0.6 %collective-permute-start.9 = (f32[1,128]{1,0:T(1,128)S(1)}, f32[1,128]{1,0:T(1,128)S(1)}, u32[]{:S(2)}, u32[]{:S(2)}) collective-permute-start(f32[1,128]{1,0:T(1,128)S(1)} %get-tuple-element.19), channel_id=1, source_target_pairs={{0,1},{1,0},{2,3},{3,2},{4,5},{5,4},{6,7},{7,6},{8,9},{9,8},{10,11... | collective-permute-start | bytes 1544 | tf_op jit(solution)/shard_map/ppermute | solution.py:138
  30.5 1.0 %shard_map.88 = (bf16[128,512]{1,0:T(8,128)(2,1)}, bf16[128,512]{1,0:T(8,128)(2,1)}, bf16[128,512]{1,0:T(8,128)(2,1)}) custom-call(bf16[128,512]{1,0:T(8,128)(2,1)S(1)} %copy-done.3, bf16[128,512]{1,0:T(8,128)(2,1)S(1)} %copy-done.5, bf16[128,512]{1,0:T(8,128)(2,1)S(1)} %copy-done.7, f32[128,512]{1,0:T(8,128)S(1)} %get-tuple-element.20.dq_part, ...), custom_call_target="tpu_custom_call" | custom-call | flops 50331648 | bytes 1835008 | tf_op jit(solution)/shard_map/pallas_call | solution.py:126
  31.5 0.4 %collective-permute-done.10 = f32[1,128]{1,0:T(1,128)S(1)} collective-permute-done((f32[1,128]{1,0:T(1,128)S(1)}, f32[1,128]{1,0:T(1,128)S(1)}, u32[]{:S(2)}, u32[]{:S(2)}) %collective-permute-start.10) | collective-permute-done | bytes 544 | tf_op jit(solution)/shard_map/ppermute | solution.py:138
  31.9 0.9 %collective-permute-done.11 = f32[1,128]{1,0:T(1,128)S(1)} collective-permute-done((f32[1,128]{1,0:T(1,128)S(1)}, f32[1,128]{1,0:T(1,128)S(1)}, u32[]{:S(2)}, u32[]{:S(2)}) %collective-permute-start.11) | collective-permute-done | bytes 544 | tf_op jit(solution)/shard_map/ppermute | solution.py:138
  32.8 0.0 collective-permute-done.9
  32.8 0.0 copy-start.8
  32.9 0.7 %copy-done.8 = f32[512]{0:T(512)S(1)} copy-done((f32[512]{0:T(512)S(1)}, f32[512]{0:T(512)}, u32[]{:S(2)}) %copy-start.8) | copy-done | bytes 2072
  33.5 0.8 %shard_map.87 = bf16[128,512]{1,0:T(8,128)(2,1)} custom-call(f32[128,512]{1,0:T(8,128)S(1)} %get-tuple-element.18.out_ref, f32[4,128]{1,0:T(4,128)S(1)} %pad_maximum_fusion.3.squares_ref, f32[1,512]{1,0:T(1,128)S(1)} %bitcast.1), custom_call_target="tpu_custom_call" | custom-call | flops 131072 | bytes 397312 | tf_op jit(solution)/shard_map/pallas_call | solution.py:126
  (11 shorter events, 0.2 us)
Async XLA Ops:
  0.6 0.9 %copy-start = (bf16[128,512]{1,0:T(8,128)(2,1)S(1)}, bf16[128,512]{1,0:T(8,128)(2,1)}, u32[]{:S(2)}) copy-start(bf16[128,512]{1,0:T(8,128)(2,1)} %q_ref.5) | copy-start | bytes 393220
  1.5 0.9 %copy-start.2 = (bf16[128,512]{1,0:T(8,128)(2,1)S(1)}, bf16[128,512]{1,0:T(8,128)(2,1)}, u32[]{:S(2)}) copy-start(bf16[128,512]{1,0:T(8,128)(2,1)} %k_ref.5) | copy-start | bytes 393220
  2.5 0.9 %copy-start.4 = (bf16[128,512]{1,0:T(8,128)(2,1)S(1)}, bf16[128,512]{1,0:T(8,128)(2,1)}, u32[]{:S(2)}) copy-start(bf16[128,512]{1,0:T(8,128)(2,1)} %v_ref.5) | copy-start | bytes 393220
  3.4 0.9 %copy-start.6 = (bf16[128,512]{1,0:T(8,128)(2,1)S(1)}, bf16[128,512]{1,0:T(8,128)(2,1)}, u32[]{:S(2)}) copy-start(bf16[128,512]{1,0:T(8,128)(2,1)} %g_ref.5) | copy-start | bytes 393220
  4.6 9.0 %collective-permute-start.5 = (f32[128,128]{1,0:T(8,128)S(1)}, f32[128,128]{1,0:T(8,128)S(1)}, u32[]{:S(2)}, u32[]{:S(2)}) collective-permute-start(f32[128,128]{1,0:T(8,128)S(1)} %get-tuple-element.37), channel_id=1, source_target_pairs={{0,4},{4,0},{8,12},{12,8},{16,20},{20,16},{24,28},{28,24},{1,5},{5... | collective-permute-start | bytes 196616 | tf_op jit(solution)/shard_map/ppermute | solution.py:138
  7.6 6.0 %collective-permute-start.1 = (f32[128,128]{1,0:T(8,128)S(1)}, f32[128,128]{1,0:T(8,128)S(1)}, u32[]{:S(2)}, u32[]{:S(2)}) collective-permute-start(f32[128,128]{1,0:T(8,128)S(1)} %get-tuple-element.37), channel_id=1, source_target_pairs={{0,12},{4,8},{8,4},{12,0},{16,28},{20,24},{24,20},{28,16},{1,13},{... | collective-permute-start | bytes 196616 | tf_op jit(solution)/shard_map/ppermute | solution.py:138
  9.2 4.4 %collective-permute-start = (f32[128,128]{1,0:T(8,128)S(1)}, f32[128,128]{1,0:T(8,128)S(1)}, u32[]{:S(2)}, u32[]{:S(2)}) collective-permute-start(f32[128,128]{1,0:T(8,128)S(1)} %get-tuple-element.38), channel_id=1, source_target_pairs={{0,8},{4,12},{8,0},{12,4},{16,24},{20,28},{24,16},{28,20},{1,9},{5... | collective-permute-start | bytes 196616 | tf_op jit(solution)/shard_map/ppermute | solution.py:138
  9.2 5.7 %collective-permute-start.2 = (f32[128,128]{1,0:T(8,128)S(1)}, f32[128,128]{1,0:T(8,128)S(1)}, u32[]{:S(2)}, u32[]{:S(2)}) collective-permute-start(f32[128,128]{1,0:T(8,128)S(1)} %get-tuple-element.40), channel_id=1, source_target_pairs={{0,8},{4,12},{8,0},{12,4},{16,24},{20,28},{24,16},{28,20},{1,9},{5... | collective-permute-start | bytes 196616 | tf_op jit(solution)/shard_map/ppermute | solution.py:138
  11.3 5.6 %collective-permute-start.3 = (f32[128,128]{1,0:T(8,128)S(1)}, f32[128,128]{1,0:T(8,128)S(1)}, u32[]{:S(2)}, u32[]{:S(2)}) collective-permute-start(f32[128,128]{1,0:T(8,128)S(1)} %get-tuple-element.39), channel_id=1, source_target_pairs={{0,12},{4,8},{8,4},{12,0},{16,28},{20,24},{24,20},{28,16},{1,13},{... | collective-permute-start | bytes 196616 | tf_op jit(solution)/shard_map/ppermute | solution.py:138
  16.9 5.6 %copy-start.5 = (bf16[128,512]{1,0:T(8,128)(2,1)S(1)}, bf16[128,512]{1,0:T(8,128)(2,1)}, u32[]{:S(2)}) copy-start(bf16[128,512]{1,0:T(8,128)(2,1)} %v_ref.5) | copy-start | bytes 393220
  16.9 5.6 %copy-start.7 = (bf16[128,512]{1,0:T(8,128)(2,1)S(1)}, bf16[128,512]{1,0:T(8,128)(2,1)}, u32[]{:S(2)}) copy-start(bf16[128,512]{1,0:T(8,128)(2,1)} %g_ref.5) | copy-start | bytes 393220
  16.9 5.6 %copy-start.1 = (bf16[128,512]{1,0:T(8,128)(2,1)S(1)}, bf16[128,512]{1,0:T(8,128)(2,1)}, u32[]{:S(2)}) copy-start(bf16[128,512]{1,0:T(8,128)(2,1)} %q_ref.5) | copy-start | bytes 393220
  16.9 5.5 %copy-start.3 = (bf16[128,512]{1,0:T(8,128)(2,1)S(1)}, bf16[128,512]{1,0:T(8,128)(2,1)}, u32[]{:S(2)}) copy-start(bf16[128,512]{1,0:T(8,128)(2,1)} %k_ref.5) | copy-start | bytes 393220
  16.9 11.0 %collective-permute-start.4 = (f32[256,128]{1,0:T(8,128)S(1)}, f32[256,128]{1,0:T(8,128)S(1)}, u32[]{:S(2)}, u32[]{:S(2)}) collective-permute-start(f32[256,128]{1,0:T(8,128)S(1)} %pad_maximum_fusion), channel_id=1, source_target_pairs={{0,4},{4,0},{8,12},{12,8},{16,20},{20,16},{24,28},{28,24},{1,5},{5... | collective-permute-start | bytes 393224 | tf_op jit(solution)/shard_map/ppermute | solution.py:138
  18.0 5.8 %collective-permute-start.7 = (f32[128,128]{1,0:T(8,128)S(1)}, f32[128,128]{1,0:T(8,128)S(1)}, u32[]{:S(2)}, u32[]{:S(2)}) collective-permute-start(f32[128,128]{1,0:T(8,128)S(1)} %get-tuple-element.39), channel_id=1, source_target_pairs={{0,4},{4,0},{8,12},{12,8},{16,20},{20,16},{24,28},{28,24},{1,5},{5... | collective-permute-start | bytes 196616 | tf_op jit(solution)/shard_map/ppermute | solution.py:138
  19.0 7.8 %collective-permute-start.6 = (f32[128,128]{1,0:T(8,128)S(1)}, f32[128,128]{1,0:T(8,128)S(1)}, u32[]{:S(2)}, u32[]{:S(2)}) collective-permute-start(f32[128,128]{1,0:T(8,128)S(1)} %get-tuple-element.28), channel_id=1, source_target_pairs={{0,20},{4,16},{8,28},{12,24},{16,4},{20,0},{24,12},{28,8},{1,21},{... | collective-permute-start | bytes 196616 | tf_op jit(solution)/shard_map/ppermute | solution.py:138
  22.1 5.8 %collective-permute-start.8 = (f32[128,128]{1,0:T(8,128)S(1)}, f32[128,128]{1,0:T(8,128)S(1)}, u32[]{:S(2)}, u32[]{:S(2)}) collective-permute-start(f32[128,128]{1,0:T(8,128)S(1)} %get-tuple-element.28), channel_id=1, source_target_pairs={{0,16},{4,20},{8,24},{12,28},{16,0},{20,4},{24,8},{28,12},{1,17},{... | collective-permute-start | bytes 196616 | tf_op jit(solution)/shard_map/ppermute | solution.py:138
  28.2 3.6 %collective-permute-start.10 = (f32[1,128]{1,0:T(1,128)S(1)}, f32[1,128]{1,0:T(1,128)S(1)}, u32[]{:S(2)}, u32[]{:S(2)}) collective-permute-start(f32[1,128]{1,0:T(1,128)S(1)} %get-tuple-element.19), channel_id=1, source_target_pairs={{0,2},{1,3},{2,0},{3,1},{4,6},{5,7},{6,4},{7,5},{8,10},{9,11},{10,... | collective-permute-start | bytes 1544 | tf_op jit(solution)/shard_map/ppermute | solution.py:138
  29.8 3.0 %collective-permute-start.11 = (f32[1,128]{1,0:T(1,128)S(1)}, f32[1,128]{1,0:T(1,128)S(1)}, u32[]{:S(2)}, u32[]{:S(2)}) collective-permute-start(f32[1,128]{1,0:T(1,128)S(1)} %get-tuple-element.19), channel_id=1, source_target_pairs={{0,3},{1,2},{2,1},{3,0},{4,7},{5,6},{6,5},{7,4},{8,11},{9,10},{10,... | collective-permute-start | bytes 1544 | tf_op jit(solution)/shard_map/ppermute | solution.py:138
  29.8 3.0 %collective-permute-start.9 = (f32[1,128]{1,0:T(1,128)S(1)}, f32[1,128]{1,0:T(1,128)S(1)}, u32[]{:S(2)}, u32[]{:S(2)}) collective-permute-start(f32[1,128]{1,0:T(1,128)S(1)} %get-tuple-element.19), channel_id=1, source_target_pairs={{0,1},{1,0},{2,3},{3,2},{4,5},{5,4},{6,7},{7,6},{8,9},{9,8},{10,11... | collective-permute-start | bytes 1544 | tf_op jit(solution)/shard_map/ppermute | solution.py:138
  32.8 0.7 %copy-start.8 = (f32[512]{0:T(512)S(1)}, f32[512]{0:T(512)}, u32[]{:S(2)}) copy-start(f32[512]{0:T(512)} %param.9) | copy-start | bytes 6148

commit v2 on v1

--- a/solution.py
+++ b/solution.py
@@ -11,6 +11,7 @@
 HEAD_DIM = 64
 BLOCK = 128
 LANES = 128
+MIB = 2**20
 
 epsilon = 1e-06
 
@@ -56,14 +57,27 @@
     return jnp.concatenate([jnp.where(low, state, zero), jnp.where(low, zero, state)], axis=0)
 
 
-def states_kernel(q_ref, k_ref, v_ref, g_ref, kv_ref, qg_ref):
+def states_kernel(q_hbm, k_hbm, v_hbm, g_hbm, kv_ref, qg_ref, q_ref, k_ref, v_ref, g_ref, sems):
+    sources = (k_hbm, v_hbm, g_hbm, q_hbm)
+    targets = (k_ref, v_ref, g_ref, q_ref)
+    copies = [
+        pltpu.make_async_copy(source, target, sems.at[i])
+        for i, (source, target) in enumerate(zip(sources, targets))
+    ]
+    for copy in copies:
+        copy.start()
+    for copy in copies:
+        copy.wait()
     for t in range(tiles(q_ref)):
         rows = slice(t * HEAD_DIM, (t + 1) * HEAD_DIM)
         kv_ref[rows] = pack_state(dot(tile(k_ref, t), tile(v_ref, t), TN))
         qg_ref[rows] = pack_state(dot(tile(g_ref, t), tile(q_ref, t), TN))
 
 
-def block_kernel(factor, q_ref, k_ref, v_ref, g_ref, out_ref, dq_ref, dk_ref, dv_ref):
+def block_kernel(
+    factor, q_ref, k_ref, v_ref, g_ref, gain_ref, out_ref, dq_ref, dk_ref, dv_ref, row_ref
+):
+    row_ref[...] = gain_ref[...]
     row = lax.broadcasted_iota(jnp.int32, (BLOCK, BLOCK), 0)
     column = lax.broadcasted_iota(jnp.int32, (BLOCK, BLOCK), 1)
     causal = row >= column
@@ -119,17 +133,18 @@
         normed_ref[:, cols] = (out_ref[:, cols] * scale * gain_ref[:, cols]).astype(bf16)
 
 
-def call(kernel, outs, args, flops):
+def call(kernel, outs, args, flops, vmem=16 * MIB, **spec):
     moved = sum(math.prod(a.shape) * jnp.dtype(a.dtype).itemsize for a in (*args, *outs))
     whole = pl.BlockSpec(memory_space=pltpu.VMEM)
     single = len(outs) == 1
     return pl.pallas_call(
         kernel,
         out_shape=outs[0] if single else tuple(outs),
-        in_specs=[whole] * len(args),
+        in_specs=[pl.BlockSpec(memory_space=spec.pop("inputs_at", pltpu.VMEM))] * len(args),
         out_specs=whole if single else tuple([whole] * len(outs)),
-        compiler_params=pltpu.CompilerParams(vmem_limit_bytes=16 * 2**20),
+        compiler_params=pltpu.CompilerParams(vmem_limit_bytes=vmem),
         cost_estimate=pl.CostEstimate(flops=flops, bytes_accessed=moved, transcendentals=0),
+        **spec,
     )(*args)
 
 
@@ -162,7 +177,7 @@
             jnp.sum(jnp.where(position < index, every_kv, 0.0), axis=0),
             jnp.sum(jnp.where(position > index, every_qg, 0.0), axis=0),
         )
-    if count < 8:
+    if count < 4:
         before, after, total_kv, total_qg = zero, zero, kv, qg
         distance = 1
         while distance < count:
@@ -175,31 +190,25 @@
     odd, upper = bit(1), bit(top)
     a, b = jnp.where(upper, qg, kv), jnp.where(upper, kv, qg)
     (a_mine, a_other), (b_mine, b_other) = halves(a, odd), halves(b, odd)
-    a1 = swap(a_other, axis, 1)
-    a2 = swap(a_mine, axis, 2)
-    a3 = swap(a_other, axis, 3)
-    b1 = swap(b_other, axis, 1)
-    b2 = swap(b_mine, axis, 2)
-    b3 = swap(b_other, axis, 3)
+    mid = a_mine.shape[0]
     a_enters = lambda d: bit(d) != upper
     b_enters = lambda d: bit(d) == upper
-    a_pair, b_pair = a2 + a3, b2 + b3
-    a_sum = jnp.where(a_enters(2), a_pair, 0.0)
-    b_sum = jnp.where(b_enters(2), b_pair, 0.0)
-    a_total, b_total = a_mine + a1 + a_pair, b_mine + b1 + b_pair
-    distance = 4
+    got = swap(jnp.concatenate([a_other, b_other], axis=0), axis, 1)
+    a1, b1 = got[:mid], got[mid:]
+    a_total, b_total = a_mine + a1, b_mine + b1
+    a_sum = b_sum = jnp.zeros_like(a_mine)
+    distance = 2
     while distance < top:
-        a_got, b_got = swap(a_total, axis, distance), swap(b_total, axis, distance)
-        a_sum = a_sum + jnp.where(a_enters(distance), a_got, 0.0)
-        b_sum = b_sum + jnp.where(b_enters(distance), b_got, 0.0)
-        a_total, b_total = a_total + a_got, b_total + b_got
+        got = swap(jnp.concatenate([a_total, b_total], axis=0), axis, distance)
+        a_sum = a_sum + jnp.where(a_enters(distance), got[:mid], 0.0)
+        b_sum = b_sum + jnp.where(b_enters(distance), got[mid:], 0.0)
+        a_total, b_total = a_total + got[:mid], b_total + got[mid:]
         distance *= 2
+    t_other = swap(a_total, axis, top | 1)
     t_mine = swap(a_total, axis, top)
-    t_other = swap(a_total, axis, top | 1)
     a_out = a_sum + jnp.where(a_enters(1), 0.0, a_mine)
     b_out = b_sum + jnp.where(b_enters(1), 0.0, b_mine)
     got = swap(jnp.concatenate([a_out, b_out], axis=0), axis, 1)
-    mid = a_mine.shape[0]
     a_own = a_sum + jnp.where(a_enters(1), a1, 0.0)
     b_own = b_sum + jnp.where(b_enters(1), b1, 0.0) + t_mine
     a_all = join(a_own, got[:mid], odd)
@@ -223,13 +232,24 @@
 def body(queries, keys, values, d_out, gain):
     length, width = queries.shape
     factor = 1.0 / math.sqrt(HEAD_DIM * length * lax.axis_size("seq"))
-    row_bytes = jax.ShapeDtypeStruct((width // LANES * HEAD_DIM, LANES), f32)
+    packed = jax.ShapeDtypeStruct((width // LANES * HEAD_DIM, LANES), f32)
     wide = jax.ShapeDtypeStruct((length, width), f32)
     narrow = jax.ShapeDtypeStruct((length, width), bf16)
     inputs = (queries, keys, values, d_out)
-    kv, qg = call(states_kernel, [row_bytes] * 2, inputs, 4 * length * LANES * width)
-    out_part, dq_part, dk_part, dv_part = call(
-        functools.partial(block_kernel, factor), [wide] * 4, inputs, 24 * length * LANES * width
+    kv, qg = call(
+        states_kernel,
+        [packed] * 2,
+        inputs,
+        4 * length * LANES * width,
+        vmem=64 * MIB - 10600 * 1024,
+        inputs_at=pltpu.HBM,
+        scratch_shapes=[pltpu.VMEM((length, width), bf16)] * 4 + [pltpu.SemaphoreType.DMA((4,))],
+    )
+    out_part, dq_part, dk_part, dv_part, gain_row = call(
+        functools.partial(block_kernel, factor),
+        [wide] * 4 + [jax.ShapeDtypeStruct((1, width), f32)],
+        (*inputs, gain[None]),
+        24 * length * LANES * width,
     )
     before, after = scan_states(kv, qg, "seq")
     out, squares = call(
@@ -248,7 +268,7 @@
     normed = call(
         functools.partial(norm_kernel, width * lax.axis_size("head")),
         [narrow],
-        (out, shares, gain[None]),
+        (out, shares, gain_row),
         2 * length * width,
     )
     return normed, dq, dk, dv

time: 34.5 us -> 29.3 us (0.85)
  starting transfers between devices: 15.8 us -> 11.3 us
  local copies, waits for them, and re-layouts: 4.31 us -> 0.03 us
  waiting for transfers between devices: 9.51 us -> 11.9 us
  Pallas kernels: 3.75 us -> 4.91 us
    ppermute x12 -> x8, starting transfers between devices: 15.8 us -> 11.3 us  [swap(): return lax.ppermute(x, axis, [(i, i ^ distance) for i in range(size)])]
    unnamed x18 -> x10, local copies, waits for them, and re-layouts: 4.31 us -> 0.03 us
    ppermute x12 -> x8, waiting for transfers between devices: 9.51 us -> 11.9 us  [swap(): return lax.ppermute(x, axis, [(i, i ^ distance) for i in range(size)])]
    pallas_call x5, Pallas kernels: 3.75 us -> 4.91 us  [call(): pl.pallas_call(kernel, out_shape=outs[0] if single else tuple(outs), in_s...]
  transfers between devices with their start and end apart: 12 -> 8, of which waited for: 7 -> 6; matrix products, arithmetic and copies ran while one was open for 0% -> 0% of each run, Pallas kernels for 7% -> 8%
where the time goes in v2:
time: 29.3 us; the launch traced here: 29.2 us
  waiting for transfers between devices  11.9 us (41%)
  starting transfers between devices  11.3 us (39%)
  Pallas kernels  4.91 us (17%)
  between operations  0.78 us (3%)
    ppermute x8, waiting for transfers between devices, swap(): return lax.ppermute(x, axis, [(i, i ^ distance) for i in range(size)])  11.9 us
    ppermute x8, starting transfers between devices, swap(): return lax.ppermute(x, axis, [(i, i ^ distance) for i in range(size)])  11.3 us
    pallas_call x5, Pallas kernels, call(): pl.pallas_call(kernel, out_shape=outs[0] if single else tuple(outs), in_s...  4.91 us
  transfers between devices with their start and end apart: 8, of which 6 were waited for; matrix products, arithmetic and copies ran while one was open for 0% of the time, Pallas kernels for 8%

profile of v2, /device:TPU:0, one launch (start us, length us, event | category | flops | bytes accessed | tf_op | source)
XLA Modules:
  0.0 29.2 jit_solution(14033623770478130026)
XLA Ops:
  0.6 1.4 %shard_map.85 = (f32[256,128]{1,0:T(8,128)S(1)}, f32[256,128]{1,0:T(8,128)S(1)}) custom-call(bf16[128,512]{1,0:T(8,128)(2,1)} %q_ref.3, bf16[128,512]{1,0:T(8,128)(2,1)} %k_ref.3, bf16[128,512]{1,0:T(8,128)(2,1)} %v_ref.3, bf16[128,512]{1,0:T(8,128)(2,1)} %g_ref.3), custom_call_target="tpu_custom_call" | custom-call | flops 33554432 | bytes 786432 | tf_op jit(solution)/shard_map/pallas_call | solution.py:140
  2.1 3.0 %collective-permute-start = (f32[256,128]{1,0:T(8,128)S(1)}, f32[256,128]{1,0:T(8,128)S(1)}, u32[]{:S(2)}, u32[]{:S(2)}) collective-permute-start(f32[256,128]{1,0:T(8,128)S(1)} %pad_maximum_fusion), channel_id=1, source_target_pairs={{0,4},{4,0},{8,12},{12,8},{16,20},{20,16},{24,28},{28,24},{1,5},{5... | collective-permute-start | bytes 393224 | tf_op jit(solution)/shard_map/ppermute | solution.py:153
  5.1 3.5 %collective-permute-done = f32[256,128]{1,0:T(8,128)S(1)} collective-permute-done((f32[256,128]{1,0:T(8,128)S(1)}, f32[256,128]{1,0:T(8,128)S(1)}, u32[]{:S(2)}, u32[]{:S(2)}) %collective-permute-start) | collective-permute-done | bytes 131104 | tf_op jit(solution)/shard_map/ppermute | solution.py:153
  8.7 1.9 %collective-permute-start.1 = (f32[256,128]{1,0:T(8,128)S(1)}, f32[256,128]{1,0:T(8,128)S(1)}, u32[]{:S(2)}, u32[]{:S(2)}) collective-permute-start(f32[256,128]{1,0:T(8,128)S(1)} %pad_maximum_fusion.1), channel_id=1, source_target_pairs={{0,8},{4,12},{8,0},{12,4},{16,24},{20,28},{24,16},{28,20},{1,9},{5... | collective-permute-start | bytes 393224 | tf_op jit(solution)/shard_map/ppermute | solution.py:153
  10.6 3.1 %collective-permute-done.1 = f32[256,128]{1,0:T(8,128)S(1)} collective-permute-done((f32[256,128]{1,0:T(8,128)S(1)}, f32[256,128]{1,0:T(8,128)S(1)}, u32[]{:S(2)}, u32[]{:S(2)}) %collective-permute-start.1) | collective-permute-done | bytes 131104 | tf_op jit(solution)/shard_map/ppermute | solution.py:153
  13.7 0.0 copy-start.2
  13.7 0.0 copy-start.3
  13.8 0.0 copy-start
  13.8 0.0 copy-start.1
  13.8 0.0 copy-start.4
  13.8 1.8 %collective-permute-start.2 = (f32[256,128]{1,0:T(8,128)S(1)}, f32[256,128]{1,0:T(8,128)S(1)}, u32[]{:S(2)}, u32[]{:S(2)}) collective-permute-start(f32[256,128]{1,0:T(8,128)S(1)} %pad_maximum_fusion.2), channel_id=1, source_target_pairs={{0,4},{4,0},{8,12},{12,8},{16,20},{20,16},{24,28},{28,24},{1,5},{5... | collective-permute-start | bytes 393224 | tf_op jit(solution)/shard_map/ppermute | solution.py:153
  15.6 2.6 %collective-permute-start.3 = (f32[128,128]{1,0:T(8,128)S(1)}, f32[128,128]{1,0:T(8,128)S(1)}, u32[]{:S(2)}, u32[]{:S(2)}) collective-permute-start(f32[128,128]{1,0:T(8,128)S(1)} %get-tuple-element.36), channel_id=1, source_target_pairs={{0,20},{4,16},{8,28},{12,24},{16,4},{20,0},{24,12},{28,8},{1,21},{... | collective-permute-start | bytes 196616 | tf_op jit(solution)/shard_map/ppermute | solution.py:153
  18.2 0.1 collective-permute-start.4
  18.3 0.0 copy-done.2
  18.3 0.0 copy-done.3
  18.3 0.0 copy-done
  18.3 0.0 copy-done.1
  18.3 0.0 copy-done.4
  18.3 1.4 %shard_map.84 = (f32[128,512]{1,0:T(8,128)S(1)}, f32[128,512]{1,0:T(8,128)S(1)}, f32[128,512]{1,0:T(8,128)S(1)}, f32[128,512]{1,0:T(8,128)S(1)}, f32[1,512]{1,0:T(1,128)S(1)}) custom-call(bf16[128,512]{1,0:T(8,128)(2,1)S(1)} %copy-done, bf16[128,512]{1,0:T(8,128)(2,1)S(1)} %copy-done.1, bf16[128,512]{1,0:T(8,128)(2,1)S(1)} %copy-done.2, ...), custom_call_target="tpu_custom_call" | custom-call | flops 201326592 | bytes 1576960 | tf_op jit(solution)/shard_map/pallas_call | solution.py:140
  19.7 3.3 %collective-permute-done.3 = f32[128,128]{1,0:T(8,128)S(1)} collective-permute-done((f32[128,128]{1,0:T(8,128)S(1)}, f32[128,128]{1,0:T(8,128)S(1)}, u32[]{:S(2)}, u32[]{:S(2)}) %collective-permute-start.3) | collective-permute-done | bytes 65568 | tf_op jit(solution)/shard_map/ppermute | solution.py:153
  23.0 0.4 %collective-permute-done.4 = f32[128,128]{1,0:T(8,128)S(1)} collective-permute-done((f32[128,128]{1,0:T(8,128)S(1)}, f32[128,128]{1,0:T(8,128)S(1)}, u32[]{:S(2)}, u32[]{:S(2)}) %collective-permute-start.4) | collective-permute-done | bytes 65568 | tf_op jit(solution)/shard_map/ppermute | solution.py:153
  23.3 0.0 collective-permute-done.2
  23.4 0.3 shard_map.86
  23.7 0.1 collective-permute-start.5
  23.8 1.6 %collective-permute-start.6 = (f32[1,128]{1,0:T(1,128)S(1)}, f32[1,128]{1,0:T(1,128)S(1)}, u32[]{:S(2)}, u32[]{:S(2)}) collective-permute-start(f32[1,128]{1,0:T(1,128)S(1)} %get-tuple-element.20), channel_id=1, source_target_pairs={{0,2},{1,3},{2,0},{3,1},{4,6},{5,7},{6,4},{7,5},{8,10},{9,11},{10,... | collective-permute-start | bytes 1544 | tf_op jit(solution)/shard_map/ppermute | solution.py:153
  25.4 0.3 collective-permute-start.7
  25.6 1.0 %shard_map.88 = (bf16[128,512]{1,0:T(8,128)(2,1)}, bf16[128,512]{1,0:T(8,128)(2,1)}, bf16[128,512]{1,0:T(8,128)(2,1)}) custom-call(bf16[128,512]{1,0:T(8,128)(2,1)S(1)} %copy-done.1, bf16[128,512]{1,0:T(8,128)(2,1)S(1)} %copy-done.2, bf16[128,512]{1,0:T(8,128)(2,1)S(1)} %copy-done.3, f32[128,512]{1,0:T(8,128)S(1)} %get-tuple-element.22.dq_part, ...), custom_call_target="tpu_custom_call" | custom-call | flops 50331648 | bytes 1835008 | tf_op jit(solution)/shard_map/pallas_call | solution.py:140
  26.7 0.0 collective-permute-done.5
  26.7 0.7 %collective-permute-done.6 = f32[1,128]{1,0:T(1,128)S(1)} collective-permute-done((f32[1,128]{1,0:T(1,128)S(1)}, f32[1,128]{1,0:T(1,128)S(1)}, u32[]{:S(2)}, u32[]{:S(2)}) %collective-permute-start.6) | collective-permute-done | bytes 544 | tf_op jit(solution)/shard_map/ppermute | solution.py:153
  27.4 0.9 %collective-permute-done.7 = f32[1,128]{1,0:T(1,128)S(1)} collective-permute-done((f32[1,128]{1,0:T(1,128)S(1)}, f32[1,128]{1,0:T(1,128)S(1)}, u32[]{:S(2)}, u32[]{:S(2)}) %collective-permute-start.7) | collective-permute-done | bytes 544 | tf_op jit(solution)/shard_map/ppermute | solution.py:153
  28.4 0.8 %shard_map.87 = bf16[128,512]{1,0:T(8,128)(2,1)} custom-call(f32[128,512]{1,0:T(8,128)S(1)} %get-tuple-element.19.out_ref, f32[4,128]{1,0:T(4,128)S(1)} %pad_maximum_fusion.5.squares_ref, f32[1,512]{1,0:T(1,128)S(1)} %get-tuple-element.21.gain_ref), custom_call_target="tpu_custom_call" | custom-call | flops 131072 | bytes 397312 | tf_op jit(solution)/shard_map/pallas_call | solution.py:140
  (11 shorter events, 0.2 us)
Async XLA Ops:
  2.1 6.5 %collective-permute-start = (f32[256,128]{1,0:T(8,128)S(1)}, f32[256,128]{1,0:T(8,128)S(1)}, u32[]{:S(2)}, u32[]{:S(2)}) collective-permute-start(f32[256,128]{1,0:T(8,128)S(1)} %pad_maximum_fusion), channel_id=1, source_target_pairs={{0,4},{4,0},{8,12},{12,8},{16,20},{20,16},{24,28},{28,24},{1,5},{5... | collective-permute-start | bytes 393224 | tf_op jit(solution)/shard_map/ppermute | solution.py:153
  8.7 5.0 %collective-permute-start.1 = (f32[256,128]{1,0:T(8,128)S(1)}, f32[256,128]{1,0:T(8,128)S(1)}, u32[]{:S(2)}, u32[]{:S(2)}) collective-permute-start(f32[256,128]{1,0:T(8,128)S(1)} %pad_maximum_fusion.1), channel_id=1, source_target_pairs={{0,8},{4,12},{8,0},{12,4},{16,24},{20,28},{24,16},{28,20},{1,9},{5... | collective-permute-start | bytes 393224 | tf_op jit(solution)/shard_map/ppermute | solution.py:153
  13.7 4.5 %copy-start.2 = (bf16[128,512]{1,0:T(8,128)(2,1)S(1)}, bf16[128,512]{1,0:T(8,128)(2,1)}, u32[]{:S(2)}) copy-start(bf16[128,512]{1,0:T(8,128)(2,1)} %v_ref.3) | copy-start | bytes 393220
  13.7 4.5 %copy-start.3 = (bf16[128,512]{1,0:T(8,128)(2,1)S(1)}, bf16[128,512]{1,0:T(8,128)(2,1)}, u32[]{:S(2)}) copy-start(bf16[128,512]{1,0:T(8,128)(2,1)} %g_ref.3) | copy-start | bytes 393220
  13.8 4.5 %copy-start = (bf16[128,512]{1,0:T(8,128)(2,1)S(1)}, bf16[128,512]{1,0:T(8,128)(2,1)}, u32[]{:S(2)}) copy-start(bf16[128,512]{1,0:T(8,128)(2,1)} %q_ref.3) | copy-start | bytes 393220
  13.8 4.5 %copy-start.1 = (bf16[128,512]{1,0:T(8,128)(2,1)S(1)}, bf16[128,512]{1,0:T(8,128)(2,1)}, u32[]{:S(2)}) copy-start(bf16[128,512]{1,0:T(8,128)(2,1)} %k_ref.3) | copy-start | bytes 393220
  13.8 4.5 %copy-start.4 = (f32[512]{0:T(512)S(1)}, f32[512]{0:T(512)}, u32[]{:S(2)}) copy-start(f32[512]{0:T(512)} %param.9) | copy-start | bytes 6148
  13.8 9.5 %collective-permute-start.2 = (f32[256,128]{1,0:T(8,128)S(1)}, f32[256,128]{1,0:T(8,128)S(1)}, u32[]{:S(2)}, u32[]{:S(2)}) collective-permute-start(f32[256,128]{1,0:T(8,128)S(1)} %pad_maximum_fusion.2), channel_id=1, source_target_pairs={{0,4},{4,0},{8,12},{12,8},{16,20},{20,16},{24,28},{28,24},{1,5},{5... | collective-permute-start | bytes 393224 | tf_op jit(solution)/shard_map/ppermute | solution.py:153
  15.6 7.4 %collective-permute-start.3 = (f32[128,128]{1,0:T(8,128)S(1)}, f32[128,128]{1,0:T(8,128)S(1)}, u32[]{:S(2)}, u32[]{:S(2)}) collective-permute-start(f32[128,128]{1,0:T(8,128)S(1)} %get-tuple-element.36), channel_id=1, source_target_pairs={{0,20},{4,16},{8,28},{12,24},{16,4},{20,0},{24,12},{28,8},{1,21},{... | collective-permute-start | bytes 196616 | tf_op jit(solution)/shard_map/ppermute | solution.py:153
  18.2 5.2 %collective-permute-start.4 = (f32[128,128]{1,0:T(8,128)S(1)}, f32[128,128]{1,0:T(8,128)S(1)}, u32[]{:S(2)}, u32[]{:S(2)}) collective-permute-start(f32[128,128]{1,0:T(8,128)S(1)} %get-tuple-element.36), channel_id=1, source_target_pairs={{0,16},{4,20},{8,24},{12,28},{16,0},{20,4},{24,8},{28,12},{1,17},{... | collective-permute-start | bytes 196616 | tf_op jit(solution)/shard_map/ppermute | solution.py:153
  23.7 3.0 %collective-permute-start.5 = (f32[1,128]{1,0:T(1,128)S(1)}, f32[1,128]{1,0:T(1,128)S(1)}, u32[]{:S(2)}, u32[]{:S(2)}) collective-permute-start(f32[1,128]{1,0:T(1,128)S(1)} %get-tuple-element.20), channel_id=1, source_target_pairs={{0,1},{1,0},{2,3},{3,2},{4,5},{5,4},{6,7},{7,6},{8,9},{9,8},{10,11... | collective-permute-start | bytes 1544 | tf_op jit(solution)/shard_map/ppermute | solution.py:153
  23.8 3.6 %collective-permute-start.6 = (f32[1,128]{1,0:T(1,128)S(1)}, f32[1,128]{1,0:T(1,128)S(1)}, u32[]{:S(2)}, u32[]{:S(2)}) collective-permute-start(f32[1,128]{1,0:T(1,128)S(1)} %get-tuple-element.20), channel_id=1, source_target_pairs={{0,2},{1,3},{2,0},{3,1},{4,6},{5,7},{6,4},{7,5},{8,10},{9,11},{10,... | collective-permute-start | bytes 1544 | tf_op jit(solution)/shard_map/ppermute | solution.py:153
  25.4 3.0 %collective-permute-start.7 = (f32[1,128]{1,0:T(1,128)S(1)}, f32[1,128]{1,0:T(1,128)S(1)}, u32[]{:S(2)}, u32[]{:S(2)}) collective-permute-start(f32[1,128]{1,0:T(1,128)S(1)} %get-tuple-element.20), channel_id=1, source_target_pairs={{0,3},{1,2},{2,1},{3,0},{4,7},{5,6},{6,5},{7,4},{8,11},{9,10},{10,... | collective-permute-start | bytes 1544 | tf_op jit(solution)/shard_map/ppermute | solution.py:153

commit v3 on v2

--- a/solution.py
+++ b/solution.py
@@ -7,6 +7,7 @@
 from jax.experimental import pallas as pl
 from jax.experimental.pallas import tpu as pltpu
 from jax.sharding import PartitionSpec as P
+
 
 HEAD_DIM = 64
 BLOCK = 128
@@ -189,26 +190,31 @@
         return before, after
     odd, upper = bit(1), bit(top)
     a, b = jnp.where(upper, qg, kv), jnp.where(upper, kv, qg)
-    (a_mine, a_other), (b_mine, b_other) = halves(a, odd), halves(b, odd)
-    mid = a_mine.shape[0]
     a_enters = lambda d: bit(d) != upper
     b_enters = lambda d: bit(d) == upper
-    got = swap(jnp.concatenate([a_other, b_other], axis=0), axis, 1)
-    a1, b1 = got[:mid], got[mid:]
+
+    def send(x, distance):
+        return swap(x, axis, distance)
+
+    (a_mine, a_other), (b_mine, b_other) = halves(a, odd), halves(b, odd)
+    a1 = send(a_other, 1)
+    b1 = send(b_other, 1)
     a_total, b_total = a_mine + a1, b_mine + b1
     a_sum = b_sum = jnp.zeros_like(a_mine)
     distance = 2
     while distance < top:
-        got = swap(jnp.concatenate([a_total, b_total], axis=0), axis, distance)
-        a_sum = a_sum + jnp.where(a_enters(distance), got[:mid], 0.0)
-        b_sum = b_sum + jnp.where(b_enters(distance), got[mid:], 0.0)
-        a_total, b_total = a_total + got[:mid], b_total + got[mid:]
+        a_got = send(a_total, distance)
+        b_got = send(b_total, distance)
+        a_sum = a_sum + jnp.where(a_enters(distance), a_got, 0.0)
+        b_sum = b_sum + jnp.where(b_enters(distance), b_got, 0.0)
+        a_total, b_total = a_total + a_got, b_total + b_got
         distance *= 2
-    t_other = swap(a_total, axis, top | 1)
-    t_mine = swap(a_total, axis, top)
+    t_other = send(a_total, top | 1)
+    t_mine = send(a_total, top)
     a_out = a_sum + jnp.where(a_enters(1), 0.0, a_mine)
     b_out = b_sum + jnp.where(b_enters(1), 0.0, b_mine)
-    got = swap(jnp.concatenate([a_out, b_out], axis=0), axis, 1)
+    got = send(jnp.concatenate([a_out, b_out], axis=0), 1)
+    mid = a_mine.shape[0]
     a_own = a_sum + jnp.where(a_enters(1), a1, 0.0)
     b_own = b_sum + jnp.where(b_enters(1), b1, 0.0) + t_mine
     a_all = join(a_own, got[:mid], odd)

time: 29.3 us -> 30.5 us (1.041)
  starting transfers between devices: 11.3 us -> 13.2 us
  waiting for transfers between devices: 11.9 us -> 11.2 us
    ppermute x8 -> x10, starting transfers between devices: 11.3 us -> 13.2 us  [swap(): return lax.ppermute(x, axis, [(i, i ^ distance) for i in range(size)])]
    ppermute x8 -> x10, waiting for transfers between devices: 11.9 us -> 11.2 us  [swap(): return lax.ppermute(x, axis, [(i, i ^ distance) for i in range(size)])]
  transfers between devices with their start and end apart: 8 -> 10, of which waited for: 6 -> 7; matrix products, arithmetic and copies ran while one was open for 0% -> 0% of each run, Pallas kernels for 8% -> 8%
where the time goes in v3:
time: 30.5 us; the launch traced here: 30.3 us
  starting transfers between devices  13.2 us (43%)
  waiting for transfers between devices  11.2 us (37%)
  Pallas kernels  4.91 us (16%)
  between operations  0.78 us (3%)
    ppermute x10, starting transfers between devices, swap(): return lax.ppermute(x, axis, [(i, i ^ distance) for i in range(size)])  13.2 us
    ppermute x10, waiting for transfers between devices, swap(): return lax.ppermute(x, axis, [(i, i ^ distance) for i in range(size)])  11.2 us
    pallas_call x5, Pallas kernels, call(): pl.pallas_call(kernel, out_shape=outs[0] if single else tuple(outs), in_s...  4.91 us
  transfers between devices with their start and end apart: 10, of which 7 were waited for; matrix products, arithmetic and copies ran while one was open for 0% of the time, Pallas kernels for 8%

profile of v3, /device:TPU:0, one launch (start us, length us, event | category | flops | bytes accessed | tf_op | source)
XLA Modules:
  0.0 30.3 jit_solution(10124173901147178854)
XLA Ops:
  0.6 1.4 %shard_map.85 = (f32[256,128]{1,0:T(8,128)S(1)}, f32[256,128]{1,0:T(8,128)S(1)}) custom-call(bf16[128,512]{1,0:T(8,128)(2,1)} %q_ref.3, bf16[128,512]{1,0:T(8,128)(2,1)} %k_ref.3, bf16[128,512]{1,0:T(8,128)(2,1)} %v_ref.3, bf16[128,512]{1,0:T(8,128)(2,1)} %g_ref.3), custom_call_target="tpu_custom_call" | custom-call | flops 33554432 | bytes 786432 | tf_op jit(solution)/shard_map/pallas_call | solution.py:141
  2.1 3.0 %collective-permute-start = (f32[128,128]{1,0:T(8,128)S(1)}, f32[128,128]{1,0:T(8,128)S(1)}, u32[]{:S(2)}, u32[]{:S(2)}) collective-permute-start(f32[128,128]{1,0:T(8,128)S(1)} %slice_select_fusion.4), channel_id=1, source_target_pairs={{0,4},{4,0},{8,12},{12,8},{16,20},{20,16},{24,28},{28,24},{1,5},{5... | collective-permute-start | bytes 196616 | tf_op jit(solution)/shard_map/ppermute | solution.py:154
  5.1 0.1 collective-permute-start.2
  5.2 2.1 %collective-permute-done = f32[128,128]{1,0:T(8,128)S(1)} collective-permute-done((f32[128,128]{1,0:T(8,128)S(1)}, f32[128,128]{1,0:T(8,128)S(1)}, u32[]{:S(2)}, u32[]{:S(2)}) %collective-permute-start) | collective-permute-done | bytes 65568 | tf_op jit(solution)/shard_map/ppermute | solution.py:154
  7.4 2.7 %collective-permute-start.1 = (f32[128,128]{1,0:T(8,128)S(1)}, f32[128,128]{1,0:T(8,128)S(1)}, u32[]{:S(2)}, u32[]{:S(2)}) collective-permute-start(f32[128,128]{1,0:T(8,128)S(1)} %fusion.2), channel_id=1, source_target_pairs={{0,8},{4,12},{8,0},{12,4},{16,24},{20,28},{24,16},{28,20},{1,9},{5... | collective-permute-start | bytes 196616 | tf_op jit(solution)/shard_map/ppermute | solution.py:154
  10.1 0.0 collective-permute-done.2
  10.1 1.0 %collective-permute-start.3 = (f32[128,128]{1,0:T(8,128)S(1)}, f32[128,128]{1,0:T(8,128)S(1)}, u32[]{:S(2)}, u32[]{:S(2)}) collective-permute-start(f32[128,128]{1,0:T(8,128)S(1)} %fusion.3), channel_id=1, source_target_pairs={{0,8},{4,12},{8,0},{12,4},{16,24},{20,28},{24,16},{28,20},{1,9},{5... | collective-permute-start | bytes 196616 | tf_op jit(solution)/shard_map/ppermute | solution.py:154
  11.1 1.4 %collective-permute-done.1 = f32[128,128]{1,0:T(8,128)S(1)} collective-permute-done((f32[128,128]{1,0:T(8,128)S(1)}, f32[128,128]{1,0:T(8,128)S(1)}, u32[]{:S(2)}, u32[]{:S(2)}) %collective-permute-start.1) | collective-permute-done | bytes 65568 | tf_op jit(solution)/shard_map/ppermute | solution.py:154
  12.5 2.0 %collective-permute-done.3 = f32[128,128]{1,0:T(8,128)S(1)} collective-permute-done((f32[128,128]{1,0:T(8,128)S(1)}, f32[128,128]{1,0:T(8,128)S(1)}, u32[]{:S(2)}, u32[]{:S(2)}) %collective-permute-start.3) | collective-permute-done | bytes 65568 | tf_op jit(solution)/shard_map/ppermute | solution.py:154
  14.5 0.0 copy-start.2
  14.5 0.0 copy-start.3
  14.5 0.0 copy-start
  14.5 0.0 copy-start.1
  14.5 0.0 copy-start.4
  14.5 1.3 %collective-permute-start.4 = (f32[256,128]{1,0:T(8,128)S(1)}, f32[256,128]{1,0:T(8,128)S(1)}, u32[]{:S(2)}, u32[]{:S(2)}) collective-permute-start(f32[256,128]{1,0:T(8,128)S(1)} %pad_maximum_fusion), channel_id=1, source_target_pairs={{0,4},{4,0},{8,12},{12,8},{16,20},{20,16},{24,28},{28,24},{1,5},{5... | collective-permute-start | bytes 393224 | tf_op jit(solution)/shard_map/ppermute | solution.py:154
  15.8 2.8 %collective-permute-start.5 = (f32[128,128]{1,0:T(8,128)S(1)}, f32[128,128]{1,0:T(8,128)S(1)}, u32[]{:S(2)}, u32[]{:S(2)}) collective-permute-start(f32[128,128]{1,0:T(8,128)S(1)} %get-tuple-element.37), channel_id=1, source_target_pairs={{0,20},{4,16},{8,28},{12,24},{16,4},{20,0},{24,12},{28,8},{1,21},{... | collective-permute-start | bytes 196616 | tf_op jit(solution)/shard_map/ppermute | solution.py:154
  18.6 0.3 %collective-permute-start.6 = (f32[128,128]{1,0:T(8,128)S(1)}, f32[128,128]{1,0:T(8,128)S(1)}, u32[]{:S(2)}, u32[]{:S(2)}) collective-permute-start(f32[128,128]{1,0:T(8,128)S(1)} %get-tuple-element.37), channel_id=1, source_target_pairs={{0,16},{4,20},{8,24},{12,28},{16,0},{20,4},{24,8},{28,12},{1,17},{... | collective-permute-start | bytes 196616 | tf_op jit(solution)/shard_map/ppermute | solution.py:154
  19.0 0.0 copy-done.2
  19.0 0.0 copy-done.3
  19.0 0.0 copy-done
  19.0 0.0 copy-done.1
  19.0 0.0 copy-done.4
  19.0 1.4 %shard_map.84 = (f32[128,512]{1,0:T(8,128)S(1)}, f32[128,512]{1,0:T(8,128)S(1)}, f32[128,512]{1,0:T(8,128)S(1)}, f32[128,512]{1,0:T(8,128)S(1)}, f32[1,512]{1,0:T(1,128)S(1)}) custom-call(bf16[128,512]{1,0:T(8,128)(2,1)S(1)} %copy-done, bf16[128,512]{1,0:T(8,128)(2,1)S(1)} %copy-done.1, bf16[128,512]{1,0:T(8,128)(2,1)S(1)} %copy-done.2, ...), custom_call_target="tpu_custom_call" | custom-call | flops 201326592 | bytes 1576960 | tf_op jit(solution)/shard_map/pallas_call | solution.py:141
  20.4 2.1 %collective-permute-done.5 = f32[128,128]{1,0:T(8,128)S(1)} collective-permute-done((f32[128,128]{1,0:T(8,128)S(1)}, f32[128,128]{1,0:T(8,128)S(1)}, u32[]{:S(2)}, u32[]{:S(2)}) %collective-permute-start.5) | collective-permute-done | bytes 65568 | tf_op jit(solution)/shard_map/ppermute | solution.py:154
  22.6 1.9 %collective-permute-done.6 = f32[128,128]{1,0:T(8,128)S(1)} collective-permute-done((f32[128,128]{1,0:T(8,128)S(1)}, f32[128,128]{1,0:T(8,128)S(1)}, u32[]{:S(2)}, u32[]{:S(2)}) %collective-permute-start.6) | collective-permute-done | bytes 65568 | tf_op jit(solution)/shard_map/ppermute | solution.py:154
  24.5 0.0 collective-permute-done.4
  24.6 0.3 shard_map.86
  24.9 0.1 collective-permute-start.7
  25.0 1.6 %collective-permute-start.8 = (f32[1,128]{1,0:T(1,128)S(1)}, f32[1,128]{1,0:T(1,128)S(1)}, u32[]{:S(2)}, u32[]{:S(2)}) collective-permute-start(f32[1,128]{1,0:T(1,128)S(1)} %get-tuple-element.20), channel_id=1, source_target_pairs={{0,2},{1,3},{2,0},{3,1},{4,6},{5,7},{6,4},{7,5},{8,10},{9,11},{10,... | collective-permute-start | bytes 1544 | tf_op jit(solution)/shard_map/ppermute | solution.py:154
  26.6 0.3 collective-permute-start.9
  26.8 1.0 %shard_map.88 = (bf16[128,512]{1,0:T(8,128)(2,1)}, bf16[128,512]{1,0:T(8,128)(2,1)}, bf16[128,512]{1,0:T(8,128)(2,1)}) custom-call(bf16[128,512]{1,0:T(8,128)(2,1)S(1)} %copy-done.1, bf16[128,512]{1,0:T(8,128)(2,1)S(1)} %copy-done.2, bf16[128,512]{1,0:T(8,128)(2,1)S(1)} %copy-done.3, f32[128,512]{1,0:T(8,128)S(1)} %get-tuple-element.22.dq_part, ...), custom_call_target="tpu_custom_call" | custom-call | flops 50331648 | bytes 1835008 | tf_op jit(solution)/shard_map/pallas_call | solution.py:141
  27.9 0.0 collective-permute-done.7
  27.9 0.7 %collective-permute-done.8 = f32[1,128]{1,0:T(1,128)S(1)} collective-permute-done((f32[1,128]{1,0:T(1,128)S(1)}, f32[1,128]{1,0:T(1,128)S(1)}, u32[]{:S(2)}, u32[]{:S(2)}) %collective-permute-start.8) | collective-permute-done | bytes 544 | tf_op jit(solution)/shard_map/ppermute | solution.py:154
  28.6 0.9 %collective-permute-done.9 = f32[1,128]{1,0:T(1,128)S(1)} collective-permute-done((f32[1,128]{1,0:T(1,128)S(1)}, f32[1,128]{1,0:T(1,128)S(1)}, u32[]{:S(2)}, u32[]{:S(2)}) %collective-permute-start.9) | collective-permute-done | bytes 544 | tf_op jit(solution)/shard_map/ppermute | solution.py:154
  29.6 0.8 %shard_map.87 = bf16[128,512]{1,0:T(8,128)(2,1)} custom-call(f32[128,512]{1,0:T(8,128)S(1)} %get-tuple-element.19.out_ref, f32[4,128]{1,0:T(4,128)S(1)} %pad_maximum_fusion.3.squares_ref, f32[1,512]{1,0:T(1,128)S(1)} %get-tuple-element.21.gain_ref), custom_call_target="tpu_custom_call" | custom-call | flops 131072 | bytes 397312 | tf_op jit(solution)/shard_map/pallas_call | solution.py:141
  (12 shorter events, 0.2 us)
Async XLA Ops:
  2.1 5.3 %collective-permute-start = (f32[128,128]{1,0:T(8,128)S(1)}, f32[128,128]{1,0:T(8,128)S(1)}, u32[]{:S(2)}, u32[]{:S(2)}) collective-permute-start(f32[128,128]{1,0:T(8,128)S(1)} %slice_select_fusion.4), channel_id=1, source_target_pairs={{0,4},{4,0},{8,12},{12,8},{16,20},{20,16},{24,28},{28,24},{1,5},{5... | collective-permute-start | bytes 196616 | tf_op jit(solution)/shard_map/ppermute | solution.py:154
  5.1 5.0 %collective-permute-start.2 = (f32[128,128]{1,0:T(8,128)S(1)}, f32[128,128]{1,0:T(8,128)S(1)}, u32[]{:S(2)}, u32[]{:S(2)}) collective-permute-start(f32[128,128]{1,0:T(8,128)S(1)} %slice_select_fusion.2), channel_id=1, source_target_pairs={{0,4},{4,0},{8,12},{12,8},{16,20},{20,16},{24,28},{28,24},{1,5},{5... | collective-permute-start | bytes 196616 | tf_op jit(solution)/shard_map/ppermute | solution.py:154
  7.4 5.1 %collective-permute-start.1 = (f32[128,128]{1,0:T(8,128)S(1)}, f32[128,128]{1,0:T(8,128)S(1)}, u32[]{:S(2)}, u32[]{:S(2)}) collective-permute-start(f32[128,128]{1,0:T(8,128)S(1)} %fusion.2), channel_id=1, source_target_pairs={{0,8},{4,12},{8,0},{12,4},{16,24},{20,28},{24,16},{28,20},{1,9},{5... | collective-permute-start | bytes 196616 | tf_op jit(solution)/shard_map/ppermute | solution.py:154
  10.1 4.3 %collective-permute-start.3 = (f32[128,128]{1,0:T(8,128)S(1)}, f32[128,128]{1,0:T(8,128)S(1)}, u32[]{:S(2)}, u32[]{:S(2)}) collective-permute-start(f32[128,128]{1,0:T(8,128)S(1)} %fusion.3), channel_id=1, source_target_pairs={{0,8},{4,12},{8,0},{12,4},{16,24},{20,28},{24,16},{28,20},{1,9},{5... | collective-permute-start | bytes 196616 | tf_op jit(solution)/shard_map/ppermute | solution.py:154
  14.5 4.5 %copy-start.2 = (bf16[128,512]{1,0:T(8,128)(2,1)S(1)}, bf16[128,512]{1,0:T(8,128)(2,1)}, u32[]{:S(2)}) copy-start(bf16[128,512]{1,0:T(8,128)(2,1)} %v_ref.3) | copy-start | bytes 393220
  14.5 4.5 %copy-start.3 = (bf16[128,512]{1,0:T(8,128)(2,1)S(1)}, bf16[128,512]{1,0:T(8,128)(2,1)}, u32[]{:S(2)}) copy-start(bf16[128,512]{1,0:T(8,128)(2,1)} %g_ref.3) | copy-start | bytes 393220
  14.5 4.5 %copy-start = (bf16[128,512]{1,0:T(8,128)(2,1)S(1)}, bf16[128,512]{1,0:T(8,128)(2,1)}, u32[]{:S(2)}) copy-start(bf16[128,512]{1,0:T(8,128)(2,1)} %q_ref.3) | copy-start | bytes 393220
  14.5 4.5 %copy-start.1 = (bf16[128,512]{1,0:T(8,128)(2,1)S(1)}, bf16[128,512]{1,0:T(8,128)(2,1)}, u32[]{:S(2)}) copy-start(bf16[128,512]{1,0:T(8,128)(2,1)} %k_ref.3) | copy-start | bytes 393220
  14.5 4.5 %copy-start.4 = (f32[512]{0:T(512)S(1)}, f32[512]{0:T(512)}, u32[]{:S(2)}) copy-start(f32[512]{0:T(512)} %param.9) | copy-start | bytes 6148
  14.5 10.0 %collective-permute-start.4 = (f32[256,128]{1,0:T(8,128)S(1)}, f32[256,128]{1,0:T(8,128)S(1)}, u32[]{:S(2)}, u32[]{:S(2)}) collective-permute-start(f32[256,128]{1,0:T(8,128)S(1)} %pad_maximum_fusion), channel_id=1, source_target_pairs={{0,4},{4,0},{8,12},{12,8},{16,20},{20,16},{24,28},{28,24},{1,5},{5... | collective-permute-start | bytes 393224 | tf_op jit(solution)/shard_map/ppermute | solution.py:154
  15.8 6.8 %collective-permute-start.5 = (f32[128,128]{1,0:T(8,128)S(1)}, f32[128,128]{1,0:T(8,128)S(1)}, u32[]{:S(2)}, u32[]{:S(2)}) collective-permute-start(f32[128,128]{1,0:T(8,128)S(1)} %get-tuple-element.37), channel_id=1, source_target_pairs={{0,20},{4,16},{8,28},{12,24},{16,4},{20,0},{24,12},{28,8},{1,21},{... | collective-permute-start | bytes 196616 | tf_op jit(solution)/shard_map/ppermute | solution.py:154
  18.6 5.9 %collective-permute-start.6 = (f32[128,128]{1,0:T(8,128)S(1)}, f32[128,128]{1,0:T(8,128)S(1)}, u32[]{:S(2)}, u32[]{:S(2)}) collective-permute-start(f32[128,128]{1,0:T(8,128)S(1)} %get-tuple-element.37), channel_id=1, source_target_pairs={{0,16},{4,20},{8,24},{12,28},{16,0},{20,4},{24,8},{28,12},{1,17},{... | collective-permute-start | bytes 196616 | tf_op jit(solution)/shard_map/ppermute | solution.py:154
  24.9 3.0 %collective-permute-start.7 = (f32[1,128]{1,0:T(1,128)S(1)}, f32[1,128]{1,0:T(1,128)S(1)}, u32[]{:S(2)}, u32[]{:S(2)}) collective-permute-start(f32[1,128]{1,0:T(1,128)S(1)} %get-tuple-element.20), channel_id=1, source_target_pairs={{0,1},{1,0},{2,3},{3,2},{4,5},{5,4},{6,7},{7,6},{8,9},{9,8},{10,11... | collective-permute-start | bytes 1544 | tf_op jit(solution)/shard_map/ppermute | solution.py:154
  25.0 3.6 %collective-permute-start.8 = (f32[1,128]{1,0:T(1,128)S(1)}, f32[1,128]{1,0:T(1,128)S(1)}, u32[]{:S(2)}, u32[]{:S(2)}) collective-permute-start(f32[1,128]{1,0:T(1,128)S(1)} %get-tuple-element.20), channel_id=1, source_target_pairs={{0,2},{1,3},{2,0},{3,1},{4,6},{5,7},{6,4},{7,5},{8,10},{9,11},{10,... | collective-permute-start | bytes 1544 | tf_op jit(solution)/shard_map/ppermute | solution.py:154
  26.6 3.0 %collective-permute-start.9 = (f32[1,128]{1,0:T(1,128)S(1)}, f32[1,128]{1,0:T(1,128)S(1)}, u32[]{:S(2)}, u32[]{:S(2)}) collective-permute-start(f32[1,128]{1,0:T(1,128)S(1)} %get-tuple-element.20), channel_id=1, source_target_pairs={{0,3},{1,2},{2,1},{3,0},{4,7},{5,6},{6,5},{7,4},{8,11},{9,10},{10,... | collective-permute-start | bytes 1544 | tf_op jit(solution)/shard_map/ppermute | solution.py:154

commit v4 on v3

--- a/solution.py
+++ b/solution.py
@@ -196,29 +196,36 @@
     def send(x, distance):
         return swap(x, axis, distance)
 
-    (a_mine, a_other), (b_mine, b_other) = halves(a, odd), halves(b, odd)
+    a_mine, a_other = halves(a, odd)
+    a3 = send(a_other, 3)
+    a2 = send(a_mine, 2)
     a1 = send(a_other, 1)
-    b1 = send(b_other, 1)
-    a_total, b_total = a_mine + a1, b_mine + b1
-    a_sum = b_sum = jnp.zeros_like(a_mine)
-    distance = 2
+    b1 = send(b, 1)
+    a_pair = a2 + a3
+    a_sum = jnp.where(a_enters(2), a_pair, 0.0)
+    a_total = a_mine + a1 + a_pair
+    b_total = b + b1
+    distance = 4
     while distance < top:
         a_got = send(a_total, distance)
-        b_got = send(b_total, distance)
         a_sum = a_sum + jnp.where(a_enters(distance), a_got, 0.0)
-        b_sum = b_sum + jnp.where(b_enters(distance), b_got, 0.0)
-        a_total, b_total = a_total + a_got, b_total + b_got
+        a_total = a_total + a_got
         distance *= 2
     t_other = send(a_total, top | 1)
     t_mine = send(a_total, top)
-    a_out = a_sum + jnp.where(a_enters(1), 0.0, a_mine)
-    b_out = b_sum + jnp.where(b_enters(1), 0.0, b_mine)
-    got = send(jnp.concatenate([a_out, b_out], axis=0), 1)
-    mid = a_mine.shape[0]
-    a_own = a_sum + jnp.where(a_enters(1), a1, 0.0)
-    b_own = b_sum + jnp.where(b_enters(1), b1, 0.0) + t_mine
-    a_all = join(a_own, got[:mid], odd)
-    b_all = join(b_own, got[mid:] + t_other, odd)
+    distance, b_parts = 2, []
+    while distance < top:
+        b_parts.append(send(b_total, distance))
+        b_total = b_total + b_parts[-1]
+        distance *= 2
+    got = send(a_sum + jnp.where(a_enters(1), 0.0, a_mine), 1)
+    a_sum, a1, got, b1, b_parts, t_mine, t_other = lax.optimization_barrier(
+        (a_sum, a1, got, b1, b_parts, t_mine, t_other)
+    )
+    a_all = join(a_sum + jnp.where(a_enters(1), a1, 0.0), got, odd)
+    b_all = join(t_mine, t_other, odd) + jnp.where(b_enters(1), b1, 0.0)
+    for i, part in enumerate(b_parts):
+        b_all = b_all + jnp.where(b_enters(2 << i), part, 0.0)
     return jnp.where(upper, b_all, a_all), jnp.where(upper, a_all, b_all)
 
 
@@ -232,7 +239,10 @@
             row = row + swap(row, axis, distance)
             distance *= 2
         return row
-    return jnp.concatenate([row] + [swap(row, axis, d) for d in range(1, count)], axis=0)
+    rows = [row]
+    for distance in range(count - 1, 0, -1):
+        rows.append(swap(row, axis, distance))
+    return jnp.concatenate(rows, axis=0)
 
 
 def body(queries, keys, values, d_out, gain):

time: 30.5 us -> 30.3 us (level)
  waiting for transfers between devices: 11.2 us -> 7.81 us
  starting transfers between devices: 13.2 us -> 15.8 us
  local copies, waits for them, and re-layouts: 0.03 us -> 0.68 us
    ppermute x10 -> x11, waiting for transfers between devices: 11.2 us -> 7.81 us  [swap(): return lax.ppermute(x, axis, [(i, i ^ distance) for i in range(size)])]
    ppermute x10 -> x11, starting transfers between devices: 13.2 us -> 15.8 us  [swap(): return lax.ppermute(x, axis, [(i, i ^ distance) for i in range(size)])]
    unnamed x10, local copies, waits for them, and re-layouts: 0.03 us -> 0.68 us
  transfers between devices with their start and end apart: 10 -> 11, of which waited for: 7 -> 5; matrix products, arithmetic and copies ran while one was open for 0% -> 0% of each run, Pallas kernels for 8% -> 8%
where the time goes in v4:
time: 30.3 us; the launch traced here: 30.1 us
  starting transfers between devices  15.8 us (52%)
  waiting for transfers between devices  7.81 us (26%)
  Pallas kernels  4.89 us (16%)
  between operations  0.76 us (3%)
  local copies, waits for them, and re-layouts  0.68 us (2%)
    ppermute x11, starting transfers between devices, swap(): return lax.ppermute(x, axis, [(i, i ^ distance) for i in range(size)])  15.8 us
    ppermute x11, waiting for transfers between devices, swap(): return lax.ppermute(x, axis, [(i, i ^ distance) for i in range(size)])  7.81 us
    pallas_call x5, Pallas kernels, call(): pl.pallas_call(kernel, out_shape=outs[0] if single else tuple(outs), in_s...  4.89 us
    unnamed x10, local copies, waits for them, and re-layouts  0.68 us
  transfers between devices with their start and end apart: 11, of which 5 were waited for; matrix products, arithmetic and copies ran while one was open for 0% of the time, Pallas kernels for 8%

profile of v4, /device:TPU:0, one launch (start us, length us, event | category | flops | bytes accessed | tf_op | source)
XLA Modules:
  0.0 30.1 jit_solution(12542860789610688115)
XLA Ops:
  0.6 1.4 %shard_map.85 = (f32[256,128]{1,0:T(8,128)S(1)}, f32[256,128]{1,0:T(8,128)S(1)}) custom-call(bf16[128,512]{1,0:T(8,128)(2,1)} %q_ref.3, bf16[128,512]{1,0:T(8,128)(2,1)} %k_ref.3, bf16[128,512]{1,0:T(8,128)(2,1)} %v_ref.3, bf16[128,512]{1,0:T(8,128)(2,1)} %g_ref.3), custom_call_target="tpu_custom_call" | custom-call | flops 33554432 | bytes 786432 | tf_op jit(solution)/shard_map/pallas_call | solution.py:141
  2.1 3.0 %collective-permute-start.4 = (f32[256,128]{1,0:T(8,128)S(1)}, f32[256,128]{1,0:T(8,128)S(1)}, u32[]{:S(2)}, u32[]{:S(2)}) collective-permute-start(f32[256,128]{1,0:T(8,128)S(1)} %get-tuple-element.46), channel_id=1, source_target_pairs={{0,4},{4,0},{8,12},{12,8},{16,20},{20,16},{24,28},{28,24},{1,5},{5... | collective-permute-start | bytes 393224 | tf_op jit(solution)/shard_map/ppermute | solution.py:154
  5.1 0.1 collective-permute-start.2
  5.2 2.1 %collective-permute-start = (f32[128,128]{1,0:T(8,128)S(1)}, f32[128,128]{1,0:T(8,128)S(1)}, u32[]{:S(2)}, u32[]{:S(2)}) collective-permute-start(f32[128,128]{1,0:T(8,128)S(1)} %get-tuple-element.54), channel_id=1, source_target_pairs={{0,8},{4,12},{8,0},{12,4},{16,24},{20,28},{24,16},{28,20},{1,9},{5... | collective-permute-start | bytes 196616 | tf_op jit(solution)/shard_map/ppermute | solution.py:154
  7.3 1.4 %collective-permute-start.1 = (f32[128,128]{1,0:T(8,128)S(1)}, f32[128,128]{1,0:T(8,128)S(1)}, u32[]{:S(2)}, u32[]{:S(2)}) collective-permute-start(f32[128,128]{1,0:T(8,128)S(1)} %get-tuple-element.53), channel_id=1, source_target_pairs={{0,12},{4,8},{8,4},{12,0},{16,28},{20,24},{24,20},{28,16},{1,13},{... | collective-permute-start | bytes 196616 | tf_op jit(solution)/shard_map/ppermute | solution.py:154
  8.7 0.6 %collective-permute-done.4 = f32[256,128]{1,0:T(8,128)S(1)} collective-permute-done((f32[256,128]{1,0:T(8,128)S(1)}, f32[256,128]{1,0:T(8,128)S(1)}, u32[]{:S(2)}, u32[]{:S(2)}) %collective-permute-start.4) | collective-permute-done | bytes 131104 | tf_op jit(solution)/shard_map/ppermute | solution.py:154
  9.3 0.0 copy-start.3
  9.3 0.0 copy-start
  9.3 0.0 copy-start.1
  9.3 0.0 copy-start.2
  9.4 2.6 %collective-permute-start.5 = (f32[256,128]{1,0:T(8,128)S(1)}, f32[256,128]{1,0:T(8,128)S(1)}, u32[]{:S(2)}, u32[]{:S(2)}) collective-permute-start(f32[256,128]{1,0:T(8,128)S(1)} %add.26), channel_id=1, source_target_pairs={{0,8},{4,12},{8,0},{12,4},{16,24},{20,28},{24,16},{28,20},{1,9},{5... | collective-permute-start | bytes 393224 | tf_op jit(solution)/shard_map/ppermute | solution.py:154
  12.0 0.0 collective-permute-done.2
  12.0 0.0 collective-permute-done
  12.0 1.2 %collective-permute-done.1 = f32[128,128]{1,0:T(8,128)S(1)} collective-permute-done((f32[128,128]{1,0:T(8,128)S(1)}, f32[128,128]{1,0:T(8,128)S(1)}, u32[]{:S(2)}, u32[]{:S(2)}) %collective-permute-start.1) | collective-permute-done | bytes 65568 | tf_op jit(solution)/shard_map/ppermute | solution.py:154
  13.2 1.1 %collective-permute-start.3 = (f32[128,128]{1,0:T(8,128)S(1)}, f32[128,128]{1,0:T(8,128)S(1)}, u32[]{:S(2)}, u32[]{:S(2)}) collective-permute-start(f32[128,128]{1,0:T(8,128)S(1)} %get-tuple-element.44), channel_id=1, source_target_pairs={{0,4},{4,0},{8,12},{12,8},{16,20},{20,16},{24,28},{28,24},{1,5},{5... | collective-permute-start | bytes 196616 | tf_op jit(solution)/shard_map/ppermute | solution.py:154
  14.2 2.7 %collective-permute-start.6 = (f32[128,128]{1,0:T(8,128)S(1)}, f32[128,128]{1,0:T(8,128)S(1)}, u32[]{:S(2)}, u32[]{:S(2)}) collective-permute-start(f32[128,128]{1,0:T(8,128)S(1)} %get-tuple-element.50), channel_id=1, source_target_pairs={{0,16},{4,20},{8,24},{12,28},{16,0},{20,4},{24,8},{28,12},{1,17},{... | collective-permute-start | bytes 196616 | tf_op jit(solution)/shard_map/ppermute | solution.py:154
  16.9 0.7 %collective-permute-start.7 = (f32[128,128]{1,0:T(8,128)S(1)}, f32[128,128]{1,0:T(8,128)S(1)}, u32[]{:S(2)}, u32[]{:S(2)}) collective-permute-start(f32[128,128]{1,0:T(8,128)S(1)} %get-tuple-element.50), channel_id=1, source_target_pairs={{0,20},{4,16},{8,28},{12,24},{16,4},{20,0},{24,12},{28,8},{1,21},{... | collective-permute-start | bytes 196616 | tf_op jit(solution)/shard_map/ppermute | solution.py:154
  17.6 0.0 copy-start.4
  17.6 0.0 copy-done.3
  17.6 0.0 copy-done
  17.6 0.0 copy-done.1
  17.6 0.0 copy-done.2
  17.7 0.7 %copy-done.4 = f32[512]{0:T(512)S(1)} copy-done((f32[512]{0:T(512)S(1)}, f32[512]{0:T(512)}, u32[]{:S(2)}) %copy-start.4) | copy-done | bytes 2072
  18.3 1.4 %shard_map.84 = (f32[128,512]{1,0:T(8,128)S(1)}, f32[128,512]{1,0:T(8,128)S(1)}, f32[128,512]{1,0:T(8,128)S(1)}, f32[128,512]{1,0:T(8,128)S(1)}, f32[1,512]{1,0:T(1,128)S(1)}) custom-call(bf16[128,512]{1,0:T(8,128)(2,1)S(1)} %copy-done, bf16[128,512]{1,0:T(8,128)(2,1)S(1)} %copy-done.1, bf16[128,512]{1,0:T(8,128)(2,1)S(1)} %copy-done.2, ...), custom_call_target="tpu_custom_call" | custom-call | flops 201326592 | bytes 1576960 | tf_op jit(solution)/shard_map/pallas_call | solution.py:141
  19.7 0.0 collective-permute-done.3
  19.7 0.7 %collective-permute-done.6 = f32[128,128]{1,0:T(8,128)S(1)} collective-permute-done((f32[128,128]{1,0:T(8,128)S(1)}, f32[128,128]{1,0:T(8,128)S(1)}, u32[]{:S(2)}, u32[]{:S(2)}) %collective-permute-start.6) | collective-permute-done | bytes 65568 | tf_op jit(solution)/shard_map/ppermute | solution.py:154
  20.5 3.2 %collective-permute-done.7 = f32[128,128]{1,0:T(8,128)S(1)} collective-permute-done((f32[128,128]{1,0:T(8,128)S(1)}, f32[128,128]{1,0:T(8,128)S(1)}, u32[]{:S(2)}, u32[]{:S(2)}) %collective-permute-start.7) | collective-permute-done | bytes 65568 | tf_op jit(solution)/shard_map/ppermute | solution.py:154
  23.7 0.0 collective-permute-done.5
  23.8 0.3 shard_map.86
  24.1 0.1 collective-permute-start.10
  24.1 1.6 %collective-permute-start.8 = (f32[1,128]{1,0:T(1,128)S(1)}, f32[1,128]{1,0:T(1,128)S(1)}, u32[]{:S(2)}, u32[]{:S(2)}) collective-permute-start(f32[1,128]{1,0:T(1,128)S(1)} %get-tuple-element.34), channel_id=1, source_target_pairs={{0,3},{1,2},{2,1},{3,0},{4,7},{5,6},{6,5},{7,4},{8,11},{9,10},{10,... | collective-permute-start | bytes 1544 | tf_op jit(solution)/shard_map/ppermute | solution.py:154
  25.8 0.5 %collective-permute-start.9 = (f32[1,128]{1,0:T(1,128)S(1)}, f32[1,128]{1,0:T(1,128)S(1)}, u32[]{:S(2)}, u32[]{:S(2)}) collective-permute-start(f32[1,128]{1,0:T(1,128)S(1)} %get-tuple-element.34), channel_id=1, source_target_pairs={{0,2},{1,3},{2,0},{3,1},{4,6},{5,7},{6,4},{7,5},{8,10},{9,11},{10,... | collective-permute-start | bytes 1544 | tf_op jit(solution)/shard_map/ppermute | solution.py:154
  26.3 1.0 %shard_map.88 = (bf16[128,512]{1,0:T(8,128)(2,1)}, bf16[128,512]{1,0:T(8,128)(2,1)}, bf16[128,512]{1,0:T(8,128)(2,1)}) custom-call(bf16[128,512]{1,0:T(8,128)(2,1)S(1)} %copy-done.1, bf16[128,512]{1,0:T(8,128)(2,1)S(1)} %copy-done.2, bf16[128,512]{1,0:T(8,128)(2,1)S(1)} %copy-done.3, f32[128,512]{1,0:T(8,128)S(1)} %get-tuple-element.36.dq_part, ...), custom_call_target="tpu_custom_call" | custom-call | flops 50331648 | bytes 1835008 | tf_op jit(solution)/shard_map/pallas_call | solution.py:141
  27.3 0.0 collective-permute-done.10
  27.3 0.0 collective-permute-done.8
  27.3 2.0 %collective-permute-done.9 = f32[1,128]{1,0:T(1,128)S(1)} collective-permute-done((f32[1,128]{1,0:T(1,128)S(1)}, f32[1,128]{1,0:T(1,128)S(1)}, u32[]{:S(2)}, u32[]{:S(2)}) %collective-permute-start.9) | collective-permute-done | bytes 544 | tf_op jit(solution)/shard_map/ppermute | solution.py:154
  29.4 0.8 %shard_map.87 = bf16[128,512]{1,0:T(8,128)(2,1)} custom-call(f32[128,512]{1,0:T(8,128)S(1)} %get-tuple-element.33.out_ref, f32[4,128]{1,0:T(4,128)S(1)} %pad_maximum_fusion.1.squares_ref, f32[1,512]{1,0:T(1,128)S(1)} %get-tuple-element.35.gain_ref), custom_call_target="tpu_custom_call" | custom-call | flops 131072 | bytes 397312 | tf_op jit(solution)/shard_map/pallas_call | solution.py:141
  (8 shorter events, 0.2 us)
Async XLA Ops:
  2.1 7.2 %collective-permute-start.4 = (f32[256,128]{1,0:T(8,128)S(1)}, f32[256,128]{1,0:T(8,128)S(1)}, u32[]{:S(2)}, u32[]{:S(2)}) collective-permute-start(f32[256,128]{1,0:T(8,128)S(1)} %get-tuple-element.46), channel_id=1, source_target_pairs={{0,4},{4,0},{8,12},{12,8},{16,20},{20,16},{24,28},{28,24},{1,5},{5... | collective-permute-start | bytes 393224 | tf_op jit(solution)/shard_map/ppermute | solution.py:154
  5.1 6.8 %collective-permute-start.2 = (f32[128,128]{1,0:T(8,128)S(1)}, f32[128,128]{1,0:T(8,128)S(1)}, u32[]{:S(2)}, u32[]{:S(2)}) collective-permute-start(f32[128,128]{1,0:T(8,128)S(1)} %get-tuple-element.53), channel_id=1, source_target_pairs={{0,4},{4,0},{8,12},{12,8},{16,20},{20,16},{24,28},{28,24},{1,5},{5... | collective-permute-start | bytes 196616 | tf_op jit(solution)/shard_map/ppermute | solution.py:154
  5.2 6.8 %collective-permute-start = (f32[128,128]{1,0:T(8,128)S(1)}, f32[128,128]{1,0:T(8,128)S(1)}, u32[]{:S(2)}, u32[]{:S(2)}) collective-permute-start(f32[128,128]{1,0:T(8,128)S(1)} %get-tuple-element.54), channel_id=1, source_target_pairs={{0,8},{4,12},{8,0},{12,4},{16,24},{20,28},{24,16},{28,20},{1,9},{5... | collective-permute-start | bytes 196616 | tf_op jit(solution)/shard_map/ppermute | solution.py:154
  7.3 5.9 %collective-permute-start.1 = (f32[128,128]{1,0:T(8,128)S(1)}, f32[128,128]{1,0:T(8,128)S(1)}, u32[]{:S(2)}, u32[]{:S(2)}) collective-permute-start(f32[128,128]{1,0:T(8,128)S(1)} %get-tuple-element.53), channel_id=1, source_target_pairs={{0,12},{4,8},{8,4},{12,0},{16,28},{20,24},{24,20},{28,16},{1,13},{... | collective-permute-start | bytes 196616 | tf_op jit(solution)/shard_map/ppermute | solution.py:154
  9.3 8.3 %copy-start.3 = (bf16[128,512]{1,0:T(8,128)(2,1)S(1)}, bf16[128,512]{1,0:T(8,128)(2,1)}, u32[]{:S(2)}) copy-start(bf16[128,512]{1,0:T(8,128)(2,1)} %g_ref.3) | copy-start | bytes 393220
  9.3 8.3 %copy-start = (bf16[128,512]{1,0:T(8,128)(2,1)S(1)}, bf16[128,512]{1,0:T(8,128)(2,1)}, u32[]{:S(2)}) copy-start(bf16[128,512]{1,0:T(8,128)(2,1)} %q_ref.3) | copy-start | bytes 393220
  9.3 8.3 %copy-start.1 = (bf16[128,512]{1,0:T(8,128)(2,1)S(1)}, bf16[128,512]{1,0:T(8,128)(2,1)}, u32[]{:S(2)}) copy-start(bf16[128,512]{1,0:T(8,128)(2,1)} %k_ref.3) | copy-start | bytes 393220
  9.3 8.3 %copy-start.2 = (bf16[128,512]{1,0:T(8,128)(2,1)S(1)}, bf16[128,512]{1,0:T(8,128)(2,1)}, u32[]{:S(2)}) copy-start(bf16[128,512]{1,0:T(8,128)(2,1)} %v_ref.3) | copy-start | bytes 393220
  9.4 14.3 %collective-permute-start.5 = (f32[256,128]{1,0:T(8,128)S(1)}, f32[256,128]{1,0:T(8,128)S(1)}, u32[]{:S(2)}, u32[]{:S(2)}) collective-permute-start(f32[256,128]{1,0:T(8,128)S(1)} %add.26), channel_id=1, source_target_pairs={{0,8},{4,12},{8,0},{12,4},{16,24},{20,28},{24,16},{28,20},{1,9},{5... | collective-permute-start | bytes 393224 | tf_op jit(solution)/shard_map/ppermute | solution.py:154
  13.2 6.6 %collective-permute-start.3 = (f32[128,128]{1,0:T(8,128)S(1)}, f32[128,128]{1,0:T(8,128)S(1)}, u32[]{:S(2)}, u32[]{:S(2)}) collective-permute-start(f32[128,128]{1,0:T(8,128)S(1)} %get-tuple-element.44), channel_id=1, source_target_pairs={{0,4},{4,0},{8,12},{12,8},{16,20},{20,16},{24,28},{28,24},{1,5},{5... | collective-permute-start | bytes 196616 | tf_op jit(solution)/shard_map/ppermute | solution.py:154
  14.2 6.2 %collective-permute-start.6 = (f32[128,128]{1,0:T(8,128)S(1)}, f32[128,128]{1,0:T(8,128)S(1)}, u32[]{:S(2)}, u32[]{:S(2)}) collective-permute-start(f32[128,128]{1,0:T(8,128)S(1)} %get-tuple-element.50), channel_id=1, source_target_pairs={{0,16},{4,20},{8,24},{12,28},{16,0},{20,4},{24,8},{28,12},{1,17},{... | collective-permute-start | bytes 196616 | tf_op jit(solution)/shard_map/ppermute | solution.py:154
  16.9 6.8 %collective-permute-start.7 = (f32[128,128]{1,0:T(8,128)S(1)}, f32[128,128]{1,0:T(8,128)S(1)}, u32[]{:S(2)}, u32[]{:S(2)}) collective-permute-start(f32[128,128]{1,0:T(8,128)S(1)} %get-tuple-element.50), channel_id=1, source_target_pairs={{0,20},{4,16},{8,28},{12,24},{16,4},{20,0},{24,12},{28,8},{1,21},{... | collective-permute-start | bytes 196616 | tf_op jit(solution)/shard_map/ppermute | solution.py:154
  17.6 0.7 %copy-start.4 = (f32[512]{0:T(512)S(1)}, f32[512]{0:T(512)}, u32[]{:S(2)}) copy-start(f32[512]{0:T(512)} %param.9) | copy-start | bytes 6148
  24.1 3.3 %collective-permute-start.10 = (f32[1,128]{1,0:T(1,128)S(1)}, f32[1,128]{1,0:T(1,128)S(1)}, u32[]{:S(2)}, u32[]{:S(2)}) collective-permute-start(f32[1,128]{1,0:T(1,128)S(1)} %get-tuple-element.34), channel_id=1, source_target_pairs={{0,1},{1,0},{2,3},{3,2},{4,5},{5,4},{6,7},{7,6},{8,9},{9,8},{10,11... | collective-permute-start | bytes 1544 | tf_op jit(solution)/shard_map/ppermute | solution.py:154
  24.1 3.2 %collective-permute-start.8 = (f32[1,128]{1,0:T(1,128)S(1)}, f32[1,128]{1,0:T(1,128)S(1)}, u32[]{:S(2)}, u32[]{:S(2)}) collective-permute-start(f32[1,128]{1,0:T(1,128)S(1)} %get-tuple-element.34), channel_id=1, source_target_pairs={{0,3},{1,2},{2,1},{3,0},{4,7},{5,6},{6,5},{7,4},{8,11},{9,10},{10,... | collective-permute-start | bytes 1544 | tf_op jit(solution)/shard_map/ppermute | solution.py:154
  25.8 3.6 %collective-permute-start.9 = (f32[1,128]{1,0:T(1,128)S(1)}, f32[1,128]{1,0:T(1,128)S(1)}, u32[]{:S(2)}, u32[]{:S(2)}) collective-permute-start(f32[1,128]{1,0:T(1,128)S(1)} %get-tuple-element.34), channel_id=1, source_target_pairs={{0,2},{1,3},{2,0},{3,1},{4,6},{5,7},{6,4},{7,5},{8,10},{9,11},{10,... | collective-permute-start | bytes 1544 | tf_op jit(solution)/shard_map/ppermute | solution.py:154

commit v5 on v4

--- a/solution.py
+++ b/solution.py
@@ -196,36 +196,42 @@
     def send(x, distance):
         return swap(x, axis, distance)
 
-    a_mine, a_other = halves(a, odd)
+    (a_mine, a_other), (b_mine, b_other) = halves(a, odd), halves(b, odd)
+    mid = a_mine.shape[0]
     a3 = send(a_other, 3)
     a2 = send(a_mine, 2)
     a1 = send(a_other, 1)
-    b1 = send(b, 1)
+    b3 = send(b_other, 3)
+    b2 = send(b_mine, 2)
+    b1 = send(b_other, 1)
     a_pair = a2 + a3
     a_sum = jnp.where(a_enters(2), a_pair, 0.0)
     a_total = a_mine + a1 + a_pair
-    b_total = b + b1
-    distance = 4
+    distance, a_later = 4, []
     while distance < top:
-        a_got = send(a_total, distance)
-        a_sum = a_sum + jnp.where(a_enters(distance), a_got, 0.0)
-        a_total = a_total + a_got
+        a_later.append(send(a_total, distance))
+        a_sum = a_sum + jnp.where(a_enters(distance), a_later[-1], 0.0)
+        a_total = a_total + a_later[-1]
         distance *= 2
     t_other = send(a_total, top | 1)
     t_mine = send(a_total, top)
-    distance, b_parts = 2, []
+    b_pair = b2 + b3
+    b_sum = jnp.where(b_enters(2), b_pair, 0.0)
+    b_total = b_mine + b1 + b_pair
+    distance = 4
     while distance < top:
-        b_parts.append(send(b_total, distance))
-        b_total = b_total + b_parts[-1]
+        b_got = send(b_total, distance)
+        b_sum = b_sum + jnp.where(b_enters(distance), b_got, 0.0)
+        b_total = b_total + b_got
         distance *= 2
-    got = send(a_sum + jnp.where(a_enters(1), 0.0, a_mine), 1)
-    a_sum, a1, got, b1, b_parts, t_mine, t_other = lax.optimization_barrier(
-        (a_sum, a1, got, b1, b_parts, t_mine, t_other)
-    )
-    a_all = join(a_sum + jnp.where(a_enters(1), a1, 0.0), got, odd)
-    b_all = join(t_mine, t_other, odd) + jnp.where(b_enters(1), b1, 0.0)
-    for i, part in enumerate(b_parts):
-        b_all = b_all + jnp.where(b_enters(2 << i), part, 0.0)
+    a_out = a_sum + jnp.where(a_enters(1), 0.0, a_mine)
+    b_out = b_sum + jnp.where(b_enters(1), 0.0, b_mine)
+    got = send(jnp.concatenate([a_out, b_out], axis=0), 1)
+    a_sum, a1, b_sum, b1, got, t_mine, t_other = lax.optimization_barrier(
+        (a_sum, a1, b_sum, b1, got, t_mine, t_other)
+    )
+    a_all = join(a_sum + jnp.where(a_enters(1), a1, 0.0), got[:mid], odd)
+    b_all = join(b_sum + jnp.where(b_enters(1), b1, 0.0) + t_mine, got[mid:] + t_other, odd)
     return jnp.where(upper, b_all, a_all), jnp.where(upper, a_all, b_all)
 
 

time: 30.3 us -> 31.4 us (1.036)
  waiting for transfers between devices: 7.81 us -> 10.1 us
  local copies, waits for them, and re-layouts: 0.68 us -> 0.03 us
  starting transfers between devices: 15.8 us -> 15.2 us
    ppermute x11 -> x12, waiting for transfers between devices: 7.81 us -> 10.1 us  [swap(): return lax.ppermute(x, axis, [(i, i ^ distance) for i in range(size)])]
    unnamed x10, local copies, waits for them, and re-layouts: 0.68 us -> 0.03 us
    ppermute x11 -> x12, starting transfers between devices: 15.8 us -> 15.2 us  [swap(): return lax.ppermute(x, axis, [(i, i ^ distance) for i in range(size)])]
  transfers between devices with their start and end apart: 11 -> 12, of which waited for: 5 -> 7; matrix products, arithmetic and copies ran while one was open for 0% -> 0% of each run, Pallas kernels for 8% -> 8%
where the time goes in v5:
time: 31.4 us; the launch traced here: 31.3 us
  starting transfers between devices  15.2 us (48%)
  waiting for transfers between devices  10.1 us (32%)
  Pallas kernels  4.91 us (16%)
  between operations  0.77 us (2%)
    ppermute x12, starting transfers between devices, swap(): return lax.ppermute(x, axis, [(i, i ^ distance) for i in range(size)])  15.2 us
    ppermute x12, waiting for transfers between devices, swap(): return lax.ppermute(x, axis, [(i, i ^ distance) for i in range(size)])  10.1 us
    pallas_call x5, Pallas kernels, call(): pl.pallas_call(kernel, out_shape=outs[0] if single else tuple(outs), in_s...  4.91 us
  transfers between devices with their start and end apart: 12, of which 7 were waited for; matrix products, arithmetic and copies ran while one was open for 0% of the time, Pallas kernels for 8%

profile of v5, /device:TPU:0, one launch (start us, length us, event | category | flops | bytes accessed | tf_op | source)
XLA Modules:
  0.0 31.3 jit_solution(10111981497979281012)
XLA Ops:
  0.6 1.4 %shard_map.85 = (f32[256,128]{1,0:T(8,128)S(1)}, f32[256,128]{1,0:T(8,128)S(1)}) custom-call(bf16[128,512]{1,0:T(8,128)(2,1)} %q_ref.3, bf16[128,512]{1,0:T(8,128)(2,1)} %k_ref.3, bf16[128,512]{1,0:T(8,128)(2,1)} %v_ref.3, bf16[128,512]{1,0:T(8,128)(2,1)} %g_ref.3), custom_call_target="tpu_custom_call" | custom-call | flops 33554432 | bytes 786432 | tf_op jit(solution)/shard_map/pallas_call | solution.py:141
  2.1 3.1 %collective-permute-start.3 = (f32[128,128]{1,0:T(8,128)S(1)}, f32[128,128]{1,0:T(8,128)S(1)}, u32[]{:S(2)}, u32[]{:S(2)}) collective-permute-start(f32[128,128]{1,0:T(8,128)S(1)} %get-tuple-element.57), channel_id=1, source_target_pairs={{0,8},{4,12},{8,0},{12,4},{16,24},{20,28},{24,16},{28,20},{1,9},{5... | collective-permute-start | bytes 196616 | tf_op jit(solution)/shard_map/ppermute | solution.py:154
  5.2 1.4 %collective-permute-start.4 = (f32[128,128]{1,0:T(8,128)S(1)}, f32[128,128]{1,0:T(8,128)S(1)}, u32[]{:S(2)}, u32[]{:S(2)}) collective-permute-start(f32[128,128]{1,0:T(8,128)S(1)} %get-tuple-element.56), channel_id=1, source_target_pairs={{0,12},{4,8},{8,4},{12,0},{16,28},{20,24},{24,20},{28,16},{1,13},{... | collective-permute-start | bytes 196616 | tf_op jit(solution)/shard_map/ppermute | solution.py:154
  6.6 0.2 collective-permute-start.2
  6.8 2.9 %collective-permute-start.1 = (f32[128,128]{1,0:T(8,128)S(1)}, f32[128,128]{1,0:T(8,128)S(1)}, u32[]{:S(2)}, u32[]{:S(2)}) collective-permute-start(f32[128,128]{1,0:T(8,128)S(1)} %get-tuple-element.58), channel_id=1, source_target_pairs={{0,12},{4,8},{8,4},{12,0},{16,28},{20,24},{24,20},{28,16},{1,13},{... | collective-permute-start | bytes 196616 | tf_op jit(solution)/shard_map/ppermute | solution.py:154
  9.7 0.4 %collective-permute-start = (f32[128,128]{1,0:T(8,128)S(1)}, f32[128,128]{1,0:T(8,128)S(1)}, u32[]{:S(2)}, u32[]{:S(2)}) collective-permute-start(f32[128,128]{1,0:T(8,128)S(1)} %get-tuple-element.59), channel_id=1, source_target_pairs={{0,8},{4,12},{8,0},{12,4},{16,24},{20,28},{24,16},{28,20},{1,9},{5... | collective-permute-start | bytes 196616 | tf_op jit(solution)/shard_map/ppermute | solution.py:154
  10.2 0.0 collective-permute-done.3
  10.2 0.9 %collective-permute-done.4 = f32[128,128]{1,0:T(8,128)S(1)} collective-permute-done((f32[128,128]{1,0:T(8,128)S(1)}, f32[128,128]{1,0:T(8,128)S(1)}, u32[]{:S(2)}, u32[]{:S(2)}) %collective-permute-start.4) | collective-permute-done | bytes 65568 | tf_op jit(solution)/shard_map/ppermute | solution.py:154
  11.0 1.6 %collective-permute-done.2 = f32[128,128]{1,0:T(8,128)S(1)} collective-permute-done((f32[128,128]{1,0:T(8,128)S(1)}, f32[128,128]{1,0:T(8,128)S(1)}, u32[]{:S(2)}, u32[]{:S(2)}) %collective-permute-start.2) | collective-permute-done | bytes 65568 | tf_op jit(solution)/shard_map/ppermute | solution.py:154
  12.6 1.4 %collective-permute-done = f32[128,128]{1,0:T(8,128)S(1)} collective-permute-done((f32[128,128]{1,0:T(8,128)S(1)}, f32[128,128]{1,0:T(8,128)S(1)}, u32[]{:S(2)}, u32[]{:S(2)}) %collective-permute-start) | collective-permute-done | bytes 65568 | tf_op jit(solution)/shard_map/ppermute | solution.py:154
  14.0 0.0 collective-permute-done.1
  14.0 0.0 copy-start.2
  14.0 0.0 copy-start.3
  14.0 0.0 copy-start
  14.0 0.0 copy-start.1
  14.1 0.0 copy-start.4
  14.1 0.6 %collective-permute-start.6 = (f32[256,128]{1,0:T(8,128)S(1)}, f32[256,128]{1,0:T(8,128)S(1)}, u32[]{:S(2)}, u32[]{:S(2)}) collective-permute-start(f32[256,128]{1,0:T(8,128)S(1)} %pad_maximum_fusion), channel_id=1, source_target_pairs={{0,4},{4,0},{8,12},{12,8},{16,20},{20,16},{24,28},{28,24},{1,5},{5... | collective-permute-start | bytes 393224 | tf_op jit(solution)/shard_map/ppermute | solution.py:154
  14.7 1.5 %collective-permute-start.5 = (f32[128,128]{1,0:T(8,128)S(1)}, f32[128,128]{1,0:T(8,128)S(1)}, u32[]{:S(2)}, u32[]{:S(2)}) collective-permute-start(f32[128,128]{1,0:T(8,128)S(1)} %get-tuple-element.56), channel_id=1, source_target_pairs={{0,4},{4,0},{8,12},{12,8},{16,20},{20,16},{24,28},{28,24},{1,5},{5... | collective-permute-start | bytes 196616 | tf_op jit(solution)/shard_map/ppermute | solution.py:154
  16.2 2.6 %collective-permute-start.7 = (f32[128,128]{1,0:T(8,128)S(1)}, f32[128,128]{1,0:T(8,128)S(1)}, u32[]{:S(2)}, u32[]{:S(2)}) collective-permute-start(f32[128,128]{1,0:T(8,128)S(1)} %get-tuple-element.54), channel_id=1, source_target_pairs={{0,16},{4,20},{8,24},{12,28},{16,0},{20,4},{24,8},{28,12},{1,17},{... | collective-permute-start | bytes 196616 | tf_op jit(solution)/shard_map/ppermute | solution.py:154
  18.7 0.3 collective-permute-start.8
  19.1 0.0 copy-done.2
  19.1 0.0 copy-done.3
  19.1 0.0 copy-done
  19.1 0.0 copy-done.1
  19.1 0.0 copy-done.4
  19.1 1.4 %shard_map.84 = (f32[128,512]{1,0:T(8,128)S(1)}, f32[128,512]{1,0:T(8,128)S(1)}, f32[128,512]{1,0:T(8,128)S(1)}, f32[128,512]{1,0:T(8,128)S(1)}, f32[1,512]{1,0:T(1,128)S(1)}) custom-call(bf16[128,512]{1,0:T(8,128)(2,1)S(1)} %copy-done, bf16[128,512]{1,0:T(8,128)(2,1)S(1)} %copy-done.1, bf16[128,512]{1,0:T(8,128)(2,1)S(1)} %copy-done.2, ...), custom_call_target="tpu_custom_call" | custom-call | flops 201326592 | bytes 1576960 | tf_op jit(solution)/shard_map/pallas_call | solution.py:141
  20.5 0.0 collective-permute-done.5
  20.5 1.8 %collective-permute-done.7 = f32[128,128]{1,0:T(8,128)S(1)} collective-permute-done((f32[128,128]{1,0:T(8,128)S(1)}, f32[128,128]{1,0:T(8,128)S(1)}, u32[]{:S(2)}, u32[]{:S(2)}) %collective-permute-start.7) | collective-permute-done | bytes 65568 | tf_op jit(solution)/shard_map/ppermute | solution.py:154
  22.4 3.1 %collective-permute-done.8 = f32[128,128]{1,0:T(8,128)S(1)} collective-permute-done((f32[128,128]{1,0:T(8,128)S(1)}, f32[128,128]{1,0:T(8,128)S(1)}, u32[]{:S(2)}, u32[]{:S(2)}) %collective-permute-start.8) | collective-permute-done | bytes 65568 | tf_op jit(solution)/shard_map/ppermute | solution.py:154
  25.5 0.0 collective-permute-done.6
  25.6 0.3 shard_map.86
  25.9 1.6 %collective-permute-start.10 = (f32[1,128]{1,0:T(1,128)S(1)}, f32[1,128]{1,0:T(1,128)S(1)}, u32[]{:S(2)}, u32[]{:S(2)}) collective-permute-start(f32[1,128]{1,0:T(1,128)S(1)} %get-tuple-element.34), channel_id=1, source_target_pairs={{0,2},{1,3},{2,0},{3,1},{4,6},{5,7},{6,4},{7,5},{8,10},{9,11},{10,... | collective-permute-start | bytes 1544 | tf_op jit(solution)/shard_map/ppermute | solution.py:154
  27.5 0.0 collective-permute-start.11
  27.5 0.6 %collective-permute-start.9 = (f32[1,128]{1,0:T(1,128)S(1)}, f32[1,128]{1,0:T(1,128)S(1)}, u32[]{:S(2)}, u32[]{:S(2)}) collective-permute-start(f32[1,128]{1,0:T(1,128)S(1)} %get-tuple-element.34), channel_id=1, source_target_pairs={{0,3},{1,2},{2,1},{3,0},{4,7},{5,6},{6,5},{7,4},{8,11},{9,10},{10,... | collective-permute-start | bytes 1544 | tf_op jit(solution)/shard_map/ppermute | solution.py:154
  28.1 1.0 %shard_map.88 = (bf16[128,512]{1,0:T(8,128)(2,1)}, bf16[128,512]{1,0:T(8,128)(2,1)}, bf16[128,512]{1,0:T(8,128)(2,1)}) custom-call(bf16[128,512]{1,0:T(8,128)(2,1)S(1)} %copy-done.1, bf16[128,512]{1,0:T(8,128)(2,1)S(1)} %copy-done.2, bf16[128,512]{1,0:T(8,128)(2,1)S(1)} %copy-done.3, f32[128,512]{1,0:T(8,128)S(1)} %get-tuple-element.36.dq_part, ...), custom_call_target="tpu_custom_call" | custom-call | flops 50331648 | bytes 1835008 | tf_op jit(solution)/shard_map/pallas_call | solution.py:141
  29.1 0.4 %collective-permute-done.10 = f32[1,128]{1,0:T(1,128)S(1)} collective-permute-done((f32[1,128]{1,0:T(1,128)S(1)}, f32[1,128]{1,0:T(1,128)S(1)}, u32[]{:S(2)}, u32[]{:S(2)}) %collective-permute-start.10) | collective-permute-done | bytes 544 | tf_op jit(solution)/shard_map/ppermute | solution.py:154
  29.5 0.0 collective-permute-done.11
  29.5 0.9 %collective-permute-done.9 = f32[1,128]{1,0:T(1,128)S(1)} collective-permute-done((f32[1,128]{1,0:T(1,128)S(1)}, f32[1,128]{1,0:T(1,128)S(1)}, u32[]{:S(2)}, u32[]{:S(2)}) %collective-permute-start.9) | collective-permute-done | bytes 544 | tf_op jit(solution)/shard_map/ppermute | solution.py:154
  30.5 0.8 %shard_map.87 = bf16[128,512]{1,0:T(8,128)(2,1)} custom-call(f32[128,512]{1,0:T(8,128)S(1)} %get-tuple-element.33.out_ref, f32[4,128]{1,0:T(4,128)S(1)} %pad_maximum_fusion.3.squares_ref, f32[1,512]{1,0:T(1,128)S(1)} %get-tuple-element.35.gain_ref), custom_call_target="tpu_custom_call" | custom-call | flops 131072 | bytes 397312 | tf_op jit(solution)/shard_map/pallas_call | solution.py:141
  (10 shorter events, 0.2 us)
Async XLA Ops:
  2.1 8.1 %collective-permute-start.3 = (f32[128,128]{1,0:T(8,128)S(1)}, f32[128,128]{1,0:T(8,128)S(1)}, u32[]{:S(2)}, u32[]{:S(2)}) collective-permute-start(f32[128,128]{1,0:T(8,128)S(1)} %get-tuple-element.57), channel_id=1, source_target_pairs={{0,8},{4,12},{8,0},{12,4},{16,24},{20,28},{24,16},{28,20},{1,9},{5... | collective-permute-start | bytes 196616 | tf_op jit(solution)/shard_map/ppermute | solution.py:154
  5.2 5.8 %collective-permute-start.4 = (f32[128,128]{1,0:T(8,128)S(1)}, f32[128,128]{1,0:T(8,128)S(1)}, u32[]{:S(2)}, u32[]{:S(2)}) collective-permute-start(f32[128,128]{1,0:T(8,128)S(1)} %get-tuple-element.56), channel_id=1, source_target_pairs={{0,12},{4,8},{8,4},{12,0},{16,28},{20,24},{24,20},{28,16},{1,13},{... | collective-permute-start | bytes 196616 | tf_op jit(solution)/shard_map/ppermute | solution.py:154
  6.6 6.0 %collective-permute-start.2 = (f32[128,128]{1,0:T(8,128)S(1)}, f32[128,128]{1,0:T(8,128)S(1)}, u32[]{:S(2)}, u32[]{:S(2)}) collective-permute-start(f32[128,128]{1,0:T(8,128)S(1)} %get-tuple-element.58), channel_id=1, source_target_pairs={{0,4},{4,0},{8,12},{12,8},{16,20},{20,16},{24,28},{28,24},{1,5},{5... | collective-permute-start | bytes 196616 | tf_op jit(solution)/shard_map/ppermute | solution.py:154
  6.8 7.1 %collective-permute-start.1 = (f32[128,128]{1,0:T(8,128)S(1)}, f32[128,128]{1,0:T(8,128)S(1)}, u32[]{:S(2)}, u32[]{:S(2)}) collective-permute-start(f32[128,128]{1,0:T(8,128)S(1)} %get-tuple-element.58), channel_id=1, source_target_pairs={{0,12},{4,8},{8,4},{12,0},{16,28},{20,24},{24,20},{28,16},{1,13},{... | collective-permute-start | bytes 196616 | tf_op jit(solution)/shard_map/ppermute | solution.py:154
  9.7 4.3 %collective-permute-start = (f32[128,128]{1,0:T(8,128)S(1)}, f32[128,128]{1,0:T(8,128)S(1)}, u32[]{:S(2)}, u32[]{:S(2)}) collective-permute-start(f32[128,128]{1,0:T(8,128)S(1)} %get-tuple-element.59), channel_id=1, source_target_pairs={{0,8},{4,12},{8,0},{12,4},{16,24},{20,28},{24,16},{28,20},{1,9},{5... | collective-permute-start | bytes 196616 | tf_op jit(solution)/shard_map/ppermute | solution.py:154
  14.0 5.1 %copy-start.2 = (bf16[128,512]{1,0:T(8,128)(2,1)S(1)}, bf16[128,512]{1,0:T(8,128)(2,1)}, u32[]{:S(2)}) copy-start(bf16[128,512]{1,0:T(8,128)(2,1)} %v_ref.3) | copy-start | bytes 393220
  14.0 5.1 %copy-start.3 = (bf16[128,512]{1,0:T(8,128)(2,1)S(1)}, bf16[128,512]{1,0:T(8,128)(2,1)}, u32[]{:S(2)}) copy-start(bf16[128,512]{1,0:T(8,128)(2,1)} %g_ref.3) | copy-start | bytes 393220
  14.0 5.1 %copy-start = (bf16[128,512]{1,0:T(8,128)(2,1)S(1)}, bf16[128,512]{1,0:T(8,128)(2,1)}, u32[]{:S(2)}) copy-start(bf16[128,512]{1,0:T(8,128)(2,1)} %q_ref.3) | copy-start | bytes 393220
  14.0 5.0 %copy-start.1 = (bf16[128,512]{1,0:T(8,128)(2,1)S(1)}, bf16[128,512]{1,0:T(8,128)(2,1)}, u32[]{:S(2)}) copy-start(bf16[128,512]{1,0:T(8,128)(2,1)} %k_ref.3) | copy-start | bytes 393220
  14.1 5.0 %copy-start.4 = (f32[512]{0:T(512)S(1)}, f32[512]{0:T(512)}, u32[]{:S(2)}) copy-start(f32[512]{0:T(512)} %param.9) | copy-start | bytes 6148
  14.1 11.5 %collective-permute-start.6 = (f32[256,128]{1,0:T(8,128)S(1)}, f32[256,128]{1,0:T(8,128)S(1)}, u32[]{:S(2)}, u32[]{:S(2)}) collective-permute-start(f32[256,128]{1,0:T(8,128)S(1)} %pad_maximum_fusion), channel_id=1, source_target_pairs={{0,4},{4,0},{8,12},{12,8},{16,20},{20,16},{24,28},{28,24},{1,5},{5... | collective-permute-start | bytes 393224 | tf_op jit(solution)/shard_map/ppermute | solution.py:154
  14.7 5.9 %collective-permute-start.5 = (f32[128,128]{1,0:T(8,128)S(1)}, f32[128,128]{1,0:T(8,128)S(1)}, u32[]{:S(2)}, u32[]{:S(2)}) collective-permute-start(f32[128,128]{1,0:T(8,128)S(1)} %get-tuple-element.56), channel_id=1, source_target_pairs={{0,4},{4,0},{8,12},{12,8},{16,20},{20,16},{24,28},{28,24},{1,5},{5... | collective-permute-start | bytes 196616 | tf_op jit(solution)/shard_map/ppermute | solution.py:154
  16.2 6.2 %collective-permute-start.7 = (f32[128,128]{1,0:T(8,128)S(1)}, f32[128,128]{1,0:T(8,128)S(1)}, u32[]{:S(2)}, u32[]{:S(2)}) collective-permute-start(f32[128,128]{1,0:T(8,128)S(1)} %get-tuple-element.54), channel_id=1, source_target_pairs={{0,16},{4,20},{8,24},{12,28},{16,0},{20,4},{24,8},{28,12},{1,17},{... | collective-permute-start | bytes 196616 | tf_op jit(solution)/shard_map/ppermute | solution.py:154
  18.7 6.8 %collective-permute-start.8 = (f32[128,128]{1,0:T(8,128)S(1)}, f32[128,128]{1,0:T(8,128)S(1)}, u32[]{:S(2)}, u32[]{:S(2)}) collective-permute-start(f32[128,128]{1,0:T(8,128)S(1)} %get-tuple-element.54), channel_id=1, source_target_pairs={{0,20},{4,16},{8,28},{12,24},{16,4},{20,0},{24,12},{28,8},{1,21},{... | collective-permute-start | bytes 196616 | tf_op jit(solution)/shard_map/ppermute | solution.py:154
  25.9 3.6 %collective-permute-start.10 = (f32[1,128]{1,0:T(1,128)S(1)}, f32[1,128]{1,0:T(1,128)S(1)}, u32[]{:S(2)}, u32[]{:S(2)}) collective-permute-start(f32[1,128]{1,0:T(1,128)S(1)} %get-tuple-element.34), channel_id=1, source_target_pairs={{0,2},{1,3},{2,0},{3,1},{4,6},{5,7},{6,4},{7,5},{8,10},{9,11},{10,... | collective-permute-start | bytes 1544 | tf_op jit(solution)/shard_map/ppermute | solution.py:154
  27.5 2.1 %collective-permute-start.11 = (f32[1,128]{1,0:T(1,128)S(1)}, f32[1,128]{1,0:T(1,128)S(1)}, u32[]{:S(2)}, u32[]{:S(2)}) collective-permute-start(f32[1,128]{1,0:T(1,128)S(1)} %get-tuple-element.34), channel_id=1, source_target_pairs={{0,1},{1,0},{2,3},{3,2},{4,5},{5,4},{6,7},{7,6},{8,9},{9,8},{10,11... | collective-permute-start | bytes 1544 | tf_op jit(solution)/shard_map/ppermute | solution.py:154
  27.5 3.0 %collective-permute-start.9 = (f32[1,128]{1,0:T(1,128)S(1)}, f32[1,128]{1,0:T(1,128)S(1)}, u32[]{:S(2)}, u32[]{:S(2)}) collective-permute-start(f32[1,128]{1,0:T(1,128)S(1)} %get-tuple-element.34), channel_id=1, source_target_pairs={{0,3},{1,2},{2,1},{3,0},{4,7},{5,6},{6,5},{7,4},{8,11},{9,10},{10,... | collective-permute-start | bytes 1544 | tf_op jit(solution)/shard_map/ppermute | solution.py:154

commit v6 on v3

--- a/solution.py
+++ b/solution.py
@@ -58,21 +58,81 @@
     return jnp.concatenate([jnp.where(low, state, zero), jnp.where(low, zero, state)], axis=0)
 
 
-def states_kernel(q_hbm, k_hbm, v_hbm, g_hbm, kv_ref, qg_ref, q_ref, k_ref, v_ref, g_ref, sems):
-    sources = (k_hbm, v_hbm, g_hbm, q_hbm)
-    targets = (k_ref, v_ref, g_ref, q_ref)
-    copies = [
-        pltpu.make_async_copy(source, target, sems.at[i])
-        for i, (source, target) in enumerate(zip(sources, targets))
-    ]
-    for copy in copies:
+def states_kernel(q_hbm, k_hbm, v_hbm, g_hbm, kv_ref, qg_ref, left_ref, right_ref, sems):
+    copies = start_loads(q_hbm, k_hbm, v_hbm, g_hbm, left_ref, right_ref, sems)
+    for out_ref, pair in ((kv_ref, 0), (qg_ref, 1)):
+        wait_loads(copies, pair)
+        for t in range(out_ref.shape[0] // HEAD_DIM):
+            lanes = slice(t * LANES, (t + 1) * LANES)
+            rows = slice(t * HEAD_DIM, (t + 1) * HEAD_DIM)
+            out_ref[rows] = pack_state(dot(left_ref[pair, :, lanes], right_ref[pair, :, lanes], TN))
+
+
+def start_loads(q_hbm, k_hbm, v_hbm, g_hbm, left_ref, right_ref, sems):
+    copies = []
+    for pair, (left, right) in enumerate(((k_hbm, v_hbm), (g_hbm, q_hbm))):
+        copies.append(
+            (
+                pltpu.make_async_copy(left, left_ref.at[pair], sems.at[pair, 0]),
+                pltpu.make_async_copy(right, right_ref.at[pair], sems.at[pair, 1]),
+            )
+        )
+    for copy in (*copies[0], *copies[1]):
         copy.start()
-    for copy in copies:
+    return copies
+
+
+def wait_loads(copies, pair):
+    for copy in copies[pair]:
         copy.wait()
-    for t in range(tiles(q_ref)):
-        rows = slice(t * HEAD_DIM, (t + 1) * HEAD_DIM)
-        kv_ref[rows] = pack_state(dot(tile(k_ref, t), tile(v_ref, t), TN))
-        qg_ref[rows] = pack_state(dot(tile(g_ref, t), tile(q_ref, t), TN))
+
+
+def place_on(axis):
+    index = lax.axis_index(axis)
+    return index // (lax.axis_size(axis) // 2), index % 2
+
+
+def halves_kernel(axis, *refs):
+    q_hbm, k_hbm, v_hbm, g_hbm, a_mine, a_other, b_mine, b_other, left_ref, right_ref, sems = refs
+    copies = start_loads(q_hbm, k_hbm, v_hbm, g_hbm, left_ref, right_ref, sems)
+    upper, odd = place_on(axis)
+    count = left_ref.shape[2] // LANES // 2
+    wait_loads(copies, 0)
+    wait_loads(copies, 1)
+    outs = ((a_mine, upper, odd), (a_other, upper, 1 - odd), (b_mine, 1 - upper, odd), (b_other, 1 - upper, 1 - odd))
+    for out_ref, pair, half in outs:
+        for t in range(count):
+            lanes = pl.ds(pl.multiple_of((half * count + t) * LANES, LANES), LANES)
+            rows = slice(t * HEAD_DIM, (t + 1) * HEAD_DIM)
+            out_ref[rows] = pack_state(dot(left_ref[pair, :, lanes], right_ref[pair, :, lanes], TN))
+
+
+def whole_states(pieces, axis):
+    if len(pieces) == 2:
+        return tuple(lambda t, ref=ref: ref[t * HEAD_DIM : (t + 1) * HEAD_DIM] for ref in pieces)
+    a_sum, a1, b_sum, b1, got, t_mine, t_other = pieces
+    upper, odd = place_on(axis)
+    mid = a_sum.shape[0]
+    count = mid // HEAD_DIM
+
+    def part(t, is_a):
+        start = t % count * HEAD_DIM
+        rows = slice(start, start + HEAD_DIM)
+        if is_a:
+            mine = a_sum[rows] + jnp.where(odd != upper, a1[rows], 0.0)
+            other = got[rows]
+        else:
+            mine = b_sum[rows] + jnp.where(odd == upper, b1[rows], 0.0) + t_mine[rows]
+            other = got[mid + start : mid + start + HEAD_DIM] + t_other[rows]
+        return jnp.where(odd == t // count, mine, other)
+
+    def kv_of(t):
+        return jnp.where(upper == 1, part(t, False), part(t, True))
+
+    def qg_of(t):
+        return jnp.where(upper == 1, part(t, True), part(t, False))
+
+    return kv_of, qg_of
 
 
 def block_kernel(
@@ -100,11 +160,13 @@
         dv_ref[:, cols] = dv
 
 
-def output_kernel(factor, q_ref, part_ref, kv_ref, out_ref, squares_ref):
+def output_kernel(factor, axis, q_ref, part_ref, *refs):
+    *pieces, out_ref, squares_ref = refs
+    kv_of, _ = whole_states(pieces, axis)
     total = None
     for t in range(tiles(q_ref)):
         cols = slice(t * LANES, (t + 1) * LANES)
-        state = unpack_state((factor * kv_ref[t * HEAD_DIM : (t + 1) * HEAD_DIM]).astype(bf16))
+        state = unpack_state((factor * kv_of(t)).astype(bf16))
         out = part_ref[:, cols] + dot(tile(q_ref, t), state)
         out_ref[:, cols] = out
         square = out * out
@@ -112,21 +174,23 @@
     squares_ref[...] = jnp.sum(total.T, axis=0, keepdims=True)
 
 
-def grads_kernel(
-    factor, k_ref, v_ref, g_ref, dq_part, dk_part, dv_part, kv_ref, qg_ref, dq_ref, dk_ref, dv_ref
-):
+def grads_kernel(factor, axis, k_ref, v_ref, g_ref, dq_part, dk_part, dv_part, *refs):
+    *pieces, dq_ref, dk_ref, dv_ref = refs
+    kv_of, qg_of = whole_states(pieces, axis)
     for t in range(tiles(k_ref)):
         cols = slice(t * LANES, (t + 1) * LANES)
-        rows = slice(t * HEAD_DIM, (t + 1) * HEAD_DIM)
-        state = unpack_state((factor * kv_ref[rows]).astype(bf16))
-        grad_state = unpack_state((factor * qg_ref[rows]).astype(bf16))
+        state = unpack_state((factor * kv_of(t)).astype(bf16))
+        grad_state = unpack_state((factor * qg_of(t)).astype(bf16))
         dq_ref[:, cols] = (dq_part[:, cols] + dot(tile(g_ref, t), state, NT)).astype(bf16)
         dk_ref[:, cols] = (dk_part[:, cols] + dot(tile(v_ref, t), grad_state)).astype(bf16)
         dv_ref[:, cols] = (dv_part[:, cols] + dot(tile(k_ref, t), grad_state, NT)).astype(bf16)
 
 
-def norm_kernel(width, out_ref, squares_ref, gain_ref, normed_ref):
-    total = jnp.sum(squares_ref[...], axis=0, keepdims=True)
+def norm_kernel(width, out_ref, gain_ref, *refs):
+    *shares, normed_ref = refs
+    total = shares[0][...]
+    for share in shares[1:]:
+        total = total + share[...]
     scale = lax.rsqrt(total / width + epsilon)
     scale = jnp.broadcast_to(scale, (LANES, scale.shape[1])).T
     for t in range(tiles(out_ref)):
@@ -154,23 +218,13 @@
     return lax.ppermute(x, axis, [(i, i ^ distance) for i in range(size)])
 
 
-def halves(x, odd):
-    mid = x.shape[0] // 2
-    low, high = x[:mid], x[mid:]
-    return jnp.where(odd, high, low), jnp.where(odd, low, high)
-
-
-def join(mine, other, odd):
-    return jnp.concatenate([jnp.where(odd, other, mine), jnp.where(odd, mine, other)], axis=0)
-
-
-def scan_states(kv, qg, axis):
+def scan_states(axis, states, halves):
     count = lax.axis_size(axis)
     index = lax.axis_index(axis)
     bit = lambda d: (index & d) != 0
-    zero = jnp.zeros_like(kv)
     top = count // 2
     if count & (count - 1):
+        kv, qg = states()
         position = jnp.arange(count)[:, None, None]
         every_kv = lax.all_gather(kv, axis)
         every_qg = lax.all_gather(qg, axis)
@@ -178,8 +232,9 @@
             jnp.sum(jnp.where(position < index, every_kv, 0.0), axis=0),
             jnp.sum(jnp.where(position > index, every_qg, 0.0), axis=0),
         )
-    if count < 4:
-        before, after, total_kv, total_qg = zero, zero, kv, qg
+    if count < 8:
+        total_kv, total_qg = states()
+        before, after = jnp.zeros_like(total_kv), jnp.zeros_like(total_qg)
         distance = 1
         while distance < count:
             got_kv, got_qg = swap(total_kv, axis, distance), swap(total_qg, axis, distance)
@@ -188,23 +243,27 @@
             total_kv, total_qg = total_kv + got_kv, total_qg + got_qg
             distance *= 2
         return before, after
-    odd, upper = bit(1), bit(top)
-    a, b = jnp.where(upper, qg, kv), jnp.where(upper, kv, qg)
+    upper = bit(top)
     a_enters = lambda d: bit(d) != upper
     b_enters = lambda d: bit(d) == upper
 
     def send(x, distance):
         return swap(x, axis, distance)
 
-    (a_mine, a_other), (b_mine, b_other) = halves(a, odd), halves(b, odd)
+    a_mine, a_other, b_mine, b_other = halves()
+    a3 = send(a_other, 3)
+    a2 = send(a_mine, 2)
     a1 = send(a_other, 1)
+    b3 = send(b_other, 3)
+    b2 = send(b_mine, 2)
     b1 = send(b_other, 1)
-    a_total, b_total = a_mine + a1, b_mine + b1
-    a_sum = b_sum = jnp.zeros_like(a_mine)
-    distance = 2
+    a_pair, b_pair = a2 + a3, b2 + b3
+    a_sum = jnp.where(a_enters(2), a_pair, 0.0)
+    b_sum = jnp.where(b_enters(2), b_pair, 0.0)
+    a_total, b_total = a_mine + a1 + a_pair, b_mine + b1 + b_pair
+    distance = 4
     while distance < top:
-        a_got = send(a_total, distance)
-        b_got = send(b_total, distance)
+        a_got, b_got = send(a_total, distance), send(b_total, distance)
         a_sum = a_sum + jnp.where(a_enters(distance), a_got, 0.0)
         b_sum = b_sum + jnp.where(b_enters(distance), b_got, 0.0)
         a_total, b_total = a_total + a_got, b_total + b_got
@@ -214,25 +273,23 @@
     a_out = a_sum + jnp.where(a_enters(1), 0.0, a_mine)
     b_out = b_sum + jnp.where(b_enters(1), 0.0, b_mine)
     got = send(jnp.concatenate([a_out, b_out], axis=0), 1)
-    mid = a_mine.shape[0]
-    a_own = a_sum + jnp.where(a_enters(1), a1, 0.0)
-    b_own = b_sum + jnp.where(b_enters(1), b1, 0.0) + t_mine
-    a_all = join(a_own, got[:mid], odd)
-    b_all = join(b_own, got[mid:] + t_other, odd)
-    return jnp.where(upper, b_all, a_all), jnp.where(upper, a_all, b_all)
+    return a_sum, a1, b_sum, b1, got, t_mine, t_other
 
 
 def all_shares(row, axis):
     count = lax.axis_size(axis)
     if count & (count - 1):
-        return lax.psum(row, axis)
+        return [lax.psum(row, axis)]
     if count > 4:
         distance = 1
         while distance < count:
             row = row + swap(row, axis, distance)
             distance *= 2
-        return row
-    return jnp.concatenate([row] + [swap(row, axis, d) for d in range(1, count)], axis=0)
+        return [row]
+    rows = [row]
+    for distance in range(count - 1, 0, -1):
+        rows.append(swap(row, axis, distance))
+    return rows
 
 
 def body(queries, keys, values, d_out, gain):
@@ -242,39 +299,48 @@
     wide = jax.ShapeDtypeStruct((length, width), f32)
     narrow = jax.ShapeDtypeStruct((length, width), bf16)
     inputs = (queries, keys, values, d_out)
-    kv, qg = call(
-        states_kernel,
-        [packed] * 2,
-        inputs,
-        4 * length * LANES * width,
-        vmem=64 * MIB - 10600 * 1024,
-        inputs_at=pltpu.HBM,
-        scratch_shapes=[pltpu.VMEM((length, width), bf16)] * 4 + [pltpu.SemaphoreType.DMA((4,))],
-    )
+    half = jax.ShapeDtypeStruct((packed.shape[0] // 2, LANES), f32)
+
+    def products(kernel, outs):
+        return call(
+            kernel,
+            outs,
+            inputs,
+            4 * length * LANES * width,
+            vmem=64 * MIB - 10600 * 1024,
+            inputs_at=pltpu.HBM,
+            scratch_shapes=[pltpu.VMEM((2, length, width), bf16)] * 2
+            + [pltpu.SemaphoreType.DMA((2, 2))],
+        )
+
     out_part, dq_part, dk_part, dv_part, gain_row = call(
         functools.partial(block_kernel, factor),
         [wide] * 4 + [jax.ShapeDtypeStruct((1, width), f32)],
         (*inputs, gain[None]),
         24 * length * LANES * width,
     )
-    before, after = scan_states(kv, qg, "seq")
+    pieces = scan_states(
+        "seq",
+        lambda: products(states_kernel, [packed] * 2),
+        lambda: products(functools.partial(halves_kernel, "seq"), [half] * 4),
+    )
     out, squares = call(
-        functools.partial(output_kernel, factor),
+        functools.partial(output_kernel, factor, "seq"),
         [wide, jax.ShapeDtypeStruct((1, length), f32)],
-        (queries, out_part, before),
+        (queries, out_part, *pieces),
         2 * length * LANES * width,
     )
     shares = all_shares(squares, "head")
     dq, dk, dv = call(
-        functools.partial(grads_kernel, factor),
+        functools.partial(grads_kernel, factor, "seq"),
         [narrow] * 3,
-        (keys, values, d_out, dq_part, dk_part, dv_part, before, after),
+        (keys, values, d_out, dq_part, dk_part, dv_part, *pieces),
         6 * length * LANES * width,
     )
     normed = call(
         functools.partial(norm_kernel, width * lax.axis_size("head")),
         [narrow],
-        (out, shares, gain_row),
+        (out, gain_row, *shares),
         2 * length * width,
     )
     return normed, dq, dk, dv

time: 30.5 us -> 30.2 us (level)
  waiting for transfers between devices: 11.2 us -> 9.42 us
  starting transfers between devices: 13.2 us -> 14.9 us
    ppermute x10 -> x12, waiting for transfers between devices: 11.2 us -> 9.42 us  [swap(): return lax.ppermute(x, axis, [(i, i ^ distance) for i in range(size)])]
    ppermute x10 -> x12, starting transfers between devices: 13.2 us -> 14.9 us  [swap(): return lax.ppermute(x, axis, [(i, i ^ distance) for i in range(size)])]
  transfers between devices with their start and end apart: 10 -> 12, of which waited for: 7 -> 6; matrix products, arithmetic and copies ran while one was open for 0% -> 0% of each run, Pallas kernels for 8% -> 8%
where the time goes in v6:
time: 30.2 us; the launch traced here: 30.1 us
  starting transfers between devices  14.9 us (49%)
  waiting for transfers between devices  9.42 us (31%)
  Pallas kernels  4.94 us (16%)
  between operations  0.75 us (2%)
    ppermute x12, starting transfers between devices, swap(): return lax.ppermute(x, axis, [(i, i ^ distance) for i in range(size)])  14.9 us
    ppermute x12, waiting for transfers between devices, swap(): return lax.ppermute(x, axis, [(i, i ^ distance) for i in range(size)])  9.42 us
    pallas_call x5, Pallas kernels, call(): pl.pallas_call(kernel, out_shape=outs[0] if single else tuple(outs), in_s...  4.94 us
  transfers between devices with their start and end apart: 12, of which 6 were waited for; matrix products, arithmetic and copies ran while one was open for 0% of the time, Pallas kernels for 8%

profile of v6, /device:TPU:0, one launch (start us, length us, event | category | flops | bytes accessed | tf_op | source)
XLA Modules:
  0.0 30.1 jit_solution(17606570074586704176)
XLA Ops:
  0.6 1.4 %shard_map.85 = (f32[128,128]{1,0:T(8,128)S(1)}, f32[128,128]{1,0:T(8,128)S(1)}, f32[128,128]{1,0:T(8,128)S(1)}, f32[128,128]{1,0:T(8,128)S(1)}) custom-call(bf16[128,512]{1,0:T(8,128)(2,1)} %q_ref.3, bf16[128,512]{1,0:T(8,128)(2,1)} %k_ref.3, bf16[128,512]{1,0:T(8,128)(2,1)} %v_ref.3, bf16[128,512]{1,0:T(8,128)(2,1)} %g_ref.3), custom_call_target="tpu_custom_call" | custom-call | flops 33554432 | bytes 786432 | tf_op jit(solution)/shard_map/pallas_call | solution.py:205
  2.0 3.1 %collective-permute-start.3 = (f32[128,128]{1,0:T(8,128)S(1)}, f32[128,128]{1,0:T(8,128)S(1)}, u32[]{:S(2)}, u32[]{:S(2)}) collective-permute-start(f32[128,128]{1,0:T(8,128)S(1)} %get-tuple-element.21), channel_id=1, source_target_pairs={{0,8},{4,12},{8,0},{12,4},{16,24},{20,28},{24,16},{28,20},{1,9},{5... | collective-permute-start | bytes 196616 | tf_op jit(solution)/shard_map/ppermute | solution.py:218
  5.2 1.4 %collective-permute-start.4 = (f32[128,128]{1,0:T(8,128)S(1)}, f32[128,128]{1,0:T(8,128)S(1)}, u32[]{:S(2)}, u32[]{:S(2)}) collective-permute-start(f32[128,128]{1,0:T(8,128)S(1)} %get-tuple-element.22), channel_id=1, source_target_pairs={{0,12},{4,8},{8,4},{12,0},{16,28},{20,24},{24,20},{28,16},{1,13},{... | collective-permute-start | bytes 196616 | tf_op jit(solution)/shard_map/ppermute | solution.py:218
  6.5 1.5 %collective-permute-start.1 = (f32[128,128]{1,0:T(8,128)S(1)}, f32[128,128]{1,0:T(8,128)S(1)}, u32[]{:S(2)}, u32[]{:S(2)}) collective-permute-start(f32[128,128]{1,0:T(8,128)S(1)} %get-tuple-element.20), channel_id=1, source_target_pairs={{0,12},{4,8},{8,4},{12,0},{16,28},{20,24},{24,20},{28,16},{1,13},{... | collective-permute-start | bytes 196616 | tf_op jit(solution)/shard_map/ppermute | solution.py:218
  8.1 1.5 %collective-permute-start.2 = (f32[128,128]{1,0:T(8,128)S(1)}, f32[128,128]{1,0:T(8,128)S(1)}, u32[]{:S(2)}, u32[]{:S(2)}) collective-permute-start(f32[128,128]{1,0:T(8,128)S(1)} %get-tuple-element.20), channel_id=1, source_target_pairs={{0,4},{4,0},{8,12},{12,8},{16,20},{20,16},{24,28},{28,24},{1,5},{5... | collective-permute-start | bytes 196616 | tf_op jit(solution)/shard_map/ppermute | solution.py:218
  9.6 0.4 %collective-permute-start = (f32[128,128]{1,0:T(8,128)S(1)}, f32[128,128]{1,0:T(8,128)S(1)}, u32[]{:S(2)}, u32[]{:S(2)}) collective-permute-start(f32[128,128]{1,0:T(8,128)S(1)} %get-tuple-element.19), channel_id=1, source_target_pairs={{0,8},{4,12},{8,0},{12,4},{16,24},{20,28},{24,16},{28,20},{1,9},{5... | collective-permute-start | bytes 196616 | tf_op jit(solution)/shard_map/ppermute | solution.py:218
  10.0 0.0 collective-permute-done.3
  10.0 1.0 %collective-permute-done.4 = f32[128,128]{1,0:T(8,128)S(1)} collective-permute-done((f32[128,128]{1,0:T(8,128)S(1)}, f32[128,128]{1,0:T(8,128)S(1)}, u32[]{:S(2)}, u32[]{:S(2)}) %collective-permute-start.4) | collective-permute-done | bytes 65568 | tf_op jit(solution)/shard_map/ppermute | solution.py:218
  11.0 2.8 %collective-permute-done = f32[128,128]{1,0:T(8,128)S(1)} collective-permute-done((f32[128,128]{1,0:T(8,128)S(1)}, f32[128,128]{1,0:T(8,128)S(1)}, u32[]{:S(2)}, u32[]{:S(2)}) %collective-permute-start) | collective-permute-done | bytes 65568 | tf_op jit(solution)/shard_map/ppermute | solution.py:218
  13.8 0.0 collective-permute-done.1
  13.8 0.0 collective-permute-done.2.refs_1_
  13.8 0.0 copy-start.2
  13.8 0.0 copy-start.3
  13.9 0.0 copy-start
  13.9 0.0 copy-start.1
  13.9 0.0 copy-start.4
  13.9 0.6 %collective-permute-start.6 = (f32[256,128]{1,0:T(8,128)S(1)}, f32[256,128]{1,0:T(8,128)S(1)}, u32[]{:S(2)}, u32[]{:S(2)}) collective-permute-start(f32[256,128]{1,0:T(8,128)S(1)} %pad_maximum_fusion), channel_id=1, source_target_pairs={{0,4},{4,0},{8,12},{12,8},{16,20},{20,16},{24,28},{28,24},{1,5},{5... | collective-permute-start | bytes 393224 | tf_op jit(solution)/shard_map/ppermute | solution.py:218
  14.5 1.5 %collective-permute-start.5 = (f32[128,128]{1,0:T(8,128)S(1)}, f32[128,128]{1,0:T(8,128)S(1)}, u32[]{:S(2)}, u32[]{:S(2)}) collective-permute-start(f32[128,128]{1,0:T(8,128)S(1)} %get-tuple-element.22), channel_id=1, source_target_pairs={{0,4},{4,0},{8,12},{12,8},{16,20},{20,16},{24,28},{28,24},{1,5},{5... | collective-permute-start | bytes 196616 | tf_op jit(solution)/shard_map/ppermute | solution.py:218
  16.0 2.6 %collective-permute-start.7 = (f32[128,128]{1,0:T(8,128)S(1)}, f32[128,128]{1,0:T(8,128)S(1)}, u32[]{:S(2)}, u32[]{:S(2)}) collective-permute-start(f32[128,128]{1,0:T(8,128)S(1)} %get-tuple-element.36), channel_id=1, source_target_pairs={{0,16},{4,20},{8,24},{12,28},{16,0},{20,4},{24,8},{28,12},{1,17},{... | collective-permute-start | bytes 196616 | tf_op jit(solution)/shard_map/ppermute | solution.py:218
  18.6 0.3 %collective-permute-start.8 = (f32[128,128]{1,0:T(8,128)S(1)}, f32[128,128]{1,0:T(8,128)S(1)}, u32[]{:S(2)}, u32[]{:S(2)}) collective-permute-start(f32[128,128]{1,0:T(8,128)S(1)} %get-tuple-element.36), channel_id=1, source_target_pairs={{0,20},{4,16},{8,28},{12,24},{16,4},{20,0},{24,12},{28,8},{1,21},{... | collective-permute-start | bytes 196616 | tf_op jit(solution)/shard_map/ppermute | solution.py:218
  18.9 0.0 copy-done.2
  18.9 0.0 copy-done.3
  18.9 0.0 copy-done
  18.9 0.0 copy-done.1
  18.9 0.0 copy-done.4
  19.0 1.4 %shard_map.84 = (f32[128,512]{1,0:T(8,128)S(1)}, f32[128,512]{1,0:T(8,128)S(1)}, f32[128,512]{1,0:T(8,128)S(1)}, f32[128,512]{1,0:T(8,128)S(1)}, f32[1,512]{1,0:T(1,128)S(1)}) custom-call(bf16[128,512]{1,0:T(8,128)(2,1)S(1)} %copy-done, bf16[128,512]{1,0:T(8,128)(2,1)S(1)} %copy-done.1, bf16[128,512]{1,0:T(8,128)(2,1)S(1)} %copy-done.2, ...), custom_call_target="tpu_custom_call" | custom-call | flops 201326592 | bytes 1576960 | tf_op jit(solution)/shard_map/pallas_call | solution.py:205
  20.4 0.0 collective-permute-done.5.refs_3_
  20.4 2.7 %collective-permute-done.7.refs_5_ = f32[128,128]{1,0:T(8,128)S(1)} collective-permute-done((f32[128,128]{1,0:T(8,128)S(1)}, f32[128,128]{1,0:T(8,128)S(1)}, u32[]{:S(2)}, u32[]{:S(2)}) %collective-permute-start.7) | collective-permute-done | bytes 65568 | tf_op jit(solution)/shard_map/ppermute | solution.py:218
  23.1 2.2 %collective-permute-done.8.refs_6_ = f32[128,128]{1,0:T(8,128)S(1)} collective-permute-done((f32[128,128]{1,0:T(8,128)S(1)}, f32[128,128]{1,0:T(8,128)S(1)}, u32[]{:S(2)}, u32[]{:S(2)}) %collective-permute-start.8) | collective-permute-done | bytes 65568 | tf_op jit(solution)/shard_map/ppermute | solution.py:218
  25.3 0.0 collective-permute-done.6.refs_4_
  25.3 0.3 shard_map.86
  25.6 0.1 collective-permute-start.9
  25.7 1.6 %collective-permute-start.10 = (f32[1,128]{1,0:T(1,128)S(1)}, f32[1,128]{1,0:T(1,128)S(1)}, u32[]{:S(2)}, u32[]{:S(2)}) collective-permute-start(f32[1,128]{1,0:T(1,128)S(1)} %get-tuple-element.25.refs_0_), channel_id=1, source_target_pairs={{0,2},{1,3},{2,0},{3,1},{4,6},{5,7},{6,4},{7,5},{8,10},{9,11},{10,... | collective-permute-start | bytes 1544 | tf_op jit(solution)/shard_map/ppermute | solution.py:218
  27.2 0.3 collective-permute-start.11
  27.5 1.1 %shard_map.88 = (bf16[128,512]{1,0:T(8,128)(2,1)}, bf16[128,512]{1,0:T(8,128)(2,1)}, bf16[128,512]{1,0:T(8,128)(2,1)}) custom-call(bf16[128,512]{1,0:T(8,128)(2,1)S(1)} %copy-done.1, bf16[128,512]{1,0:T(8,128)(2,1)S(1)} %copy-done.2, bf16[128,512]{1,0:T(8,128)(2,1)S(1)} %copy-done.3, f32[128,512]{1,0:T(8,128)S(1)} %get-tuple-element.26.dq_part, ...), custom_call_target="tpu_custom_call" | custom-call | flops 50331648 | bytes 2097152 | tf_op jit(solution)/shard_map/pallas_call | solution.py:205
  28.6 0.1 collective-permute-done.9.refs_1_
  28.6 0.7 %collective-permute-done.10.refs_2_ = f32[1,128]{1,0:T(1,128)S(1)} collective-permute-done((f32[1,128]{1,0:T(1,128)S(1)}, f32[1,128]{1,0:T(1,128)S(1)}, u32[]{:S(2)}, u32[]{:S(2)}) %collective-permute-start.10) | collective-permute-done | bytes 544 | tf_op jit(solution)/shard_map/ppermute | solution.py:218
  29.3 0.0 collective-permute-done.11.refs_3_
  29.3 0.8 %shard_map.87 = bf16[128,512]{1,0:T(8,128)(2,1)} custom-call(f32[128,512]{1,0:T(8,128)S(1)} %get-tuple-element.23.out_ref, f32[1,512]{1,0:T(1,128)S(1)} %get-tuple-element.24.gain_ref, f32[1,128]{1,0:T(1,128)S(1)} %get-tuple-element.25.refs_0_, f32[1,128]{1,0:T(1,128)S(1)} %collective-permute-done.9.refs_1_, f32[1,128]{1,0:T(1,128)S(1)} %collective-permute-done.10.refs_2_, ...), custom_call_target="tpu_custom_call" | custom-call | flops 131072 | bytes 397312 | tf_op jit(solution)/shard_map/pallas_call | solution.py:205
  (3 shorter events, 0.1 us)
Async XLA Ops:
  2.0 8.0 %collective-permute-start.3 = (f32[128,128]{1,0:T(8,128)S(1)}, f32[128,128]{1,0:T(8,128)S(1)}, u32[]{:S(2)}, u32[]{:S(2)}) collective-permute-start(f32[128,128]{1,0:T(8,128)S(1)} %get-tuple-element.21), channel_id=1, source_target_pairs={{0,8},{4,12},{8,0},{12,4},{16,24},{20,28},{24,16},{28,20},{1,9},{5... | collective-permute-start | bytes 196616 | tf_op jit(solution)/shard_map/ppermute | solution.py:218
  5.2 5.8 %collective-permute-start.4 = (f32[128,128]{1,0:T(8,128)S(1)}, f32[128,128]{1,0:T(8,128)S(1)}, u32[]{:S(2)}, u32[]{:S(2)}) collective-permute-start(f32[128,128]{1,0:T(8,128)S(1)} %get-tuple-element.22), channel_id=1, source_target_pairs={{0,12},{4,8},{8,4},{12,0},{16,28},{20,24},{24,20},{28,16},{1,13},{... | collective-permute-start | bytes 196616 | tf_op jit(solution)/shard_map/ppermute | solution.py:218
  6.5 7.3 %collective-permute-start.1 = (f32[128,128]{1,0:T(8,128)S(1)}, f32[128,128]{1,0:T(8,128)S(1)}, u32[]{:S(2)}, u32[]{:S(2)}) collective-permute-start(f32[128,128]{1,0:T(8,128)S(1)} %get-tuple-element.20), channel_id=1, source_target_pairs={{0,12},{4,8},{8,4},{12,0},{16,28},{20,24},{24,20},{28,16},{1,13},{... | collective-permute-start | bytes 196616 | tf_op jit(solution)/shard_map/ppermute | solution.py:218
  8.1 5.8 %collective-permute-start.2 = (f32[128,128]{1,0:T(8,128)S(1)}, f32[128,128]{1,0:T(8,128)S(1)}, u32[]{:S(2)}, u32[]{:S(2)}) collective-permute-start(f32[128,128]{1,0:T(8,128)S(1)} %get-tuple-element.20), channel_id=1, source_target_pairs={{0,4},{4,0},{8,12},{12,8},{16,20},{20,16},{24,28},{28,24},{1,5},{5... | collective-permute-start | bytes 196616 | tf_op jit(solution)/shard_map/ppermute | solution.py:218
  9.6 4.3 %collective-permute-start = (f32[128,128]{1,0:T(8,128)S(1)}, f32[128,128]{1,0:T(8,128)S(1)}, u32[]{:S(2)}, u32[]{:S(2)}) collective-permute-start(f32[128,128]{1,0:T(8,128)S(1)} %get-tuple-element.19), channel_id=1, source_target_pairs={{0,8},{4,12},{8,0},{12,4},{16,24},{20,28},{24,16},{28,20},{1,9},{5... | collective-permute-start | bytes 196616 | tf_op jit(solution)/shard_map/ppermute | solution.py:218
  13.8 5.1 %copy-start.2 = (bf16[128,512]{1,0:T(8,128)(2,1)S(1)}, bf16[128,512]{1,0:T(8,128)(2,1)}, u32[]{:S(2)}) copy-start(bf16[128,512]{1,0:T(8,128)(2,1)} %v_ref.3) | copy-start | bytes 393220
  13.8 5.1 %copy-start.3 = (bf16[128,512]{1,0:T(8,128)(2,1)S(1)}, bf16[128,512]{1,0:T(8,128)(2,1)}, u32[]{:S(2)}) copy-start(bf16[128,512]{1,0:T(8,128)(2,1)} %g_ref.3) | copy-start | bytes 393220
  13.9 5.1 %copy-start = (bf16[128,512]{1,0:T(8,128)(2,1)S(1)}, bf16[128,512]{1,0:T(8,128)(2,1)}, u32[]{:S(2)}) copy-start(bf16[128,512]{1,0:T(8,128)(2,1)} %q_ref.3) | copy-start | bytes 393220
  13.9 5.0 %copy-start.1 = (bf16[128,512]{1,0:T(8,128)(2,1)S(1)}, bf16[128,512]{1,0:T(8,128)(2,1)}, u32[]{:S(2)}) copy-start(bf16[128,512]{1,0:T(8,128)(2,1)} %k_ref.3) | copy-start | bytes 393220
  13.9 5.0 %copy-start.4 = (f32[512]{0:T(512)S(1)}, f32[512]{0:T(512)}, u32[]{:S(2)}) copy-start(f32[512]{0:T(512)} %param.9) | copy-start | bytes 6148
  13.9 11.3 %collective-permute-start.6 = (f32[256,128]{1,0:T(8,128)S(1)}, f32[256,128]{1,0:T(8,128)S(1)}, u32[]{:S(2)}, u32[]{:S(2)}) collective-permute-start(f32[256,128]{1,0:T(8,128)S(1)} %pad_maximum_fusion), channel_id=1, source_target_pairs={{0,4},{4,0},{8,12},{12,8},{16,20},{20,16},{24,28},{28,24},{1,5},{5... | collective-permute-start | bytes 393224 | tf_op jit(solution)/shard_map/ppermute | solution.py:218
  14.5 5.8 %collective-permute-start.5 = (f32[128,128]{1,0:T(8,128)S(1)}, f32[128,128]{1,0:T(8,128)S(1)}, u32[]{:S(2)}, u32[]{:S(2)}) collective-permute-start(f32[128,128]{1,0:T(8,128)S(1)} %get-tuple-element.22), channel_id=1, source_target_pairs={{0,4},{4,0},{8,12},{12,8},{16,20},{20,16},{24,28},{28,24},{1,5},{5... | collective-permute-start | bytes 196616 | tf_op jit(solution)/shard_map/ppermute | solution.py:218
  16.0 7.0 %collective-permute-start.7 = (f32[128,128]{1,0:T(8,128)S(1)}, f32[128,128]{1,0:T(8,128)S(1)}, u32[]{:S(2)}, u32[]{:S(2)}) collective-permute-start(f32[128,128]{1,0:T(8,128)S(1)} %get-tuple-element.36), channel_id=1, source_target_pairs={{0,16},{4,20},{8,24},{12,28},{16,0},{20,4},{24,8},{28,12},{1,17},{... | collective-permute-start | bytes 196616 | tf_op jit(solution)/shard_map/ppermute | solution.py:218
  18.6 6.7 %collective-permute-start.8 = (f32[128,128]{1,0:T(8,128)S(1)}, f32[128,128]{1,0:T(8,128)S(1)}, u32[]{:S(2)}, u32[]{:S(2)}) collective-permute-start(f32[128,128]{1,0:T(8,128)S(1)} %get-tuple-element.36), channel_id=1, source_target_pairs={{0,20},{4,16},{8,28},{12,24},{16,4},{20,0},{24,12},{28,8},{1,21},{... | collective-permute-start | bytes 196616 | tf_op jit(solution)/shard_map/ppermute | solution.py:218
  25.6 3.1 %collective-permute-start.9 = (f32[1,128]{1,0:T(1,128)S(1)}, f32[1,128]{1,0:T(1,128)S(1)}, u32[]{:S(2)}, u32[]{:S(2)}) collective-permute-start(f32[1,128]{1,0:T(1,128)S(1)} %get-tuple-element.25.refs_0_), channel_id=1, source_target_pairs={{0,3},{1,2},{2,1},{3,0},{4,7},{5,6},{6,5},{7,4},{8,11},{9,10},{10,... | collective-permute-start | bytes 1544 | tf_op jit(solution)/shard_map/ppermute | solution.py:218
  25.7 3.6 %collective-permute-start.10 = (f32[1,128]{1,0:T(1,128)S(1)}, f32[1,128]{1,0:T(1,128)S(1)}, u32[]{:S(2)}, u32[]{:S(2)}) collective-permute-start(f32[1,128]{1,0:T(1,128)S(1)} %get-tuple-element.25.refs_0_), channel_id=1, source_target_pairs={{0,2},{1,3},{2,0},{3,1},{4,6},{5,7},{6,4},{7,5},{8,10},{9,11},{10,... | collective-permute-start | bytes 1544 | tf_op jit(solution)/shard_map/ppermute | solution.py:218
  27.2 2.1 %collective-permute-start.11 = (f32[1,128]{1,0:T(1,128)S(1)}, f32[1,128]{1,0:T(1,128)S(1)}, u32[]{:S(2)}, u32[]{:S(2)}) collective-permute-start(f32[1,128]{1,0:T(1,128)S(1)} %get-tuple-element.25.refs_0_), channel_id=1, source_target_pairs={{0,1},{1,0},{2,3},{3,2},{4,5},{5,4},{6,7},{7,6},{8,9},{9,8},{10,11... | collective-permute-start | bytes 1544 | tf_op jit(solution)/shard_map/ppermute | solution.py:218

commit v7 on v6

--- a/solution.py
+++ b/solution.py
@@ -107,32 +107,22 @@
             out_ref[rows] = pack_state(dot(left_ref[pair, :, lanes], right_ref[pair, :, lanes], TN))
 
 
-def whole_states(pieces, axis):
-    if len(pieces) == 2:
-        return tuple(lambda t, ref=ref: ref[t * HEAD_DIM : (t + 1) * HEAD_DIM] for ref in pieces)
-    a_sum, a1, b_sum, b1, got, t_mine, t_other = pieces
+def whole_state(pieces, axis, is_qg):
+    if len(pieces) == 1:
+        return lambda t: pieces[0][t * HEAD_DIM : (t + 1) * HEAD_DIM]
+    a_sum, a1, b_sum, b1, t_mine, t_other, got = pieces
     upper, odd = place_on(axis)
-    mid = a_sum.shape[0]
-    count = mid // HEAD_DIM
-
-    def part(t, is_a):
-        start = t % count * HEAD_DIM
-        rows = slice(start, start + HEAD_DIM)
-        if is_a:
-            mine = a_sum[rows] + jnp.where(odd != upper, a1[rows], 0.0)
-            other = got[rows]
-        else:
-            mine = b_sum[rows] + jnp.where(odd == upper, b1[rows], 0.0) + t_mine[rows]
-            other = got[mid + start : mid + start + HEAD_DIM] + t_other[rows]
-        return jnp.where(odd == t // count, mine, other)
-
-    def kv_of(t):
-        return jnp.where(upper == 1, part(t, False), part(t, True))
-
-    def qg_of(t):
-        return jnp.where(upper == 1, part(t, True), part(t, False))
-
-    return kv_of, qg_of
+    is_a = upper == is_qg
+    count = a_sum.shape[0] // HEAD_DIM
+
+    def rows_of(t):
+        rows = slice(t % count * HEAD_DIM, (t % count + 1) * HEAD_DIM)
+        a_own = a_sum[rows] + jnp.where(odd != upper, a1[rows], 0.0)
+        b_own = b_sum[rows] + jnp.where(odd == upper, b1[rows], 0.0) + t_mine[rows]
+        other = got[rows] + jnp.where(is_a, 0.0, t_other[rows])
+        return jnp.where(odd == t // count, jnp.where(is_a, a_own, b_own), other)
+
+    return rows_of
 
 
 def block_kernel(
@@ -162,7 +152,7 @@
 
 def output_kernel(factor, axis, q_ref, part_ref, *refs):
     *pieces, out_ref, squares_ref = refs
-    kv_of, _ = whole_states(pieces, axis)
+    kv_of = whole_state(pieces, axis, 0)
     total = None
     for t in range(tiles(q_ref)):
         cols = slice(t * LANES, (t + 1) * LANES)
@@ -176,7 +166,8 @@
 
 def grads_kernel(factor, axis, k_ref, v_ref, g_ref, dq_part, dk_part, dv_part, *refs):
     *pieces, dq_ref, dk_ref, dv_ref = refs
-    kv_of, qg_of = whole_states(pieces, axis)
+    kv_of = whole_state(pieces[: len(pieces) // 2], axis, 0)
+    qg_of = whole_state(pieces[len(pieces) // 2 :], axis, 1)
     for t in range(tiles(k_ref)):
         cols = slice(t * LANES, (t + 1) * LANES)
         state = unpack_state((factor * kv_of(t)).astype(bf16))
@@ -228,10 +219,9 @@
         position = jnp.arange(count)[:, None, None]
         every_kv = lax.all_gather(kv, axis)
         every_qg = lax.all_gather(qg, axis)
-        return (
-            jnp.sum(jnp.where(position < index, every_kv, 0.0), axis=0),
-            jnp.sum(jnp.where(position > index, every_qg, 0.0), axis=0),
-        )
+        before = jnp.sum(jnp.where(position < index, every_kv, 0.0), axis=0)
+        after = jnp.sum(jnp.where(position > index, every_qg, 0.0), axis=0)
+        return (before,), (after,)
     if count < 8:
         total_kv, total_qg = states()
         before, after = jnp.zeros_like(total_kv), jnp.zeros_like(total_qg)
@@ -242,7 +232,7 @@
             after = after + jnp.where(bit(distance), 0.0, got_qg)
             total_kv, total_qg = total_kv + got_kv, total_qg + got_qg
             distance *= 2
-        return before, after
+        return (before,), (after,)
     upper = bit(top)
     a_enters = lambda d: bit(d) != upper
     b_enters = lambda d: bit(d) == upper
@@ -258,9 +248,11 @@
     b2 = send(b_mine, 2)
     b1 = send(b_other, 1)
     a_pair, b_pair = a2 + a3, b2 + b3
-    a_sum = jnp.where(a_enters(2), a_pair, 0.0)
-    b_sum = jnp.where(b_enters(2), b_pair, 0.0)
-    a_total, b_total = a_mine + a1 + a_pair, b_mine + b1 + b_pair
+    a_in, b_in = lax.optimization_barrier((a_pair, b_pair))
+    a_sum = jnp.where(a_enters(2), a_in, 0.0)
+    b_sum = jnp.where(b_enters(2), b_in, 0.0)
+    a_total = a_mine + a1 + a_pair
+    b_total = b_mine + b1 + b_pair
     distance = 4
     while distance < top:
         a_got, b_got = send(a_total, distance), send(b_total, distance)
@@ -272,8 +264,10 @@
     t_mine = send(a_total, top)
     a_out = a_sum + jnp.where(a_enters(1), 0.0, a_mine)
     b_out = b_sum + jnp.where(b_enters(1), 0.0, b_mine)
-    got = send(jnp.concatenate([a_out, b_out], axis=0), 1)
-    return a_sum, a1, b_sum, b1, got, t_mine, t_other
+    got_kv = send(jnp.where(upper, b_out, a_out), 1)
+    got_qg = send(jnp.where(upper, a_out, b_out), 1)
+    own = (a_sum, a1, b_sum, b1)
+    return (*own, t_mine, t_other, got_kv), (*own, t_mine, t_other, got_qg)
 
 
 def all_shares(row, axis):
@@ -319,7 +313,7 @@
         (*inputs, gain[None]),
         24 * length * LANES * width,
     )
-    pieces = scan_states(
+    kv_pieces, qg_pieces = scan_states(
         "seq",
         lambda: products(states_kernel, [packed] * 2),
         lambda: products(functools.partial(halves_kernel, "seq"), [half] * 4),
@@ -327,14 +321,14 @@
     out, squares = call(
         functools.partial(output_kernel, factor, "seq"),
         [wide, jax.ShapeDtypeStruct((1, length), f32)],
-        (queries, out_part, *pieces),
+        (queries, out_part, *kv_pieces),
         2 * length * LANES * width,
     )
     shares = all_shares(squares, "head")
     dq, dk, dv = call(
         functools.partial(grads_kernel, factor, "seq"),
         [narrow] * 3,
-        (keys, values, d_out, dq_part, dk_part, dv_part, *pieces),
+        (keys, values, d_out, dq_part, dk_part, dv_part, *kv_pieces, *qg_pieces),
         6 * length * LANES * width,
     )
     normed = call(

time: 30.2 us -> 26.3 us (0.87)
  waiting for transfers between devices: 9.42 us -> 4.69 us
  starting transfers between devices: 14.9 us -> 15.6 us
    ppermute x12 -> x13, waiting for transfers between devices: 9.42 us -> 4.69 us  [swap(): return lax.ppermute(x, axis, [(i, i ^ distance) for i in range(size)])]
    ppermute x12 -> x13, starting transfers between devices: 14.9 us -> 15.6 us  [swap(): return lax.ppermute(x, axis, [(i, i ^ distance) for i in range(size)])]
  transfers between devices with their start and end apart: 12 -> 13, of which waited for: 6 -> 4; matrix products, arithmetic and copies ran while one was open for 0% -> 0% of each run, Pallas kernels for 8% -> 11%
where the time goes in v7:
time: 26.3 us; the launch traced here: 26.1 us
  starting transfers between devices  15.6 us (59%)
  Pallas kernels  4.94 us (19%)
  waiting for transfers between devices  4.69 us (18%)
  between operations  0.76 us (3%)
    ppermute x13, starting transfers between devices, swap(): return lax.ppermute(x, axis, [(i, i ^ distance) for i in range(size)])  15.6 us
    pallas_call x5, Pallas kernels, call(): pl.pallas_call(kernel, out_shape=outs[0] if single else tuple(outs), in_s...  4.94 us
    ppermute x13, waiting for transfers between devices, swap(): return lax.ppermute(x, axis, [(i, i ^ distance) for i in range(size)])  4.69 us
  transfers between devices with their start and end apart: 13, of which 4 were waited for; matrix products, arithmetic and copies ran while one was open for 0% of the time, Pallas kernels for 11%

profile of v7, /device:TPU:0, one launch (start us, length us, event | category | flops | bytes accessed | tf_op | source)
XLA Modules:
  0.0 26.1 jit_solution(7772966875285584418)
XLA Ops:
  0.6 1.4 %shard_map.85 = (f32[128,128]{1,0:T(8,128)S(1)}, f32[128,128]{1,0:T(8,128)S(1)}, f32[128,128]{1,0:T(8,128)S(1)}, f32[128,128]{1,0:T(8,128)S(1)}) custom-call(bf16[128,512]{1,0:T(8,128)(2,1)} %q_ref.3, bf16[128,512]{1,0:T(8,128)(2,1)} %k_ref.3, bf16[128,512]{1,0:T(8,128)(2,1)} %v_ref.3, bf16[128,512]{1,0:T(8,128)(2,1)} %g_ref.3), custom_call_target="tpu_custom_call" | custom-call | flops 33554432 | bytes 786432 | tf_op jit(solution)/shard_map/pallas_call | solution.py:196
  2.0 3.0 %collective-permute-start.4 = (f32[128,128]{1,0:T(8,128)S(1)}, f32[128,128]{1,0:T(8,128)S(1)}, u32[]{:S(2)}, u32[]{:S(2)}) collective-permute-start(f32[128,128]{1,0:T(8,128)S(1)} %get-tuple-element.22), channel_id=1, source_target_pairs={{0,4},{4,0},{8,12},{12,8},{16,20},{20,16},{24,28},{28,24},{1,5},{5... | collective-permute-start | bytes 196616 | tf_op jit(solution)/shard_map/ppermute | solution.py:209
  5.1 1.6 %collective-permute-start = (f32[128,128]{1,0:T(8,128)S(1)}, f32[128,128]{1,0:T(8,128)S(1)}, u32[]{:S(2)}, u32[]{:S(2)}) collective-permute-start(f32[128,128]{1,0:T(8,128)S(1)} %get-tuple-element.21), channel_id=1, source_target_pairs={{0,8},{4,12},{8,0},{12,4},{16,24},{20,28},{24,16},{28,20},{1,9},{5... | collective-permute-start | bytes 196616 | tf_op jit(solution)/shard_map/ppermute | solution.py:209
  6.6 0.0 collective-permute-start.1
  6.6 2.9 %collective-permute-start.3 = (f32[128,128]{1,0:T(8,128)S(1)}, f32[128,128]{1,0:T(8,128)S(1)}, u32[]{:S(2)}, u32[]{:S(2)}) collective-permute-start(f32[128,128]{1,0:T(8,128)S(1)} %get-tuple-element.24), channel_id=1, source_target_pairs={{0,12},{4,8},{8,4},{12,0},{16,28},{20,24},{24,20},{28,16},{1,13},{... | collective-permute-start | bytes 196616 | tf_op jit(solution)/shard_map/ppermute | solution.py:209
  9.6 0.5 %collective-permute-start.5 = (f32[128,128]{1,0:T(8,128)S(1)}, f32[128,128]{1,0:T(8,128)S(1)}, u32[]{:S(2)}, u32[]{:S(2)}) collective-permute-start(f32[128,128]{1,0:T(8,128)S(1)} %get-tuple-element.24), channel_id=1, source_target_pairs={{0,4},{4,0},{8,12},{12,8},{16,20},{20,16},{24,28},{28,24},{1,5},{5... | collective-permute-start | bytes 196616 | tf_op jit(solution)/shard_map/ppermute | solution.py:209
  10.1 0.0 collective-permute-done.4.refs_1_.refs_8_
  10.1 0.1 collective-permute-start.2
  10.2 0.0 collective-permute-done
  10.2 1.7 %collective-permute-done.1 = f32[128,128]{1,0:T(8,128)S(1)} collective-permute-done((f32[128,128]{1,0:T(8,128)S(1)}, f32[128,128]{1,0:T(8,128)S(1)}, u32[]{:S(2)}, u32[]{:S(2)}) %collective-permute-start.1) | collective-permute-done | bytes 65568 | tf_op jit(solution)/shard_map/ppermute | solution.py:209
  11.9 2.7 %collective-permute-start.6 = (f32[128,128]{1,0:T(8,128)S(1)}, f32[128,128]{1,0:T(8,128)S(1)}, u32[]{:S(2)}, u32[]{:S(2)}) collective-permute-start(f32[128,128]{1,0:T(8,128)S(1)} %get-tuple-element.39), channel_id=1, source_target_pairs={{0,16},{4,20},{8,24},{12,28},{16,0},{20,4},{24,8},{28,12},{1,17},{... | collective-permute-start | bytes 196616 | tf_op jit(solution)/shard_map/ppermute | solution.py:209
  14.6 0.9 %collective-permute-start.7 = (f32[128,128]{1,0:T(8,128)S(1)}, f32[128,128]{1,0:T(8,128)S(1)}, u32[]{:S(2)}, u32[]{:S(2)}) collective-permute-start(f32[128,128]{1,0:T(8,128)S(1)} %get-tuple-element.39), channel_id=1, source_target_pairs={{0,20},{4,16},{8,28},{12,24},{16,4},{20,0},{24,12},{28,8},{1,21},{... | collective-permute-start | bytes 196616 | tf_op jit(solution)/shard_map/ppermute | solution.py:209
  15.4 0.0 collective-permute-done.2
  15.4 0.0 collective-permute-done.3
  15.5 0.0 copy-start.2
  15.5 0.0 copy-start.3
  15.5 0.0 copy-start
  15.5 0.0 copy-start.1
  15.6 0.0 copy-start.4
  15.6 1.0 %collective-permute-start.8 = (f32[128,128]{1,0:T(8,128)S(1)}, f32[128,128]{1,0:T(8,128)S(1)}, u32[]{:S(2)}, u32[]{:S(2)}) collective-permute-start(f32[128,128]{1,0:T(8,128)S(1)} %broadcast_select_fusion.3), channel_id=1, source_target_pairs={{0,4},{4,0},{8,12},{12,8},{16,20},{20,16},{24,28},{28,24},{1,5},{5... | collective-permute-start | bytes 196616 | tf_op jit(solution)/shard_map/ppermute | solution.py:209
  16.6 1.1 %collective-permute-start.12 = (f32[128,128]{1,0:T(8,128)S(1)}, f32[128,128]{1,0:T(8,128)S(1)}, u32[]{:S(2)}, u32[]{:S(2)}) collective-permute-start(f32[128,128]{1,0:T(8,128)S(1)} %get-tuple-element.36), channel_id=1, source_target_pairs={{0,4},{4,0},{8,12},{12,8},{16,20},{20,16},{24,28},{28,24},{1,5},{5... | collective-permute-start | bytes 196616 | tf_op jit(solution)/shard_map/ppermute | solution.py:209
  17.7 0.0 copy-done.2
  17.7 0.0 copy-done.3
  17.7 0.0 copy-done
  17.7 0.0 copy-done.1
  17.7 0.0 copy-done.4
  17.7 1.4 %shard_map.84 = (f32[128,512]{1,0:T(8,128)S(1)}, f32[128,512]{1,0:T(8,128)S(1)}, f32[128,512]{1,0:T(8,128)S(1)}, f32[128,512]{1,0:T(8,128)S(1)}, f32[1,512]{1,0:T(1,128)S(1)}) custom-call(bf16[128,512]{1,0:T(8,128)(2,1)S(1)} %copy-done.3, bf16[128,512]{1,0:T(8,128)(2,1)S(1)} %copy-done, bf16[128,512]{1,0:T(8,128)(2,1)S(1)} %copy-done.1, ...), custom_call_target="tpu_custom_call" | custom-call | flops 201326592 | bytes 1576960 | tf_op jit(solution)/shard_map/pallas_call | solution.py:196
  19.1 0.0 collective-permute-done.5.refs_3_.refs_10_
  19.1 0.0 collective-permute-done.6.refs_4_.refs_11_
  19.1 2.2 %collective-permute-done.7.refs_5_.refs_12_ = f32[128,128]{1,0:T(8,128)S(1)} collective-permute-done((f32[128,128]{1,0:T(8,128)S(1)}, f32[128,128]{1,0:T(8,128)S(1)}, u32[]{:S(2)}, u32[]{:S(2)}) %collective-permute-start.7) | collective-permute-done | bytes 65568 | tf_op jit(solution)/shard_map/ppermute | solution.py:209
  21.3 0.0 collective-permute-done.8.refs_6_
  21.4 0.3 %shard_map.86 = (f32[128,512]{1,0:T(8,128)S(1)}, f32[1,128]{1,0:T(1,128)S(1)}) custom-call(bf16[128,512]{1,0:T(8,128)(2,1)S(1)} %copy-done.3, f32[128,512]{1,0:T(8,128)S(1)} %get-tuple-element.20.part_ref, f32[128,128]{1,0:T(8,128)S(1)} %get-tuple-element.38.refs_0_.refs_7_, f32[128,128]{1,0:T(8,128)S(1)} %collective-permute-done.4.refs_1_.refs_8_, ...), custom_call_target="tpu_custom_call" | custom-call | flops 16777216 | bytes 1114624 | tf_op jit(solution)/shard_map/pallas_call | solution.py:196
  21.7 0.1 collective-permute-start.9
  21.7 1.6 %collective-permute-start.10 = (f32[1,128]{1,0:T(1,128)S(1)}, f32[1,128]{1,0:T(1,128)S(1)}, u32[]{:S(2)}, u32[]{:S(2)}) collective-permute-start(f32[1,128]{1,0:T(1,128)S(1)} %get-tuple-element.29.refs_0_), channel_id=1, source_target_pairs={{0,2},{1,3},{2,0},{3,1},{4,6},{5,7},{6,4},{7,5},{8,10},{9,11},{10,... | collective-permute-start | bytes 1544 | tf_op jit(solution)/shard_map/ppermute | solution.py:209
  23.3 0.3 %collective-permute-start.11 = (f32[1,128]{1,0:T(1,128)S(1)}, f32[1,128]{1,0:T(1,128)S(1)}, u32[]{:S(2)}, u32[]{:S(2)}) collective-permute-start(f32[1,128]{1,0:T(1,128)S(1)} %get-tuple-element.29.refs_0_), channel_id=1, source_target_pairs={{0,1},{1,0},{2,3},{3,2},{4,5},{5,4},{6,7},{7,6},{8,9},{9,8},{10,11... | collective-permute-start | bytes 1544 | tf_op jit(solution)/shard_map/ppermute | solution.py:209
  23.6 0.0 collective-permute-done.12.refs_13_
  23.6 1.1 %shard_map.88 = (bf16[128,512]{1,0:T(8,128)(2,1)}, bf16[128,512]{1,0:T(8,128)(2,1)}, bf16[128,512]{1,0:T(8,128)(2,1)}) custom-call(bf16[128,512]{1,0:T(8,128)(2,1)S(1)} %copy-done, bf16[128,512]{1,0:T(8,128)(2,1)S(1)} %copy-done.1, bf16[128,512]{1,0:T(8,128)(2,1)S(1)} %copy-done.2, f32[128,512]{1,0:T(8,128)S(1)} %get-tuple-element.30.dq_part, ...), custom_call_target="tpu_custom_call" | custom-call | flops 50331648 | bytes 2490368 | tf_op jit(solution)/shard_map/pallas_call | solution.py:196
  24.7 0.1 collective-permute-done.9.refs_1_
  24.7 0.7 %collective-permute-done.10.refs_2_ = f32[1,128]{1,0:T(1,128)S(1)} collective-permute-done((f32[1,128]{1,0:T(1,128)S(1)}, f32[1,128]{1,0:T(1,128)S(1)}, u32[]{:S(2)}, u32[]{:S(2)}) %collective-permute-start.10) | collective-permute-done | bytes 544 | tf_op jit(solution)/shard_map/ppermute | solution.py:209
  25.4 0.0 collective-permute-done.11.refs_3_
  25.4 0.8 %shard_map.87 = bf16[128,512]{1,0:T(8,128)(2,1)} custom-call(f32[128,512]{1,0:T(8,128)S(1)} %get-tuple-element.27.out_ref, f32[1,512]{1,0:T(1,128)S(1)} %get-tuple-element.28.gain_ref, f32[1,128]{1,0:T(1,128)S(1)} %get-tuple-element.29.refs_0_, f32[1,128]{1,0:T(1,128)S(1)} %collective-permute-done.9.refs_1_, f32[1,128]{1,0:T(1,128)S(1)} %collective-permute-done.10.refs_2_, ...), custom_call_target="tpu_custom_call" | custom-call | flops 131072 | bytes 397312 | tf_op jit(solution)/shard_map/pallas_call | solution.py:196
  (4 shorter events, 0.1 us)
Async XLA Ops:
  2.0 8.1 %collective-permute-start.4 = (f32[128,128]{1,0:T(8,128)S(1)}, f32[128,128]{1,0:T(8,128)S(1)}, u32[]{:S(2)}, u32[]{:S(2)}) collective-permute-start(f32[128,128]{1,0:T(8,128)S(1)} %get-tuple-element.22), channel_id=1, source_target_pairs={{0,4},{4,0},{8,12},{12,8},{16,20},{20,16},{24,28},{28,24},{1,5},{5... | collective-permute-start | bytes 196616 | tf_op jit(solution)/shard_map/ppermute | solution.py:209
  5.1 5.1 %collective-permute-start = (f32[128,128]{1,0:T(8,128)S(1)}, f32[128,128]{1,0:T(8,128)S(1)}, u32[]{:S(2)}, u32[]{:S(2)}) collective-permute-start(f32[128,128]{1,0:T(8,128)S(1)} %get-tuple-element.21), channel_id=1, source_target_pairs={{0,8},{4,12},{8,0},{12,4},{16,24},{20,28},{24,16},{28,20},{1,9},{5... | collective-permute-start | bytes 196616 | tf_op jit(solution)/shard_map/ppermute | solution.py:209
  6.6 5.3 %collective-permute-start.1 = (f32[128,128]{1,0:T(8,128)S(1)}, f32[128,128]{1,0:T(8,128)S(1)}, u32[]{:S(2)}, u32[]{:S(2)}) collective-permute-start(f32[128,128]{1,0:T(8,128)S(1)} %get-tuple-element.22), channel_id=1, source_target_pairs={{0,12},{4,8},{8,4},{12,0},{16,28},{20,24},{24,20},{28,16},{1,13},{... | collective-permute-start | bytes 196616 | tf_op jit(solution)/shard_map/ppermute | solution.py:209
  6.6 8.8 %collective-permute-start.3 = (f32[128,128]{1,0:T(8,128)S(1)}, f32[128,128]{1,0:T(8,128)S(1)}, u32[]{:S(2)}, u32[]{:S(2)}) collective-permute-start(f32[128,128]{1,0:T(8,128)S(1)} %get-tuple-element.24), channel_id=1, source_target_pairs={{0,12},{4,8},{8,4},{12,0},{16,28},{20,24},{24,20},{28,16},{1,13},{... | collective-permute-start | bytes 196616 | tf_op jit(solution)/shard_map/ppermute | solution.py:209
  9.6 9.6 %collective-permute-start.5 = (f32[128,128]{1,0:T(8,128)S(1)}, f32[128,128]{1,0:T(8,128)S(1)}, u32[]{:S(2)}, u32[]{:S(2)}) collective-permute-start(f32[128,128]{1,0:T(8,128)S(1)} %get-tuple-element.24), channel_id=1, source_target_pairs={{0,4},{4,0},{8,12},{12,8},{16,20},{20,16},{24,28},{28,24},{1,5},{5... | collective-permute-start | bytes 196616 | tf_op jit(solution)/shard_map/ppermute | solution.py:209
  10.1 5.3 %collective-permute-start.2 = (f32[128,128]{1,0:T(8,128)S(1)}, f32[128,128]{1,0:T(8,128)S(1)}, u32[]{:S(2)}, u32[]{:S(2)}) collective-permute-start(f32[128,128]{1,0:T(8,128)S(1)} %get-tuple-element.23), channel_id=1, source_target_pairs={{0,8},{4,12},{8,0},{12,4},{16,24},{20,28},{24,16},{28,20},{1,9},{5... | collective-permute-start | bytes 196616 | tf_op jit(solution)/shard_map/ppermute | solution.py:209
  11.9 7.2 %collective-permute-start.6 = (f32[128,128]{1,0:T(8,128)S(1)}, f32[128,128]{1,0:T(8,128)S(1)}, u32[]{:S(2)}, u32[]{:S(2)}) collective-permute-start(f32[128,128]{1,0:T(8,128)S(1)} %get-tuple-element.39), channel_id=1, source_target_pairs={{0,16},{4,20},{8,24},{12,28},{16,0},{20,4},{24,8},{28,12},{1,17},{... | collective-permute-start | bytes 196616 | tf_op jit(solution)/shard_map/ppermute | solution.py:209
  14.6 6.8 %collective-permute-start.7 = (f32[128,128]{1,0:T(8,128)S(1)}, f32[128,128]{1,0:T(8,128)S(1)}, u32[]{:S(2)}, u32[]{:S(2)}) collective-permute-start(f32[128,128]{1,0:T(8,128)S(1)} %get-tuple-element.39), channel_id=1, source_target_pairs={{0,20},{4,16},{8,28},{12,24},{16,4},{20,0},{24,12},{28,8},{1,21},{... | collective-permute-start | bytes 196616 | tf_op jit(solution)/shard_map/ppermute | solution.py:209
  15.5 2.2 %copy-start.2 = (bf16[128,512]{1,0:T(8,128)(2,1)S(1)}, bf16[128,512]{1,0:T(8,128)(2,1)}, u32[]{:S(2)}) copy-start(bf16[128,512]{1,0:T(8,128)(2,1)} %g_ref.3) | copy-start | bytes 393220
  15.5 2.2 %copy-start.3 = (bf16[128,512]{1,0:T(8,128)(2,1)S(1)}, bf16[128,512]{1,0:T(8,128)(2,1)}, u32[]{:S(2)}) copy-start(bf16[128,512]{1,0:T(8,128)(2,1)} %q_ref.3) | copy-start | bytes 393220
  15.5 2.2 %copy-start = (bf16[128,512]{1,0:T(8,128)(2,1)S(1)}, bf16[128,512]{1,0:T(8,128)(2,1)}, u32[]{:S(2)}) copy-start(bf16[128,512]{1,0:T(8,128)(2,1)} %k_ref.3) | copy-start | bytes 393220
  15.5 2.2 %copy-start.1 = (bf16[128,512]{1,0:T(8,128)(2,1)S(1)}, bf16[128,512]{1,0:T(8,128)(2,1)}, u32[]{:S(2)}) copy-start(bf16[128,512]{1,0:T(8,128)(2,1)} %v_ref.3) | copy-start | bytes 393220
  15.6 2.1 %copy-start.4 = (f32[512]{0:T(512)S(1)}, f32[512]{0:T(512)}, u32[]{:S(2)}) copy-start(f32[512]{0:T(512)} %param.9) | copy-start | bytes 6148
  15.6 5.8 %collective-permute-start.8 = (f32[128,128]{1,0:T(8,128)S(1)}, f32[128,128]{1,0:T(8,128)S(1)}, u32[]{:S(2)}, u32[]{:S(2)}) collective-permute-start(f32[128,128]{1,0:T(8,128)S(1)} %broadcast_select_fusion.3), channel_id=1, source_target_pairs={{0,4},{4,0},{8,12},{12,8},{16,20},{20,16},{24,28},{28,24},{1,5},{5... | collective-permute-start | bytes 196616 | tf_op jit(solution)/shard_map/ppermute | solution.py:209
  16.6 7.0 %collective-permute-start.12 = (f32[128,128]{1,0:T(8,128)S(1)}, f32[128,128]{1,0:T(8,128)S(1)}, u32[]{:S(2)}, u32[]{:S(2)}) collective-permute-start(f32[128,128]{1,0:T(8,128)S(1)} %get-tuple-element.36), channel_id=1, source_target_pairs={{0,4},{4,0},{8,12},{12,8},{16,20},{20,16},{24,28},{28,24},{1,5},{5... | collective-permute-start | bytes 196616 | tf_op jit(solution)/shard_map/ppermute | solution.py:209
  21.7 3.1 %collective-permute-start.9 = (f32[1,128]{1,0:T(1,128)S(1)}, f32[1,128]{1,0:T(1,128)S(1)}, u32[]{:S(2)}, u32[]{:S(2)}) collective-permute-start(f32[1,128]{1,0:T(1,128)S(1)} %get-tuple-element.29.refs_0_), channel_id=1, source_target_pairs={{0,3},{1,2},{2,1},{3,0},{4,7},{5,6},{6,5},{7,4},{8,11},{9,10},{10,... | collective-permute-start | bytes 1544 | tf_op jit(solution)/shard_map/ppermute | solution.py:209
  21.7 3.6 %collective-permute-start.10 = (f32[1,128]{1,0:T(1,128)S(1)}, f32[1,128]{1,0:T(1,128)S(1)}, u32[]{:S(2)}, u32[]{:S(2)}) collective-permute-start(f32[1,128]{1,0:T(1,128)S(1)} %get-tuple-element.29.refs_0_), channel_id=1, source_target_pairs={{0,2},{1,3},{2,0},{3,1},{4,6},{5,7},{6,4},{7,5},{8,10},{9,11},{10,... | collective-permute-start | bytes 1544 | tf_op jit(solution)/shard_map/ppermute | solution.py:209
  23.3 2.1 %collective-permute-start.11 = (f32[1,128]{1,0:T(1,128)S(1)}, f32[1,128]{1,0:T(1,128)S(1)}, u32[]{:S(2)}, u32[]{:S(2)}) collective-permute-start(f32[1,128]{1,0:T(1,128)S(1)} %get-tuple-element.29.refs_0_), channel_id=1, source_target_pairs={{0,1},{1,0},{2,3},{3,2},{4,5},{5,4},{6,7},{7,6},{8,9},{9,8},{10,11... | collective-permute-start | bytes 1544 | tf_op jit(solution)/shard_map/ppermute | solution.py:209

commit v8 on v7

--- a/solution.py
+++ b/solution.py
@@ -113,13 +113,16 @@
     a_sum, a1, b_sum, b1, t_mine, t_other, got = pieces
     upper, odd = place_on(axis)
     is_a = upper == is_qg
+    swapped = lax.axis_index("head") % 2 == 1
     count = a_sum.shape[0] // HEAD_DIM
 
     def rows_of(t):
         rows = slice(t % count * HEAD_DIM, (t % count + 1) * HEAD_DIM)
         a_own = a_sum[rows] + jnp.where(odd != upper, a1[rows], 0.0)
-        b_own = b_sum[rows] + jnp.where(odd == upper, b1[rows], 0.0) + t_mine[rows]
-        other = got[rows] + jnp.where(is_a, 0.0, t_other[rows])
+        b_own = b_sum[rows] + jnp.where(odd == upper, b1[rows], 0.0)
+        b_own = b_own + jnp.where(swapped, t_other[rows], t_mine[rows])
+        t_rows = jnp.where(swapped, t_mine[rows], t_other[rows])
+        other = got[rows] + jnp.where(is_a, 0.0, t_rows)
         return jnp.where(odd == t // count, jnp.where(is_a, a_own, b_own), other)
 
     return rows_of
@@ -240,6 +243,13 @@
     def send(x, distance):
         return swap(x, axis, distance)
 
+    def send_by_core(x, distances):
+        heads = lax.axis_size("head")
+        pairs = [
+            (i * heads + h, (i ^ distances[h % 2]) * heads + h) for i in range(count) for h in range(heads)
+        ]
+        return lax.ppermute(x, (axis, "head"), pairs)
+
     a_mine, a_other, b_mine, b_other = halves()
     a3 = send(a_other, 3)
     a2 = send(a_mine, 2)
@@ -260,8 +270,8 @@
         b_sum = b_sum + jnp.where(b_enters(distance), b_got, 0.0)
         a_total, b_total = a_total + a_got, b_total + b_got
         distance *= 2
-    t_other = send(a_total, top | 1)
-    t_mine = send(a_total, top)
+    t_other = send_by_core(a_total, (top | 1, top))
+    t_mine = send_by_core(a_total, (top, top | 1))
     a_out = a_sum + jnp.where(a_enters(1), 0.0, a_mine)
     b_out = b_sum + jnp.where(b_enters(1), 0.0, b_mine)
     got_kv = send(jnp.where(upper, b_out, a_out), 1)

time: 26.3 us -> 26.3 us (level)
    ppermute x13 -> x11, starting transfers between devices: 15.6 us -> 12.1 us  [swap(): return lax.ppermute(x, axis, [(i, i ^ distance) for i in range(size)])]
    ppermute x0 -> x2, starting transfers between devices: none -> 3.51 us  [send_by_core(): return lax.ppermute(x, (axis, 'head'), pairs)]
    ppermute x13 -> x11, waiting for transfers between devices: 4.69 us -> 2.47 us  [swap(): return lax.ppermute(x, axis, [(i, i ^ distance) for i in range(size)])]
    ppermute x0 -> x2, waiting for transfers between devices: none -> 2.21 us  [send_by_core(): return lax.ppermute(x, (axis, 'head'), pairs)]
where the time goes in v8:
time: 26.3 us; the launch traced here: 26.1 us
  starting transfers between devices  15.6 us (59%)
  Pallas kernels  4.95 us (19%)
  waiting for transfers between devices  4.68 us (18%)
  between operations  0.76 us (3%)
    ppermute x11, starting transfers between devices, swap(): return lax.ppermute(x, axis, [(i, i ^ distance) for i in range(size)])  12.1 us
    pallas_call x5, Pallas kernels, call(): pl.pallas_call(kernel, out_shape=outs[0] if single else tuple(outs), in_s...  4.95 us
    ppermute x2, starting transfers between devices, send_by_core(): return lax.ppermute(x, (axis, 'head'), pairs)  3.51 us
    ppermute x11, waiting for transfers between devices, swap(): return lax.ppermute(x, axis, [(i, i ^ distance) for i in range(size)])  2.47 us
    ppermute x2, waiting for transfers between devices, send_by_core(): return lax.ppermute(x, (axis, 'head'), pairs)  2.21 us
  transfers between devices with their start and end apart: 13, of which 4 were waited for; matrix products, arithmetic and copies ran while one was open for 0% of the time, Pallas kernels for 11%

profile of v8, /device:TPU:0, one launch (start us, length us, event | category | flops | bytes accessed | tf_op | source)
XLA Modules:
  0.0 26.1 jit_solution(10785781339982246253)
XLA Ops:
  0.6 1.4 %shard_map.85 = (f32[128,128]{1,0:T(8,128)S(1)}, f32[128,128]{1,0:T(8,128)S(1)}, f32[128,128]{1,0:T(8,128)S(1)}, f32[128,128]{1,0:T(8,128)S(1)}) custom-call(bf16[128,512]{1,0:T(8,128)(2,1)} %q_ref.3, bf16[128,512]{1,0:T(8,128)(2,1)} %k_ref.3, bf16[128,512]{1,0:T(8,128)(2,1)} %v_ref.3, bf16[128,512]{1,0:T(8,128)(2,1)} %g_ref.3), custom_call_target="tpu_custom_call" | custom-call | flops 33554432 | bytes 786432 | tf_op jit(solution)/shard_map/pallas_call | solution.py:199
  2.0 3.0 %collective-permute-start.4 = (f32[128,128]{1,0:T(8,128)S(1)}, f32[128,128]{1,0:T(8,128)S(1)}, u32[]{:S(2)}, u32[]{:S(2)}) collective-permute-start(f32[128,128]{1,0:T(8,128)S(1)} %get-tuple-element.22), channel_id=1, source_target_pairs={{0,4},{4,0},{8,12},{12,8},{16,20},{20,16},{24,28},{28,24},{1,5},{5... | collective-permute-start | bytes 196616 | tf_op jit(solution)/shard_map/ppermute | solution.py:212
  5.1 1.6 %collective-permute-start = (f32[128,128]{1,0:T(8,128)S(1)}, f32[128,128]{1,0:T(8,128)S(1)}, u32[]{:S(2)}, u32[]{:S(2)}) collective-permute-start(f32[128,128]{1,0:T(8,128)S(1)} %get-tuple-element.21), channel_id=1, source_target_pairs={{0,8},{4,12},{8,0},{12,4},{16,24},{20,28},{24,16},{28,20},{1,9},{5... | collective-permute-start | bytes 196616 | tf_op jit(solution)/shard_map/ppermute | solution.py:212
  6.6 0.0 collective-permute-start.1
  6.6 2.9 %collective-permute-start.3 = (f32[128,128]{1,0:T(8,128)S(1)}, f32[128,128]{1,0:T(8,128)S(1)}, u32[]{:S(2)}, u32[]{:S(2)}) collective-permute-start(f32[128,128]{1,0:T(8,128)S(1)} %get-tuple-element.24), channel_id=1, source_target_pairs={{0,12},{4,8},{8,4},{12,0},{16,28},{20,24},{24,20},{28,16},{1,13},{... | collective-permute-start | bytes 196616 | tf_op jit(solution)/shard_map/ppermute | solution.py:212
  9.6 0.5 %collective-permute-start.5 = (f32[128,128]{1,0:T(8,128)S(1)}, f32[128,128]{1,0:T(8,128)S(1)}, u32[]{:S(2)}, u32[]{:S(2)}) collective-permute-start(f32[128,128]{1,0:T(8,128)S(1)} %get-tuple-element.24), channel_id=1, source_target_pairs={{0,4},{4,0},{8,12},{12,8},{16,20},{20,16},{24,28},{28,24},{1,5},{5... | collective-permute-start | bytes 196616 | tf_op jit(solution)/shard_map/ppermute | solution.py:212
  10.1 0.0 collective-permute-done.4.refs_1_.refs_8_
  10.1 0.1 collective-permute-start.2
  10.2 0.0 collective-permute-done
  10.2 1.7 %collective-permute-done.1 = f32[128,128]{1,0:T(8,128)S(1)} collective-permute-done((f32[128,128]{1,0:T(8,128)S(1)}, f32[128,128]{1,0:T(8,128)S(1)}, u32[]{:S(2)}, u32[]{:S(2)}) %collective-permute-start.1) | collective-permute-done | bytes 65568 | tf_op jit(solution)/shard_map/ppermute | solution.py:212
  11.9 2.7 %collective-permute-start.6 = (f32[128,128]{1,0:T(8,128)S(1)}, f32[128,128]{1,0:T(8,128)S(1)}, u32[]{:S(2)}, u32[]{:S(2)}) collective-permute-start(f32[128,128]{1,0:T(8,128)S(1)} %get-tuple-element.39), channel_id=1, source_target_pairs={{0,16},{1,21},{2,18},{3,23},{4,20},{5,17},{6,22},{7,19},{8,24},{9,... | collective-permute-start | bytes 196616 | tf_op jit(solution)/shard_map/ppermute | solution.py:251
  14.6 0.9 %collective-permute-start.7 = (f32[128,128]{1,0:T(8,128)S(1)}, f32[128,128]{1,0:T(8,128)S(1)}, u32[]{:S(2)}, u32[]{:S(2)}) collective-permute-start(f32[128,128]{1,0:T(8,128)S(1)} %get-tuple-element.39), channel_id=1, source_target_pairs={{0,20},{1,17},{2,22},{3,19},{4,16},{5,21},{6,18},{7,23},{8,28},{9,... | collective-permute-start | bytes 196616 | tf_op jit(solution)/shard_map/ppermute | solution.py:251
  15.4 0.0 collective-permute-done.2
  15.4 0.0 collective-permute-done.3
  15.5 0.0 copy-start.2
  15.5 0.0 copy-start.3
  15.5 0.0 copy-start
  15.5 0.0 copy-start.1
  15.6 0.0 copy-start.4
  15.6 1.0 %collective-permute-start.8 = (f32[128,128]{1,0:T(8,128)S(1)}, f32[128,128]{1,0:T(8,128)S(1)}, u32[]{:S(2)}, u32[]{:S(2)}) collective-permute-start(f32[128,128]{1,0:T(8,128)S(1)} %broadcast_select_fusion.3), channel_id=1, source_target_pairs={{0,4},{4,0},{8,12},{12,8},{16,20},{20,16},{24,28},{28,24},{1,5},{5... | collective-permute-start | bytes 196616 | tf_op jit(solution)/shard_map/ppermute | solution.py:212
  16.6 1.1 %collective-permute-start.12 = (f32[128,128]{1,0:T(8,128)S(1)}, f32[128,128]{1,0:T(8,128)S(1)}, u32[]{:S(2)}, u32[]{:S(2)}) collective-permute-start(f32[128,128]{1,0:T(8,128)S(1)} %get-tuple-element.36), channel_id=1, source_target_pairs={{0,4},{4,0},{8,12},{12,8},{16,20},{20,16},{24,28},{28,24},{1,5},{5... | collective-permute-start | bytes 196616 | tf_op jit(solution)/shard_map/ppermute | solution.py:212
  17.7 0.0 copy-done.2
  17.7 0.0 copy-done.3
  17.7 0.0 copy-done
  17.7 0.0 copy-done.1
  17.7 0.0 copy-done.4
  17.7 1.4 %shard_map.84 = (f32[128,512]{1,0:T(8,128)S(1)}, f32[128,512]{1,0:T(8,128)S(1)}, f32[128,512]{1,0:T(8,128)S(1)}, f32[128,512]{1,0:T(8,128)S(1)}, f32[1,512]{1,0:T(1,128)S(1)}) custom-call(bf16[128,512]{1,0:T(8,128)(2,1)S(1)} %copy-done.3, bf16[128,512]{1,0:T(8,128)(2,1)S(1)} %copy-done, bf16[128,512]{1,0:T(8,128)(2,1)S(1)} %copy-done.1, ...), custom_call_target="tpu_custom_call" | custom-call | flops 201326592 | bytes 1576960 | tf_op jit(solution)/shard_map/pallas_call | solution.py:199
  19.1 0.0 collective-permute-done.5.refs_3_.refs_10_
  19.1 0.0 collective-permute-done.6.refs_4_.refs_11_
  19.1 2.2 %collective-permute-done.7.refs_5_.refs_12_ = f32[128,128]{1,0:T(8,128)S(1)} collective-permute-done((f32[128,128]{1,0:T(8,128)S(1)}, f32[128,128]{1,0:T(8,128)S(1)}, u32[]{:S(2)}, u32[]{:S(2)}) %collective-permute-start.7) | collective-permute-done | bytes 65568 | tf_op jit(solution)/shard_map/ppermute | solution.py:251
  21.3 0.0 collective-permute-done.8.refs_6_
  21.4 0.3 %shard_map.86 = (f32[128,512]{1,0:T(8,128)S(1)}, f32[1,128]{1,0:T(1,128)S(1)}) custom-call(bf16[128,512]{1,0:T(8,128)(2,1)S(1)} %copy-done.3, f32[128,512]{1,0:T(8,128)S(1)} %get-tuple-element.20.part_ref, f32[128,128]{1,0:T(8,128)S(1)} %get-tuple-element.38.refs_0_.refs_7_, f32[128,128]{1,0:T(8,128)S(1)} %collective-permute-done.4.refs_1_.refs_8_, ...), custom_call_target="tpu_custom_call" | custom-call | flops 16777216 | bytes 1114624 | tf_op jit(solution)/shard_map/pallas_call | solution.py:199
  21.7 0.1 collective-permute-start.9
  21.7 1.6 %collective-permute-start.10 = (f32[1,128]{1,0:T(1,128)S(1)}, f32[1,128]{1,0:T(1,128)S(1)}, u32[]{:S(2)}, u32[]{:S(2)}) collective-permute-start(f32[1,128]{1,0:T(1,128)S(1)} %get-tuple-element.29.refs_0_), channel_id=1, source_target_pairs={{0,2},{1,3},{2,0},{3,1},{4,6},{5,7},{6,4},{7,5},{8,10},{9,11},{10,... | collective-permute-start | bytes 1544 | tf_op jit(solution)/shard_map/ppermute | solution.py:212
  23.3 0.3 %collective-permute-start.11 = (f32[1,128]{1,0:T(1,128)S(1)}, f32[1,128]{1,0:T(1,128)S(1)}, u32[]{:S(2)}, u32[]{:S(2)}) collective-permute-start(f32[1,128]{1,0:T(1,128)S(1)} %get-tuple-element.29.refs_0_), channel_id=1, source_target_pairs={{0,1},{1,0},{2,3},{3,2},{4,5},{5,4},{6,7},{7,6},{8,9},{9,8},{10,11... | collective-permute-start | bytes 1544 | tf_op jit(solution)/shard_map/ppermute | solution.py:212
  23.6 0.0 collective-permute-done.12.refs_13_
  23.6 1.1 %shard_map.88 = (bf16[128,512]{1,0:T(8,128)(2,1)}, bf16[128,512]{1,0:T(8,128)(2,1)}, bf16[128,512]{1,0:T(8,128)(2,1)}) custom-call(bf16[128,512]{1,0:T(8,128)(2,1)S(1)} %copy-done, bf16[128,512]{1,0:T(8,128)(2,1)S(1)} %copy-done.1, bf16[128,512]{1,0:T(8,128)(2,1)S(1)} %copy-done.2, f32[128,512]{1,0:T(8,128)S(1)} %get-tuple-element.30.dq_part, ...), custom_call_target="tpu_custom_call" | custom-call | flops 50331648 | bytes 2490368 | tf_op jit(solution)/shard_map/pallas_call | solution.py:199
  24.7 0.1 collective-permute-done.9.refs_1_
  24.7 0.7 %collective-permute-done.10.refs_2_ = f32[1,128]{1,0:T(1,128)S(1)} collective-permute-done((f32[1,128]{1,0:T(1,128)S(1)}, f32[1,128]{1,0:T(1,128)S(1)}, u32[]{:S(2)}, u32[]{:S(2)}) %collective-permute-start.10) | collective-permute-done | bytes 544 | tf_op jit(solution)/shard_map/ppermute | solution.py:212
  25.4 0.0 collective-permute-done.11.refs_3_
  25.4 0.8 %shard_map.87 = bf16[128,512]{1,0:T(8,128)(2,1)} custom-call(f32[128,512]{1,0:T(8,128)S(1)} %get-tuple-element.27.out_ref, f32[1,512]{1,0:T(1,128)S(1)} %get-tuple-element.28.gain_ref, f32[1,128]{1,0:T(1,128)S(1)} %get-tuple-element.29.refs_0_, f32[1,128]{1,0:T(1,128)S(1)} %collective-permute-done.9.refs_1_, f32[1,128]{1,0:T(1,128)S(1)} %collective-permute-done.10.refs_2_, ...), custom_call_target="tpu_custom_call" | custom-call | flops 131072 | bytes 397312 | tf_op jit(solution)/shard_map/pallas_call | solution.py:199
  (4 shorter events, 0.1 us)
Async XLA Ops:
  2.0 8.1 %collective-permute-start.4 = (f32[128,128]{1,0:T(8,128)S(1)}, f32[128,128]{1,0:T(8,128)S(1)}, u32[]{:S(2)}, u32[]{:S(2)}) collective-permute-start(f32[128,128]{1,0:T(8,128)S(1)} %get-tuple-element.22), channel_id=1, source_target_pairs={{0,4},{4,0},{8,12},{12,8},{16,20},{20,16},{24,28},{28,24},{1,5},{5... | collective-permute-start | bytes 196616 | tf_op jit(solution)/shard_map/ppermute | solution.py:212
  5.1 5.1 %collective-permute-start = (f32[128,128]{1,0:T(8,128)S(1)}, f32[128,128]{1,0:T(8,128)S(1)}, u32[]{:S(2)}, u32[]{:S(2)}) collective-permute-start(f32[128,128]{1,0:T(8,128)S(1)} %get-tuple-element.21), channel_id=1, source_target_pairs={{0,8},{4,12},{8,0},{12,4},{16,24},{20,28},{24,16},{28,20},{1,9},{5... | collective-permute-start | bytes 196616 | tf_op jit(solution)/shard_map/ppermute | solution.py:212
  6.6 5.3 %collective-permute-start.1 = (f32[128,128]{1,0:T(8,128)S(1)}, f32[128,128]{1,0:T(8,128)S(1)}, u32[]{:S(2)}, u32[]{:S(2)}) collective-permute-start(f32[128,128]{1,0:T(8,128)S(1)} %get-tuple-element.22), channel_id=1, source_target_pairs={{0,12},{4,8},{8,4},{12,0},{16,28},{20,24},{24,20},{28,16},{1,13},{... | collective-permute-start | bytes 196616 | tf_op jit(solution)/shard_map/ppermute | solution.py:212
  6.6 8.8 %collective-permute-start.3 = (f32[128,128]{1,0:T(8,128)S(1)}, f32[128,128]{1,0:T(8,128)S(1)}, u32[]{:S(2)}, u32[]{:S(2)}) collective-permute-start(f32[128,128]{1,0:T(8,128)S(1)} %get-tuple-element.24), channel_id=1, source_target_pairs={{0,12},{4,8},{8,4},{12,0},{16,28},{20,24},{24,20},{28,16},{1,13},{... | collective-permute-start | bytes 196616 | tf_op jit(solution)/shard_map/ppermute | solution.py:212
  9.6 9.6 %collective-permute-start.5 = (f32[128,128]{1,0:T(8,128)S(1)}, f32[128,128]{1,0:T(8,128)S(1)}, u32[]{:S(2)}, u32[]{:S(2)}) collective-permute-start(f32[128,128]{1,0:T(8,128)S(1)} %get-tuple-element.24), channel_id=1, source_target_pairs={{0,4},{4,0},{8,12},{12,8},{16,20},{20,16},{24,28},{28,24},{1,5},{5... | collective-permute-start | bytes 196616 | tf_op jit(solution)/shard_map/ppermute | solution.py:212
  10.1 5.3 %collective-permute-start.2 = (f32[128,128]{1,0:T(8,128)S(1)}, f32[128,128]{1,0:T(8,128)S(1)}, u32[]{:S(2)}, u32[]{:S(2)}) collective-permute-start(f32[128,128]{1,0:T(8,128)S(1)} %get-tuple-element.23), channel_id=1, source_target_pairs={{0,8},{4,12},{8,0},{12,4},{16,24},{20,28},{24,16},{28,20},{1,9},{5... | collective-permute-start | bytes 196616 | tf_op jit(solution)/shard_map/ppermute | solution.py:212
  11.9 7.2 %collective-permute-start.6 = (f32[128,128]{1,0:T(8,128)S(1)}, f32[128,128]{1,0:T(8,128)S(1)}, u32[]{:S(2)}, u32[]{:S(2)}) collective-permute-start(f32[128,128]{1,0:T(8,128)S(1)} %get-tuple-element.39), channel_id=1, source_target_pairs={{0,16},{1,21},{2,18},{3,23},{4,20},{5,17},{6,22},{7,19},{8,24},{9,... | collective-permute-start | bytes 196616 | tf_op jit(solution)/shard_map/ppermute | solution.py:251
  14.6 6.8 %collective-permute-start.7 = (f32[128,128]{1,0:T(8,128)S(1)}, f32[128,128]{1,0:T(8,128)S(1)}, u32[]{:S(2)}, u32[]{:S(2)}) collective-permute-start(f32[128,128]{1,0:T(8,128)S(1)} %get-tuple-element.39), channel_id=1, source_target_pairs={{0,20},{1,17},{2,22},{3,19},{4,16},{5,21},{6,18},{7,23},{8,28},{9,... | collective-permute-start | bytes 196616 | tf_op jit(solution)/shard_map/ppermute | solution.py:251
  15.5 2.2 %copy-start.2 = (bf16[128,512]{1,0:T(8,128)(2,1)S(1)}, bf16[128,512]{1,0:T(8,128)(2,1)}, u32[]{:S(2)}) copy-start(bf16[128,512]{1,0:T(8,128)(2,1)} %g_ref.3) | copy-start | bytes 393220
  15.5 2.2 %copy-start.3 = (bf16[128,512]{1,0:T(8,128)(2,1)S(1)}, bf16[128,512]{1,0:T(8,128)(2,1)}, u32[]{:S(2)}) copy-start(bf16[128,512]{1,0:T(8,128)(2,1)} %q_ref.3) | copy-start | bytes 393220
  15.5 2.2 %copy-start = (bf16[128,512]{1,0:T(8,128)(2,1)S(1)}, bf16[128,512]{1,0:T(8,128)(2,1)}, u32[]{:S(2)}) copy-start(bf16[128,512]{1,0:T(8,128)(2,1)} %k_ref.3) | copy-start | bytes 393220
  15.5 2.2 %copy-start.1 = (bf16[128,512]{1,0:T(8,128)(2,1)S(1)}, bf16[128,512]{1,0:T(8,128)(2,1)}, u32[]{:S(2)}) copy-start(bf16[128,512]{1,0:T(8,128)(2,1)} %v_ref.3) | copy-start | bytes 393220
  15.6 2.1 %copy-start.4 = (f32[512]{0:T(512)S(1)}, f32[512]{0:T(512)}, u32[]{:S(2)}) copy-start(f32[512]{0:T(512)} %param.9) | copy-start | bytes 6148
  15.6 5.8 %collective-permute-start.8 = (f32[128,128]{1,0:T(8,128)S(1)}, f32[128,128]{1,0:T(8,128)S(1)}, u32[]{:S(2)}, u32[]{:S(2)}) collective-permute-start(f32[128,128]{1,0:T(8,128)S(1)} %broadcast_select_fusion.3), channel_id=1, source_target_pairs={{0,4},{4,0},{8,12},{12,8},{16,20},{20,16},{24,28},{28,24},{1,5},{5... | collective-permute-start | bytes 196616 | tf_op jit(solution)/shard_map/ppermute | solution.py:212
  16.6 7.0 %collective-permute-start.12 = (f32[128,128]{1,0:T(8,128)S(1)}, f32[128,128]{1,0:T(8,128)S(1)}, u32[]{:S(2)}, u32[]{:S(2)}) collective-permute-start(f32[128,128]{1,0:T(8,128)S(1)} %get-tuple-element.36), channel_id=1, source_target_pairs={{0,4},{4,0},{8,12},{12,8},{16,20},{20,16},{24,28},{28,24},{1,5},{5... | collective-permute-start | bytes 196616 | tf_op jit(solution)/shard_map/ppermute | solution.py:212
  21.7 3.1 %collective-permute-start.9 = (f32[1,128]{1,0:T(1,128)S(1)}, f32[1,128]{1,0:T(1,128)S(1)}, u32[]{:S(2)}, u32[]{:S(2)}) collective-permute-start(f32[1,128]{1,0:T(1,128)S(1)} %get-tuple-element.29.refs_0_), channel_id=1, source_target_pairs={{0,3},{1,2},{2,1},{3,0},{4,7},{5,6},{6,5},{7,4},{8,11},{9,10},{10,... | collective-permute-start | bytes 1544 | tf_op jit(solution)/shard_map/ppermute | solution.py:212
  21.7 3.6 %collective-permute-start.10 = (f32[1,128]{1,0:T(1,128)S(1)}, f32[1,128]{1,0:T(1,128)S(1)}, u32[]{:S(2)}, u32[]{:S(2)}) collective-permute-start(f32[1,128]{1,0:T(1,128)S(1)} %get-tuple-element.29.refs_0_), channel_id=1, source_target_pairs={{0,2},{1,3},{2,0},{3,1},{4,6},{5,7},{6,4},{7,5},{8,10},{9,11},{10,... | collective-permute-start | bytes 1544 | tf_op jit(solution)/shard_map/ppermute | solution.py:212
  23.3 2.1 %collective-permute-start.11 = (f32[1,128]{1,0:T(1,128)S(1)}, f32[1,128]{1,0:T(1,128)S(1)}, u32[]{:S(2)}, u32[]{:S(2)}) collective-permute-start(f32[1,128]{1,0:T(1,128)S(1)} %get-tuple-element.29.refs_0_), channel_id=1, source_target_pairs={{0,1},{1,0},{2,3},{3,2},{4,5},{5,4},{6,7},{7,6},{8,9},{9,8},{10,11... | collective-permute-start | bytes 1544 | tf_op jit(solution)/shard_map/ppermute | solution.py:212

commit v9 on v7

--- a/solution.py
+++ b/solution.py
@@ -70,7 +70,7 @@
 
 def start_loads(q_hbm, k_hbm, v_hbm, g_hbm, left_ref, right_ref, sems):
     copies = []
-    for pair, (left, right) in enumerate(((k_hbm, v_hbm), (g_hbm, q_hbm))):
+    for pair, (left, right) in enumerate(((v_hbm, k_hbm), (g_hbm, q_hbm))):
         copies.append(
             (
                 pltpu.make_async_copy(left, left_ref.at[pair], sems.at[pair, 0]),
@@ -139,12 +139,12 @@
         for qh, gh, kh, vh in zip(by_head(q), by_head(g), by_head(k), by_head(v)):
             weights = (factor * jnp.where(causal, dot(qh, k, NT), 0.0)).astype(bf16)
             dweights = (factor * jnp.where(causal, dot(gh, v, NT), 0.0)).astype(bf16)
-            parts = (dot(weights, vh), dot(dweights, kh), dot(dweights, qh, TN), dot(weights, gh, TN))
+            parts = (dot(vh, weights, ((0,), (1,))), dot(dweights, kh), dot(dweights, qh, TN), dot(weights, gh, TN))
             if out is None:
                 out, dq, dk, dv = parts
             else:
                 out, dq, dk, dv = (x + y for x, y in zip((out, dq, dk, dv), parts))
-        out_ref[:, cols] = out
+        out_ref[cols] = out
         dq_ref[:, cols] = dq
         dk_ref[:, cols] = dk
         dv_ref[:, cols] = dv
@@ -157,24 +157,25 @@
     for t in range(tiles(q_ref)):
         cols = slice(t * LANES, (t + 1) * LANES)
         state = unpack_state((factor * kv_of(t)).astype(bf16))
-        out = part_ref[:, cols] + dot(tile(q_ref, t), state)
-        out_ref[:, cols] = out
+        out = part_ref[cols] + dot(state, tile(q_ref, t), NT)
+        out_ref[cols] = out
         square = out * out
         total = square if total is None else total + square
-    squares_ref[...] = jnp.sum(total.T, axis=0, keepdims=True)
-
-
-def grads_kernel(factor, axis, k_ref, v_ref, g_ref, dq_part, dk_part, dv_part, *refs):
-    *pieces, dq_ref, dk_ref, dv_ref = refs
+    squares_ref[...] = jnp.sum(total, axis=0, keepdims=True)
+
+
+def grads_kernel(factor, axis, k_ref, v_ref, g_ref, dq_part, dk_part, dv_part, turned_ref, *refs):
+    *pieces, dq_ref, dk_ref, dv_ref, out_ref = refs
     kv_of = whole_state(pieces[: len(pieces) // 2], axis, 0)
     qg_of = whole_state(pieces[len(pieces) // 2 :], axis, 1)
     for t in range(tiles(k_ref)):
         cols = slice(t * LANES, (t + 1) * LANES)
         state = unpack_state((factor * kv_of(t)).astype(bf16))
         grad_state = unpack_state((factor * qg_of(t)).astype(bf16))
-        dq_ref[:, cols] = (dq_part[:, cols] + dot(tile(g_ref, t), state, NT)).astype(bf16)
+        dq_ref[:, cols] = (dq_part[:, cols] + dot(tile(g_ref, t), state)).astype(bf16)
         dk_ref[:, cols] = (dk_part[:, cols] + dot(tile(v_ref, t), grad_state)).astype(bf16)
         dv_ref[:, cols] = (dv_part[:, cols] + dot(tile(k_ref, t), grad_state, NT)).astype(bf16)
+        out_ref[:, cols] = turned_ref[cols].T
 
 
 def norm_kernel(width, out_ref, gain_ref, *refs):
@@ -292,6 +293,7 @@
     packed = jax.ShapeDtypeStruct((width // LANES * HEAD_DIM, LANES), f32)
     wide = jax.ShapeDtypeStruct((length, width), f32)
     narrow = jax.ShapeDtypeStruct((length, width), bf16)
+    turned = jax.ShapeDtypeStruct((width, length), f32)
     inputs = (queries, keys, values, d_out)
     half = jax.ShapeDtypeStruct((packed.shape[0] // 2, LANES), f32)
 
@@ -309,7 +311,7 @@
 
     out_part, dq_part, dk_part, dv_part, gain_row = call(
         functools.partial(block_kernel, factor),
-        [wide] * 4 + [jax.ShapeDtypeStruct((1, width), f32)],
+        [turned] + [wide] * 3 + [jax.ShapeDtypeStruct((1, width), f32)],
         (*inputs, gain[None]),
         24 * length * LANES * width,
     )
@@ -318,17 +320,17 @@
         lambda: products(states_kernel, [packed] * 2),
         lambda: products(functools.partial(halves_kernel, "seq"), [half] * 4),
     )
-    out, squares = call(
+    turned_out, squares = call(
         functools.partial(output_kernel, factor, "seq"),
-        [wide, jax.ShapeDtypeStruct((1, length), f32)],
+        [turned, jax.ShapeDtypeStruct((1, length), f32)],
         (queries, out_part, *kv_pieces),
         2 * length * LANES * width,
     )
     shares = all_shares(squares, "head")
-    dq, dk, dv = call(
+    dq, dk, dv, out = call(
         functools.partial(grads_kernel, factor, "seq"),
-        [narrow] * 3,
-        (keys, values, d_out, dq_part, dk_part, dv_part, *kv_pieces, *qg_pieces),
+        [narrow] * 3 + [wide],
+        (keys, values, d_out, dq_part, dk_part, dv_part, turned_out, *kv_pieces, *qg_pieces),
         6 * length * LANES * width,
     )
     normed = call(

time: 26.3 us -> 29.8 us (1.13)
  waiting for transfers between devices: 4.69 us -> 8.32 us
    ppermute x13, waiting for transfers between devices: 4.69 us -> 8.32 us  [swap(): return lax.ppermute(x, axis, [(i, i ^ distance) for i in range(size)])]
  transfers between devices with their start and end apart: 13 -> 13, of which waited for: 4 -> 8; matrix products, arithmetic and copies ran while one was open for 0% -> 0% of each run, Pallas kernels for 11% -> 9%
where the time goes in v9:
time: 29.8 us; the launch traced here: 29.6 us
  starting transfers between devices  15.6 us (52%)
  waiting for transfers between devices  8.32 us (28%)
  Pallas kernels  4.8 us (16%)
  between operations  0.75 us (3%)
    ppermute x13, starting transfers between devices, swap(): return lax.ppermute(x, axis, [(i, i ^ distance) for i in range(size)])  15.6 us
    ppermute x13, waiting for transfers between devices, swap(): return lax.ppermute(x, axis, [(i, i ^ distance) for i in range(size)])  8.32 us
    pallas_call x5, Pallas kernels, call(): pl.pallas_call(kernel, out_shape=outs[0] if single else tuple(outs), in_s...  4.8 us
  transfers between devices with their start and end apart: 13, of which 8 were waited for; matrix products, arithmetic and copies ran while one was open for 0% of the time, Pallas kernels for 9%

profile of v9, /device:TPU:0, one launch (start us, length us, event | category | flops | bytes accessed | tf_op | source)
XLA Modules:
  0.0 29.6 jit_solution(17235309793254605709)
XLA Ops:
  0.6 1.4 %shard_map.85 = (f32[128,128]{1,0:T(8,128)S(1)}, f32[128,128]{1,0:T(8,128)S(1)}, f32[128,128]{1,0:T(8,128)S(1)}, f32[128,128]{1,0:T(8,128)S(1)}) custom-call(bf16[128,512]{1,0:T(8,128)(2,1)} %q_ref.3, bf16[128,512]{1,0:T(8,128)(2,1)} %k_ref.3, bf16[128,512]{1,0:T(8,128)(2,1)} %v_ref.3, bf16[128,512]{1,0:T(8,128)(2,1)} %g_ref.3), custom_call_target="tpu_custom_call" | custom-call | flops 33554432 | bytes 786432 | tf_op jit(solution)/shard_map/pallas_call | solution.py:197
  2.0 4.0 %collective-permute-start.3 = (f32[128,128]{1,0:T(8,128)S(1)}, f32[128,128]{1,0:T(8,128)S(1)}, u32[]{:S(2)}, u32[]{:S(2)}) collective-permute-start(f32[128,128]{1,0:T(8,128)S(1)} %get-tuple-element.28), channel_id=1, source_target_pairs={{0,12},{4,8},{8,4},{12,0},{16,28},{20,24},{24,20},{28,16},{1,13},{... | collective-permute-start | bytes 196616 | tf_op jit(solution)/shard_map/ppermute | solution.py:210
  6.1 0.4 %collective-permute-start.2 = (f32[128,128]{1,0:T(8,128)S(1)}, f32[128,128]{1,0:T(8,128)S(1)}, u32[]{:S(2)}, u32[]{:S(2)}) collective-permute-start(f32[128,128]{1,0:T(8,128)S(1)} %get-tuple-element.27), channel_id=1, source_target_pairs={{0,8},{4,12},{8,0},{12,4},{16,24},{20,28},{24,16},{28,20},{1,9},{5... | collective-permute-start | bytes 196616 | tf_op jit(solution)/shard_map/ppermute | solution.py:210
  6.5 0.2 collective-permute-start.4
  6.7 2.8 %collective-permute-start.1 = (f32[128,128]{1,0:T(8,128)S(1)}, f32[128,128]{1,0:T(8,128)S(1)}, u32[]{:S(2)}, u32[]{:S(2)}) collective-permute-start(f32[128,128]{1,0:T(8,128)S(1)} %get-tuple-element.26), channel_id=1, source_target_pairs={{0,12},{4,8},{8,4},{12,0},{16,28},{20,24},{24,20},{28,16},{1,13},{... | collective-permute-start | bytes 196616 | tf_op jit(solution)/shard_map/ppermute | solution.py:210
  9.6 0.4 %collective-permute-start = (f32[128,128]{1,0:T(8,128)S(1)}, f32[128,128]{1,0:T(8,128)S(1)}, u32[]{:S(2)}, u32[]{:S(2)}) collective-permute-start(f32[128,128]{1,0:T(8,128)S(1)} %get-tuple-element.25), channel_id=1, source_target_pairs={{0,8},{4,12},{8,0},{12,4},{16,24},{20,28},{24,16},{28,20},{1,9},{5... | collective-permute-start | bytes 196616 | tf_op jit(solution)/shard_map/ppermute | solution.py:210
  10.0 0.0 collective-permute-done.3
  10.0 0.7 %collective-permute-start.5 = (f32[128,128]{1,0:T(8,128)S(1)}, f32[128,128]{1,0:T(8,128)S(1)}, u32[]{:S(2)}, u32[]{:S(2)}) collective-permute-start(f32[128,128]{1,0:T(8,128)S(1)} %get-tuple-element.28), channel_id=1, source_target_pairs={{0,4},{4,0},{8,12},{12,8},{16,20},{20,16},{24,28},{28,24},{1,5},{5... | collective-permute-start | bytes 196616 | tf_op jit(solution)/shard_map/ppermute | solution.py:210
  10.8 0.3 collective-permute-done.2
  11.1 0.2 collective-permute-done.4.refs_1_.refs_8_
  11.2 1.2 %collective-permute-done.1 = f32[128,128]{1,0:T(8,128)S(1)} collective-permute-done((f32[128,128]{1,0:T(8,128)S(1)}, f32[128,128]{1,0:T(8,128)S(1)}, u32[]{:S(2)}, u32[]{:S(2)}) %collective-permute-start.1) | collective-permute-done | bytes 65568 | tf_op jit(solution)/shard_map/ppermute | solution.py:210
  12.4 1.4 %collective-permute-done = f32[128,128]{1,0:T(8,128)S(1)} collective-permute-done((f32[128,128]{1,0:T(8,128)S(1)}, f32[128,128]{1,0:T(8,128)S(1)}, u32[]{:S(2)}, u32[]{:S(2)}) %collective-permute-start) | collective-permute-done | bytes 65568 | tf_op jit(solution)/shard_map/ppermute | solution.py:210
  13.9 0.0 copy-start.2
  13.9 0.0 copy-start.3
  13.9 0.0 copy-start
  13.9 0.0 copy-start.1
  14.0 0.6 %collective-permute-start.8 = (f32[128,128]{1,0:T(8,128)S(1)}, f32[128,128]{1,0:T(8,128)S(1)}, u32[]{:S(2)}, u32[]{:S(2)}) collective-permute-start(f32[128,128]{1,0:T(8,128)S(1)} %broadcast_select_fusion.3), channel_id=1, source_target_pairs={{0,4},{4,0},{8,12},{12,8},{16,20},{20,16},{24,28},{28,24},{1,5},{5... | collective-permute-start | bytes 196616 | tf_op jit(solution)/shard_map/ppermute | solution.py:210
  14.6 0.0 copy-start.4
  14.6 3.5 %collective-permute-start.7 = (f32[128,128]{1,0:T(8,128)S(1)}, f32[128,128]{1,0:T(8,128)S(1)}, u32[]{:S(2)}, u32[]{:S(2)}) collective-permute-start(f32[128,128]{1,0:T(8,128)S(1)} %get-tuple-element.41), channel_id=1, source_target_pairs={{0,20},{4,16},{8,28},{12,24},{16,4},{20,0},{24,12},{28,8},{1,21},{... | collective-permute-start | bytes 196616 | tf_op jit(solution)/shard_map/ppermute | solution.py:210
  18.1 0.3 %collective-permute-start.6 = (f32[128,128]{1,0:T(8,128)S(1)}, f32[128,128]{1,0:T(8,128)S(1)}, u32[]{:S(2)}, u32[]{:S(2)}) collective-permute-start(f32[128,128]{1,0:T(8,128)S(1)} %get-tuple-element.41), channel_id=1, source_target_pairs={{0,16},{4,20},{8,24},{12,28},{16,0},{20,4},{24,8},{28,12},{1,17},{... | collective-permute-start | bytes 196616 | tf_op jit(solution)/shard_map/ppermute | solution.py:210
  18.4 0.5 %collective-permute-start.9 = (f32[128,128]{1,0:T(8,128)S(1)}, f32[128,128]{1,0:T(8,128)S(1)}, u32[]{:S(2)}, u32[]{:S(2)}) collective-permute-start(f32[128,128]{1,0:T(8,128)S(1)} %get-tuple-element.38), channel_id=1, source_target_pairs={{0,4},{4,0},{8,12},{12,8},{16,20},{20,16},{24,28},{28,24},{1,5},{5... | collective-permute-start | bytes 196616 | tf_op jit(solution)/shard_map/ppermute | solution.py:210
  19.0 0.0 copy-done.2
  19.0 0.0 copy-done.3
  19.0 0.0 copy-done
  19.0 0.0 copy-done.1
  19.0 0.0 copy-done.4
  19.0 1.4 %shard_map.84 = (f32[512,128]{1,0:T(8,128)S(1)}, f32[128,512]{1,0:T(8,128)S(1)}, f32[128,512]{1,0:T(8,128)S(1)}, f32[128,512]{1,0:T(8,128)S(1)}, f32[1,512]{1,0:T(1,128)S(1)}) custom-call(bf16[128,512]{1,0:T(8,128)(2,1)S(1)} %copy-done.3, bf16[128,512]{1,0:T(8,128)(2,1)S(1)} %copy-done, bf16[128,512]{1,0:T(8,128)(2,1)S(1)} %copy-done.1, ...), custom_call_target="tpu_custom_call" | custom-call | flops 201326592 | bytes 1576960 | tf_op jit(solution)/shard_map/pallas_call | solution.py:197
  20.4 0.0 collective-permute-done.5.refs_3_.refs_10_
  20.4 0.0 collective-permute-done.8.refs_6_
  20.4 1.3 %collective-permute-done.7.refs_5_.refs_12_ = f32[128,128]{1,0:T(8,128)S(1)} collective-permute-done((f32[128,128]{1,0:T(8,128)S(1)}, f32[128,128]{1,0:T(8,128)S(1)}, u32[]{:S(2)}, u32[]{:S(2)}) %collective-permute-start.7) | collective-permute-done | bytes 65568 | tf_op jit(solution)/shard_map/ppermute | solution.py:210
  21.7 2.2 %collective-permute-done.6.refs_4_.refs_11_ = f32[128,128]{1,0:T(8,128)S(1)} collective-permute-done((f32[128,128]{1,0:T(8,128)S(1)}, f32[128,128]{1,0:T(8,128)S(1)}, u32[]{:S(2)}, u32[]{:S(2)}) %collective-permute-start.6) | collective-permute-done | bytes 65568 | tf_op jit(solution)/shard_map/ppermute | solution.py:210
  23.9 0.2 shard_map.86
  24.2 0.1 collective-permute-start.12
  24.2 1.6 %collective-permute-start.11 = (f32[1,128]{1,0:T(1,128)S(1)}, f32[1,128]{1,0:T(1,128)S(1)}, u32[]{:S(2)}, u32[]{:S(2)}) collective-permute-start(f32[1,128]{1,0:T(1,128)S(1)} %get-tuple-element.34.refs_0_), channel_id=1, source_target_pairs={{0,2},{1,3},{2,0},{3,1},{4,6},{5,7},{6,4},{7,5},{8,10},{9,11},{10,... | collective-permute-start | bytes 1544 | tf_op jit(solution)/shard_map/ppermute | solution.py:210
  25.8 0.3 collective-permute-start.10
  26.1 0.0 collective-permute-done.9.refs_13_
  26.1 1.0 %shard_map.87 = (bf16[128,512]{1,0:T(8,128)(2,1)}, bf16[128,512]{1,0:T(8,128)(2,1)}, bf16[128,512]{1,0:T(8,128)(2,1)}, f32[128,512]{1,0:T(8,128)S(1)}) custom-call(bf16[128,512]{1,0:T(8,128)(2,1)S(1)} %copy-done, bf16[128,512]{1,0:T(8,128)(2,1)S(1)} %copy-done.1, bf16[128,512]{1,0:T(8,128)(2,1)S(1)} %copy-done.2, f32[128,512]{1,0:T(8,128)S(1)} %get-tuple-element.21.dq_part, ...), custom_call_target="tpu_custom_call" | custom-call | flops 50331648 | bytes 3014656 | tf_op jit(solution)/shard_map/pallas_call | solution.py:197
  27.1 0.0 collective-permute-done.12.refs_3_
  27.1 0.7 %collective-permute-done.11.refs_2_ = f32[1,128]{1,0:T(1,128)S(1)} collective-permute-done((f32[1,128]{1,0:T(1,128)S(1)}, f32[1,128]{1,0:T(1,128)S(1)}, u32[]{:S(2)}, u32[]{:S(2)}) %collective-permute-start.11) | collective-permute-done | bytes 544 | tf_op jit(solution)/shard_map/ppermute | solution.py:210
  27.9 0.9 %collective-permute-done.10.refs_1_ = f32[1,128]{1,0:T(1,128)S(1)} collective-permute-done((f32[1,128]{1,0:T(1,128)S(1)}, f32[1,128]{1,0:T(1,128)S(1)}, u32[]{:S(2)}, u32[]{:S(2)}) %collective-permute-start.10) | collective-permute-done | bytes 544 | tf_op jit(solution)/shard_map/ppermute | solution.py:210
  28.8 0.8 %shard_map.88 = bf16[128,512]{1,0:T(8,128)(2,1)} custom-call(f32[128,512]{1,0:T(8,128)S(1)} %get-tuple-element.32.out_ref, f32[1,512]{1,0:T(1,128)S(1)} %get-tuple-element.33.gain_ref, f32[1,128]{1,0:T(1,128)S(1)} %get-tuple-element.34.refs_0_, f32[1,128]{1,0:T(1,128)S(1)} %collective-permute-done.10.refs_1_, f32[1,128]{1,0:T(1,128)S(1)} %collective-permute-done.11.refs_2_, ...), custom_call_target="tpu_custom_call" | custom-call | flops 131072 | bytes 397312 | tf_op jit(solution)/shard_map/pallas_call | solution.py:197
  (4 shorter events, 0.1 us)
Async XLA Ops:
  2.0 8.0 %collective-permute-start.3 = (f32[128,128]{1,0:T(8,128)S(1)}, f32[128,128]{1,0:T(8,128)S(1)}, u32[]{:S(2)}, u32[]{:S(2)}) collective-permute-start(f32[128,128]{1,0:T(8,128)S(1)} %get-tuple-element.28), channel_id=1, source_target_pairs={{0,12},{4,8},{8,4},{12,0},{16,28},{20,24},{24,20},{28,16},{1,13},{... | collective-permute-start | bytes 196616 | tf_op jit(solution)/shard_map/ppermute | solution.py:210
  6.1 5.0 %collective-permute-start.2 = (f32[128,128]{1,0:T(8,128)S(1)}, f32[128,128]{1,0:T(8,128)S(1)}, u32[]{:S(2)}, u32[]{:S(2)}) collective-permute-start(f32[128,128]{1,0:T(8,128)S(1)} %get-tuple-element.27), channel_id=1, source_target_pairs={{0,8},{4,12},{8,0},{12,4},{16,24},{20,28},{24,16},{28,20},{1,9},{5... | collective-permute-start | bytes 196616 | tf_op jit(solution)/shard_map/ppermute | solution.py:210
  6.5 4.7 %collective-permute-start.4 = (f32[128,128]{1,0:T(8,128)S(1)}, f32[128,128]{1,0:T(8,128)S(1)}, u32[]{:S(2)}, u32[]{:S(2)}) collective-permute-start(f32[128,128]{1,0:T(8,128)S(1)} %get-tuple-element.26), channel_id=1, source_target_pairs={{0,4},{4,0},{8,12},{12,8},{16,20},{20,16},{24,28},{28,24},{1,5},{5... | collective-permute-start | bytes 196616 | tf_op jit(solution)/shard_map/ppermute | solution.py:210
  6.7 5.7 %collective-permute-start.1 = (f32[128,128]{1,0:T(8,128)S(1)}, f32[128,128]{1,0:T(8,128)S(1)}, u32[]{:S(2)}, u32[]{:S(2)}) collective-permute-start(f32[128,128]{1,0:T(8,128)S(1)} %get-tuple-element.26), channel_id=1, source_target_pairs={{0,12},{4,8},{8,4},{12,0},{16,28},{20,24},{24,20},{28,16},{1,13},{... | collective-permute-start | bytes 196616 | tf_op jit(solution)/shard_map/ppermute | solution.py:210
  9.6 4.3 %collective-permute-start = (f32[128,128]{1,0:T(8,128)S(1)}, f32[128,128]{1,0:T(8,128)S(1)}, u32[]{:S(2)}, u32[]{:S(2)}) collective-permute-start(f32[128,128]{1,0:T(8,128)S(1)} %get-tuple-element.25), channel_id=1, source_target_pairs={{0,8},{4,12},{8,0},{12,4},{16,24},{20,28},{24,16},{28,20},{1,9},{5... | collective-permute-start | bytes 196616 | tf_op jit(solution)/shard_map/ppermute | solution.py:210
  10.0 10.3 %collective-permute-start.5 = (f32[128,128]{1,0:T(8,128)S(1)}, f32[128,128]{1,0:T(8,128)S(1)}, u32[]{:S(2)}, u32[]{:S(2)}) collective-permute-start(f32[128,128]{1,0:T(8,128)S(1)} %get-tuple-element.28), channel_id=1, source_target_pairs={{0,4},{4,0},{8,12},{12,8},{16,20},{20,16},{24,28},{28,24},{1,5},{5... | collective-permute-start | bytes 196616 | tf_op jit(solution)/shard_map/ppermute | solution.py:210
  13.9 5.1 %copy-start.2 = (bf16[128,512]{1,0:T(8,128)(2,1)S(1)}, bf16[128,512]{1,0:T(8,128)(2,1)}, u32[]{:S(2)}) copy-start(bf16[128,512]{1,0:T(8,128)(2,1)} %g_ref.3) | copy-start | bytes 393220
  13.9 5.1 %copy-start.3 = (bf16[128,512]{1,0:T(8,128)(2,1)S(1)}, bf16[128,512]{1,0:T(8,128)(2,1)}, u32[]{:S(2)}) copy-start(bf16[128,512]{1,0:T(8,128)(2,1)} %q_ref.3) | copy-start | bytes 393220
  13.9 5.0 %copy-start = (bf16[128,512]{1,0:T(8,128)(2,1)S(1)}, bf16[128,512]{1,0:T(8,128)(2,1)}, u32[]{:S(2)}) copy-start(bf16[128,512]{1,0:T(8,128)(2,1)} %k_ref.3) | copy-start | bytes 393220
  13.9 5.0 %copy-start.1 = (bf16[128,512]{1,0:T(8,128)(2,1)S(1)}, bf16[128,512]{1,0:T(8,128)(2,1)}, u32[]{:S(2)}) copy-start(bf16[128,512]{1,0:T(8,128)(2,1)} %v_ref.3) | copy-start | bytes 393220
  14.0 6.4 %collective-permute-start.8 = (f32[128,128]{1,0:T(8,128)S(1)}, f32[128,128]{1,0:T(8,128)S(1)}, u32[]{:S(2)}, u32[]{:S(2)}) collective-permute-start(f32[128,128]{1,0:T(8,128)S(1)} %broadcast_select_fusion.3), channel_id=1, source_target_pairs={{0,4},{4,0},{8,12},{12,8},{16,20},{20,16},{24,28},{28,24},{1,5},{5... | collective-permute-start | bytes 196616 | tf_op jit(solution)/shard_map/ppermute | solution.py:210
  14.6 4.4 %copy-start.4 = (f32[512]{0:T(512)S(1)}, f32[512]{0:T(512)}, u32[]{:S(2)}) copy-start(f32[512]{0:T(512)} %param.9) | copy-start | bytes 6148
  14.6 7.2 %collective-permute-start.7 = (f32[128,128]{1,0:T(8,128)S(1)}, f32[128,128]{1,0:T(8,128)S(1)}, u32[]{:S(2)}, u32[]{:S(2)}) collective-permute-start(f32[128,128]{1,0:T(8,128)S(1)} %get-tuple-element.41), channel_id=1, source_target_pairs={{0,20},{4,16},{8,28},{12,24},{16,4},{20,0},{24,12},{28,8},{1,21},{... | collective-permute-start | bytes 196616 | tf_op jit(solution)/shard_map/ppermute | solution.py:210
  18.1 5.9 %collective-permute-start.6 = (f32[128,128]{1,0:T(8,128)S(1)}, f32[128,128]{1,0:T(8,128)S(1)}, u32[]{:S(2)}, u32[]{:S(2)}) collective-permute-start(f32[128,128]{1,0:T(8,128)S(1)} %get-tuple-element.41), channel_id=1, source_target_pairs={{0,16},{4,20},{8,24},{12,28},{16,0},{20,4},{24,8},{28,12},{1,17},{... | collective-permute-start | bytes 196616 | tf_op jit(solution)/shard_map/ppermute | solution.py:210
  18.4 7.7 %collective-permute-start.9 = (f32[128,128]{1,0:T(8,128)S(1)}, f32[128,128]{1,0:T(8,128)S(1)}, u32[]{:S(2)}, u32[]{:S(2)}) collective-permute-start(f32[128,128]{1,0:T(8,128)S(1)} %get-tuple-element.38), channel_id=1, source_target_pairs={{0,4},{4,0},{8,12},{12,8},{16,20},{20,16},{24,28},{28,24},{1,5},{5... | collective-permute-start | bytes 196616 | tf_op jit(solution)/shard_map/ppermute | solution.py:210
  24.2 3.0 %collective-permute-start.12 = (f32[1,128]{1,0:T(1,128)S(1)}, f32[1,128]{1,0:T(1,128)S(1)}, u32[]{:S(2)}, u32[]{:S(2)}) collective-permute-start(f32[1,128]{1,0:T(1,128)S(1)} %get-tuple-element.34.refs_0_), channel_id=1, source_target_pairs={{0,1},{1,0},{2,3},{3,2},{4,5},{5,4},{6,7},{7,6},{8,9},{9,8},{10,11... | collective-permute-start | bytes 1544 | tf_op jit(solution)/shard_map/ppermute | solution.py:210
  24.2 3.6 %collective-permute-start.11 = (f32[1,128]{1,0:T(1,128)S(1)}, f32[1,128]{1,0:T(1,128)S(1)}, u32[]{:S(2)}, u32[]{:S(2)}) collective-permute-start(f32[1,128]{1,0:T(1,128)S(1)} %get-tuple-element.34.refs_0_), channel_id=1, source_target_pairs={{0,2},{1,3},{2,0},{3,1},{4,6},{5,7},{6,4},{7,5},{8,10},{9,11},{10,... | collective-permute-start | bytes 1544 | tf_op jit(solution)/shard_map/ppermute | solution.py:210
  25.8 3.0 %collective-permute-start.10 = (f32[1,128]{1,0:T(1,128)S(1)}, f32[1,128]{1,0:T(1,128)S(1)}, u32[]{:S(2)}, u32[]{:S(2)}) collective-permute-start(f32[1,128]{1,0:T(1,128)S(1)} %get-tuple-element.34.refs_0_), channel_id=1, source_target_pairs={{0,3},{1,2},{2,1},{3,0},{4,7},{5,6},{6,5},{7,4},{8,11},{9,10},{10,... | collective-permute-start | bytes 1544 | tf_op jit(solution)/shard_map/ppermute | solution.py:210

commit v10 on v9

--- a/solution.py
+++ b/solution.py
@@ -113,13 +113,16 @@
     a_sum, a1, b_sum, b1, t_mine, t_other, got = pieces
     upper, odd = place_on(axis)
     is_a = upper == is_qg
+    swapped = lax.axis_index("head") % 2 == 1
     count = a_sum.shape[0] // HEAD_DIM
 
     def rows_of(t):
         rows = slice(t % count * HEAD_DIM, (t % count + 1) * HEAD_DIM)
         a_own = a_sum[rows] + jnp.where(odd != upper, a1[rows], 0.0)
-        b_own = b_sum[rows] + jnp.where(odd == upper, b1[rows], 0.0) + t_mine[rows]
-        other = got[rows] + jnp.where(is_a, 0.0, t_other[rows])
+        b_own = b_sum[rows] + jnp.where(odd == upper, b1[rows], 0.0)
+        b_own = b_own + jnp.where(swapped, t_other[rows], t_mine[rows])
+        t_rows = jnp.where(swapped, t_mine[rows], t_other[rows])
+        other = got[rows] + jnp.where(is_a, 0.0, t_rows)
         return jnp.where(odd == t // count, jnp.where(is_a, a_own, b_own), other)
 
     return rows_of
@@ -241,6 +244,13 @@
     def send(x, distance):
         return swap(x, axis, distance)
 
+    def send_by_core(x, distances):
+        heads = lax.axis_size("head")
+        pairs = [
+            (i * heads + h, (i ^ distances[h % 2]) * heads + h) for i in range(count) for h in range(heads)
+        ]
+        return lax.ppermute(x, (axis, "head"), pairs)
+
     a_mine, a_other, b_mine, b_other = halves()
     a3 = send(a_other, 3)
     a2 = send(a_mine, 2)
@@ -261,8 +271,8 @@
         b_sum = b_sum + jnp.where(b_enters(distance), b_got, 0.0)
         a_total, b_total = a_total + a_got, b_total + b_got
         distance *= 2
-    t_other = send(a_total, top | 1)
-    t_mine = send(a_total, top)
+    t_other = send_by_core(a_total, (top | 1, top))
+    t_mine = send_by_core(a_total, (top, top | 1))
     a_out = a_sum + jnp.where(a_enters(1), 0.0, a_mine)
     b_out = b_sum + jnp.where(b_enters(1), 0.0, b_mine)
     got_kv = send(jnp.where(upper, b_out, a_out), 1)

time: 29.8 us -> 29.7 us (level)
    ppermute x0 -> x2, starting transfers between devices: none -> 3.85 us  [send_by_core(): return lax.ppermute(x, (axis, 'head'), pairs)]
    ppermute x13 -> x11, starting transfers between devices: 15.6 us -> 11.8 us  [swap(): return lax.ppermute(x, axis, [(i, i ^ distance) for i in range(size)])]
    ppermute x13 -> x11, waiting for transfers between devices: 8.32 us -> 4.74 us  [swap(): return lax.ppermute(x, axis, [(i, i ^ distance) for i in range(size)])]
    ppermute x0 -> x2, waiting for transfers between devices: none -> 3.57 us  [send_by_core(): return lax.ppermute(x, (axis, 'head'), pairs)]
where the time goes in v10:
time: 29.7 us; the launch traced here: 29.6 us
  starting transfers between devices  15.6 us (53%)
  waiting for transfers between devices  8.31 us (28%)
  Pallas kernels  4.8 us (16%)
  between operations  0.75 us (3%)
    ppermute x11, starting transfers between devices, swap(): return lax.ppermute(x, axis, [(i, i ^ distance) for i in range(size)])  11.8 us
    pallas_call x5, Pallas kernels, call(): pl.pallas_call(kernel, out_shape=outs[0] if single else tuple(outs), in_s...  4.8 us
    ppermute x11, waiting for transfers between devices, swap(): return lax.ppermute(x, axis, [(i, i ^ distance) for i in range(size)])  4.74 us
    ppermute x2, starting transfers between devices, send_by_core(): return lax.ppermute(x, (axis, 'head'), pairs)  3.85 us
    ppermute x2, waiting for transfers between devices, send_by_core(): return lax.ppermute(x, (axis, 'head'), pairs)  3.57 us
  transfers between devices with their start and end apart: 13, of which 8 were waited for; matrix products, arithmetic and copies ran while one was open for 0% of the time, Pallas kernels for 9%

profile of v10, /device:TPU:0, one launch (start us, length us, event | category | flops | bytes accessed | tf_op | source)
XLA Modules:
  0.0 29.6 jit_solution(16711797629358630513)
XLA Ops:
  0.6 1.4 %shard_map.85 = (f32[128,128]{1,0:T(8,128)S(1)}, f32[128,128]{1,0:T(8,128)S(1)}, f32[128,128]{1,0:T(8,128)S(1)}, f32[128,128]{1,0:T(8,128)S(1)}) custom-call(bf16[128,512]{1,0:T(8,128)(2,1)} %q_ref.3, bf16[128,512]{1,0:T(8,128)(2,1)} %k_ref.3, bf16[128,512]{1,0:T(8,128)(2,1)} %v_ref.3, bf16[128,512]{1,0:T(8,128)(2,1)} %g_ref.3), custom_call_target="tpu_custom_call" | custom-call | flops 33554432 | bytes 786432 | tf_op jit(solution)/shard_map/pallas_call | solution.py:200
  2.0 4.0 %collective-permute-start.3 = (f32[128,128]{1,0:T(8,128)S(1)}, f32[128,128]{1,0:T(8,128)S(1)}, u32[]{:S(2)}, u32[]{:S(2)}) collective-permute-start(f32[128,128]{1,0:T(8,128)S(1)} %get-tuple-element.28), channel_id=1, source_target_pairs={{0,12},{4,8},{8,4},{12,0},{16,28},{20,24},{24,20},{28,16},{1,13},{... | collective-permute-start | bytes 196616 | tf_op jit(solution)/shard_map/ppermute | solution.py:213
  6.1 0.4 %collective-permute-start.2 = (f32[128,128]{1,0:T(8,128)S(1)}, f32[128,128]{1,0:T(8,128)S(1)}, u32[]{:S(2)}, u32[]{:S(2)}) collective-permute-start(f32[128,128]{1,0:T(8,128)S(1)} %get-tuple-element.27), channel_id=1, source_target_pairs={{0,8},{4,12},{8,0},{12,4},{16,24},{20,28},{24,16},{28,20},{1,9},{5... | collective-permute-start | bytes 196616 | tf_op jit(solution)/shard_map/ppermute | solution.py:213
  6.5 0.2 collective-permute-start.4
  6.7 2.8 %collective-permute-start.1 = (f32[128,128]{1,0:T(8,128)S(1)}, f32[128,128]{1,0:T(8,128)S(1)}, u32[]{:S(2)}, u32[]{:S(2)}) collective-permute-start(f32[128,128]{1,0:T(8,128)S(1)} %get-tuple-element.26), channel_id=1, source_target_pairs={{0,12},{4,8},{8,4},{12,0},{16,28},{20,24},{24,20},{28,16},{1,13},{... | collective-permute-start | bytes 196616 | tf_op jit(solution)/shard_map/ppermute | solution.py:213
  9.6 0.4 %collective-permute-start = (f32[128,128]{1,0:T(8,128)S(1)}, f32[128,128]{1,0:T(8,128)S(1)}, u32[]{:S(2)}, u32[]{:S(2)}) collective-permute-start(f32[128,128]{1,0:T(8,128)S(1)} %get-tuple-element.25), channel_id=1, source_target_pairs={{0,8},{4,12},{8,0},{12,4},{16,24},{20,28},{24,16},{28,20},{1,9},{5... | collective-permute-start | bytes 196616 | tf_op jit(solution)/shard_map/ppermute | solution.py:213
  10.0 0.0 collective-permute-done.3
  10.0 0.7 %collective-permute-start.5 = (f32[128,128]{1,0:T(8,128)S(1)}, f32[128,128]{1,0:T(8,128)S(1)}, u32[]{:S(2)}, u32[]{:S(2)}) collective-permute-start(f32[128,128]{1,0:T(8,128)S(1)} %get-tuple-element.28), channel_id=1, source_target_pairs={{0,4},{4,0},{8,12},{12,8},{16,20},{20,16},{24,28},{28,24},{1,5},{5... | collective-permute-start | bytes 196616 | tf_op jit(solution)/shard_map/ppermute | solution.py:213
  10.8 0.3 collective-permute-done.2
  11.1 0.2 collective-permute-done.4.refs_1_.refs_8_
  11.2 1.2 %collective-permute-done.1 = f32[128,128]{1,0:T(8,128)S(1)} collective-permute-done((f32[128,128]{1,0:T(8,128)S(1)}, f32[128,128]{1,0:T(8,128)S(1)}, u32[]{:S(2)}, u32[]{:S(2)}) %collective-permute-start.1) | collective-permute-done | bytes 65568 | tf_op jit(solution)/shard_map/ppermute | solution.py:213
  12.4 1.4 %collective-permute-done = f32[128,128]{1,0:T(8,128)S(1)} collective-permute-done((f32[128,128]{1,0:T(8,128)S(1)}, f32[128,128]{1,0:T(8,128)S(1)}, u32[]{:S(2)}, u32[]{:S(2)}) %collective-permute-start) | collective-permute-done | bytes 65568 | tf_op jit(solution)/shard_map/ppermute | solution.py:213
  13.9 0.0 copy-start.2
  13.9 0.0 copy-start.3
  13.9 0.0 copy-start
  13.9 0.0 copy-start.1
  14.0 0.6 %collective-permute-start.8 = (f32[128,128]{1,0:T(8,128)S(1)}, f32[128,128]{1,0:T(8,128)S(1)}, u32[]{:S(2)}, u32[]{:S(2)}) collective-permute-start(f32[128,128]{1,0:T(8,128)S(1)} %broadcast_select_fusion.3), channel_id=1, source_target_pairs={{0,4},{4,0},{8,12},{12,8},{16,20},{20,16},{24,28},{28,24},{1,5},{5... | collective-permute-start | bytes 196616 | tf_op jit(solution)/shard_map/ppermute | solution.py:213
  14.6 0.0 copy-start.4
  14.6 3.5 %collective-permute-start.7 = (f32[128,128]{1,0:T(8,128)S(1)}, f32[128,128]{1,0:T(8,128)S(1)}, u32[]{:S(2)}, u32[]{:S(2)}) collective-permute-start(f32[128,128]{1,0:T(8,128)S(1)} %get-tuple-element.41), channel_id=1, source_target_pairs={{0,20},{1,17},{2,22},{3,19},{4,16},{5,21},{6,18},{7,23},{8,28},{9,... | collective-permute-start | bytes 196616 | tf_op jit(solution)/shard_map/ppermute | solution.py:252
  18.1 0.3 %collective-permute-start.6 = (f32[128,128]{1,0:T(8,128)S(1)}, f32[128,128]{1,0:T(8,128)S(1)}, u32[]{:S(2)}, u32[]{:S(2)}) collective-permute-start(f32[128,128]{1,0:T(8,128)S(1)} %get-tuple-element.41), channel_id=1, source_target_pairs={{0,16},{1,21},{2,18},{3,23},{4,20},{5,17},{6,22},{7,19},{8,24},{9,... | collective-permute-start | bytes 196616 | tf_op jit(solution)/shard_map/ppermute | solution.py:252
  18.4 0.5 %collective-permute-start.9 = (f32[128,128]{1,0:T(8,128)S(1)}, f32[128,128]{1,0:T(8,128)S(1)}, u32[]{:S(2)}, u32[]{:S(2)}) collective-permute-start(f32[128,128]{1,0:T(8,128)S(1)} %get-tuple-element.38), channel_id=1, source_target_pairs={{0,4},{4,0},{8,12},{12,8},{16,20},{20,16},{24,28},{28,24},{1,5},{5... | collective-permute-start | bytes 196616 | tf_op jit(solution)/shard_map/ppermute | solution.py:213
  19.0 0.0 copy-done.2
  19.0 0.0 copy-done.3
  19.0 0.0 copy-done
  19.0 0.0 copy-done.1
  19.0 0.0 copy-done.4
  19.0 1.4 %shard_map.84 = (f32[512,128]{1,0:T(8,128)S(1)}, f32[128,512]{1,0:T(8,128)S(1)}, f32[128,512]{1,0:T(8,128)S(1)}, f32[128,512]{1,0:T(8,128)S(1)}, f32[1,512]{1,0:T(1,128)S(1)}) custom-call(bf16[128,512]{1,0:T(8,128)(2,1)S(1)} %copy-done.3, bf16[128,512]{1,0:T(8,128)(2,1)S(1)} %copy-done, bf16[128,512]{1,0:T(8,128)(2,1)S(1)} %copy-done.1, ...), custom_call_target="tpu_custom_call" | custom-call | flops 201326592 | bytes 1576960 | tf_op jit(solution)/shard_map/pallas_call | solution.py:200
  20.4 0.0 collective-permute-done.5.refs_3_.refs_10_
  20.4 0.0 collective-permute-done.8.refs_6_
  20.4 1.3 %collective-permute-done.7.refs_5_.refs_12_ = f32[128,128]{1,0:T(8,128)S(1)} collective-permute-done((f32[128,128]{1,0:T(8,128)S(1)}, f32[128,128]{1,0:T(8,128)S(1)}, u32[]{:S(2)}, u32[]{:S(2)}) %collective-permute-start.7) | collective-permute-done | bytes 65568 | tf_op jit(solution)/shard_map/ppermute | solution.py:252
  21.7 2.2 %collective-permute-done.6.refs_4_.refs_11_ = f32[128,128]{1,0:T(8,128)S(1)} collective-permute-done((f32[128,128]{1,0:T(8,128)S(1)}, f32[128,128]{1,0:T(8,128)S(1)}, u32[]{:S(2)}, u32[]{:S(2)}) %collective-permute-start.6) | collective-permute-done | bytes 65568 | tf_op jit(solution)/shard_map/ppermute | solution.py:252
  23.9 0.2 shard_map.86
  24.2 0.1 collective-permute-start.12
  24.2 1.6 %collective-permute-start.11 = (f32[1,128]{1,0:T(1,128)S(1)}, f32[1,128]{1,0:T(1,128)S(1)}, u32[]{:S(2)}, u32[]{:S(2)}) collective-permute-start(f32[1,128]{1,0:T(1,128)S(1)} %get-tuple-element.34.refs_0_), channel_id=1, source_target_pairs={{0,2},{1,3},{2,0},{3,1},{4,6},{5,7},{6,4},{7,5},{8,10},{9,11},{10,... | collective-permute-start | bytes 1544 | tf_op jit(solution)/shard_map/ppermute | solution.py:213
  25.8 0.3 collective-permute-start.10
  26.1 0.0 collective-permute-done.9.refs_13_
  26.1 1.1 %shard_map.87 = (bf16[128,512]{1,0:T(8,128)(2,1)}, bf16[128,512]{1,0:T(8,128)(2,1)}, bf16[128,512]{1,0:T(8,128)(2,1)}, f32[128,512]{1,0:T(8,128)S(1)}) custom-call(bf16[128,512]{1,0:T(8,128)(2,1)S(1)} %copy-done, bf16[128,512]{1,0:T(8,128)(2,1)S(1)} %copy-done.1, bf16[128,512]{1,0:T(8,128)(2,1)S(1)} %copy-done.2, f32[128,512]{1,0:T(8,128)S(1)} %get-tuple-element.21.dq_part, ...), custom_call_target="tpu_custom_call" | custom-call | flops 50331648 | bytes 3014656 | tf_op jit(solution)/shard_map/pallas_call | solution.py:200
  27.2 0.0 collective-permute-done.12.refs_3_
  27.2 0.7 %collective-permute-done.11.refs_2_ = f32[1,128]{1,0:T(1,128)S(1)} collective-permute-done((f32[1,128]{1,0:T(1,128)S(1)}, f32[1,128]{1,0:T(1,128)S(1)}, u32[]{:S(2)}, u32[]{:S(2)}) %collective-permute-start.11) | collective-permute-done | bytes 544 | tf_op jit(solution)/shard_map/ppermute | solution.py:213
  27.9 0.9 %collective-permute-done.10.refs_1_ = f32[1,128]{1,0:T(1,128)S(1)} collective-permute-done((f32[1,128]{1,0:T(1,128)S(1)}, f32[1,128]{1,0:T(1,128)S(1)}, u32[]{:S(2)}, u32[]{:S(2)}) %collective-permute-start.10) | collective-permute-done | bytes 544 | tf_op jit(solution)/shard_map/ppermute | solution.py:213
  28.8 0.8 %shard_map.88 = bf16[128,512]{1,0:T(8,128)(2,1)} custom-call(f32[128,512]{1,0:T(8,128)S(1)} %get-tuple-element.32.out_ref, f32[1,512]{1,0:T(1,128)S(1)} %get-tuple-element.33.gain_ref, f32[1,128]{1,0:T(1,128)S(1)} %get-tuple-element.34.refs_0_, f32[1,128]{1,0:T(1,128)S(1)} %collective-permute-done.10.refs_1_, f32[1,128]{1,0:T(1,128)S(1)} %collective-permute-done.11.refs_2_, ...), custom_call_target="tpu_custom_call" | custom-call | flops 131072 | bytes 397312 | tf_op jit(solution)/shard_map/pallas_call | solution.py:200
  (4 shorter events, 0.1 us)
Async XLA Ops:
  2.0 8.0 %collective-permute-start.3 = (f32[128,128]{1,0:T(8,128)S(1)}, f32[128,128]{1,0:T(8,128)S(1)}, u32[]{:S(2)}, u32[]{:S(2)}) collective-permute-start(f32[128,128]{1,0:T(8,128)S(1)} %get-tuple-element.28), channel_id=1, source_target_pairs={{0,12},{4,8},{8,4},{12,0},{16,28},{20,24},{24,20},{28,16},{1,13},{... | collective-permute-start | bytes 196616 | tf_op jit(solution)/shard_map/ppermute | solution.py:213
  6.1 5.0 %collective-permute-start.2 = (f32[128,128]{1,0:T(8,128)S(1)}, f32[128,128]{1,0:T(8,128)S(1)}, u32[]{:S(2)}, u32[]{:S(2)}) collective-permute-start(f32[128,128]{1,0:T(8,128)S(1)} %get-tuple-element.27), channel_id=1, source_target_pairs={{0,8},{4,12},{8,0},{12,4},{16,24},{20,28},{24,16},{28,20},{1,9},{5... | collective-permute-start | bytes 196616 | tf_op jit(solution)/shard_map/ppermute | solution.py:213
  6.5 4.7 %collective-permute-start.4 = (f32[128,128]{1,0:T(8,128)S(1)}, f32[128,128]{1,0:T(8,128)S(1)}, u32[]{:S(2)}, u32[]{:S(2)}) collective-permute-start(f32[128,128]{1,0:T(8,128)S(1)} %get-tuple-element.26), channel_id=1, source_target_pairs={{0,4},{4,0},{8,12},{12,8},{16,20},{20,16},{24,28},{28,24},{1,5},{5... | collective-permute-start | bytes 196616 | tf_op jit(solution)/shard_map/ppermute | solution.py:213
  6.7 5.7 %collective-permute-start.1 = (f32[128,128]{1,0:T(8,128)S(1)}, f32[128,128]{1,0:T(8,128)S(1)}, u32[]{:S(2)}, u32[]{:S(2)}) collective-permute-start(f32[128,128]{1,0:T(8,128)S(1)} %get-tuple-element.26), channel_id=1, source_target_pairs={{0,12},{4,8},{8,4},{12,0},{16,28},{20,24},{24,20},{28,16},{1,13},{... | collective-permute-start | bytes 196616 | tf_op jit(solution)/shard_map/ppermute | solution.py:213
  9.6 4.3 %collective-permute-start = (f32[128,128]{1,0:T(8,128)S(1)}, f32[128,128]{1,0:T(8,128)S(1)}, u32[]{:S(2)}, u32[]{:S(2)}) collective-permute-start(f32[128,128]{1,0:T(8,128)S(1)} %get-tuple-element.25), channel_id=1, source_target_pairs={{0,8},{4,12},{8,0},{12,4},{16,24},{20,28},{24,16},{28,20},{1,9},{5... | collective-permute-start | bytes 196616 | tf_op jit(solution)/shard_map/ppermute | solution.py:213
  10.0 10.3 %collective-permute-start.5 = (f32[128,128]{1,0:T(8,128)S(1)}, f32[128,128]{1,0:T(8,128)S(1)}, u32[]{:S(2)}, u32[]{:S(2)}) collective-permute-start(f32[128,128]{1,0:T(8,128)S(1)} %get-tuple-element.28), channel_id=1, source_target_pairs={{0,4},{4,0},{8,12},{12,8},{16,20},{20,16},{24,28},{28,24},{1,5},{5... | collective-permute-start | bytes 196616 | tf_op jit(solution)/shard_map/ppermute | solution.py:213
  13.9 5.1 %copy-start.2 = (bf16[128,512]{1,0:T(8,128)(2,1)S(1)}, bf16[128,512]{1,0:T(8,128)(2,1)}, u32[]{:S(2)}) copy-start(bf16[128,512]{1,0:T(8,128)(2,1)} %g_ref.3) | copy-start | bytes 393220
  13.9 5.1 %copy-start.3 = (bf16[128,512]{1,0:T(8,128)(2,1)S(1)}, bf16[128,512]{1,0:T(8,128)(2,1)}, u32[]{:S(2)}) copy-start(bf16[128,512]{1,0:T(8,128)(2,1)} %q_ref.3) | copy-start | bytes 393220
  13.9 5.0 %copy-start = (bf16[128,512]{1,0:T(8,128)(2,1)S(1)}, bf16[128,512]{1,0:T(8,128)(2,1)}, u32[]{:S(2)}) copy-start(bf16[128,512]{1,0:T(8,128)(2,1)} %k_ref.3) | copy-start | bytes 393220
  13.9 5.0 %copy-start.1 = (bf16[128,512]{1,0:T(8,128)(2,1)S(1)}, bf16[128,512]{1,0:T(8,128)(2,1)}, u32[]{:S(2)}) copy-start(bf16[128,512]{1,0:T(8,128)(2,1)} %v_ref.3) | copy-start | bytes 393220
  14.0 6.4 %collective-permute-start.8 = (f32[128,128]{1,0:T(8,128)S(1)}, f32[128,128]{1,0:T(8,128)S(1)}, u32[]{:S(2)}, u32[]{:S(2)}) collective-permute-start(f32[128,128]{1,0:T(8,128)S(1)} %broadcast_select_fusion.3), channel_id=1, source_target_pairs={{0,4},{4,0},{8,12},{12,8},{16,20},{20,16},{24,28},{28,24},{1,5},{5... | collective-permute-start | bytes 196616 | tf_op jit(solution)/shard_map/ppermute | solution.py:213
  14.6 4.4 %copy-start.4 = (f32[512]{0:T(512)S(1)}, f32[512]{0:T(512)}, u32[]{:S(2)}) copy-start(f32[512]{0:T(512)} %param.9) | copy-start | bytes 6148
  14.6 7.2 %collective-permute-start.7 = (f32[128,128]{1,0:T(8,128)S(1)}, f32[128,128]{1,0:T(8,128)S(1)}, u32[]{:S(2)}, u32[]{:S(2)}) collective-permute-start(f32[128,128]{1,0:T(8,128)S(1)} %get-tuple-element.41), channel_id=1, source_target_pairs={{0,20},{1,17},{2,22},{3,19},{4,16},{5,21},{6,18},{7,23},{8,28},{9,... | collective-permute-start | bytes 196616 | tf_op jit(solution)/shard_map/ppermute | solution.py:252
  18.1 5.9 %collective-permute-start.6 = (f32[128,128]{1,0:T(8,128)S(1)}, f32[128,128]{1,0:T(8,128)S(1)}, u32[]{:S(2)}, u32[]{:S(2)}) collective-permute-start(f32[128,128]{1,0:T(8,128)S(1)} %get-tuple-element.41), channel_id=1, source_target_pairs={{0,16},{1,21},{2,18},{3,23},{4,20},{5,17},{6,22},{7,19},{8,24},{9,... | collective-permute-start | bytes 196616 | tf_op jit(solution)/shard_map/ppermute | solution.py:252
  18.4 7.7 %collective-permute-start.9 = (f32[128,128]{1,0:T(8,128)S(1)}, f32[128,128]{1,0:T(8,128)S(1)}, u32[]{:S(2)}, u32[]{:S(2)}) collective-permute-start(f32[128,128]{1,0:T(8,128)S(1)} %get-tuple-element.38), channel_id=1, source_target_pairs={{0,4},{4,0},{8,12},{12,8},{16,20},{20,16},{24,28},{28,24},{1,5},{5... | collective-permute-start | bytes 196616 | tf_op jit(solution)/shard_map/ppermute | solution.py:213
  24.2 3.0 %collective-permute-start.12 = (f32[1,128]{1,0:T(1,128)S(1)}, f32[1,128]{1,0:T(1,128)S(1)}, u32[]{:S(2)}, u32[]{:S(2)}) collective-permute-start(f32[1,128]{1,0:T(1,128)S(1)} %get-tuple-element.34.refs_0_), channel_id=1, source_target_pairs={{0,1},{1,0},{2,3},{3,2},{4,5},{5,4},{6,7},{7,6},{8,9},{9,8},{10,11... | collective-permute-start | bytes 1544 | tf_op jit(solution)/shard_map/ppermute | solution.py:213
  24.2 3.6 %collective-permute-start.11 = (f32[1,128]{1,0:T(1,128)S(1)}, f32[1,128]{1,0:T(1,128)S(1)}, u32[]{:S(2)}, u32[]{:S(2)}) collective-permute-start(f32[1,128]{1,0:T(1,128)S(1)} %get-tuple-element.34.refs_0_), channel_id=1, source_target_pairs={{0,2},{1,3},{2,0},{3,1},{4,6},{5,7},{6,4},{7,5},{8,10},{9,11},{10,... | collective-permute-start | bytes 1544 | tf_op jit(solution)/shard_map/ppermute | solution.py:213
  25.8 3.0 %collective-permute-start.10 = (f32[1,128]{1,0:T(1,128)S(1)}, f32[1,128]{1,0:T(1,128)S(1)}, u32[]{:S(2)}, u32[]{:S(2)}) collective-permute-start(f32[1,128]{1,0:T(1,128)S(1)} %get-tuple-element.34.refs_0_), channel_id=1, source_target_pairs={{0,3},{1,2},{2,1},{3,0},{4,7},{5,6},{6,5},{7,4},{8,11},{9,10},{10,... | collective-permute-start | bytes 1544 | tf_op jit(solution)/shard_map/ppermute | solution.py:213
